TPU v7x, 256 devices: a whole 4x4x8 slice. The times are simulated.
256 devices in a mesh: leaf: 32 (over x, z), sub: 8 (over y, core).
Axes of the slice: x: 4, y: 4, z: 8, core: 2. Of those that a mesh axis runs over, the one named last changes fastest.
Arguments:
- leaf_right: bfloat16 [1024, 512, 256], P(('leaf', 'sub')), may hold values from -6 to 6
- leaf_inverse: bfloat16 [1024, 512, 512], P(('leaf', 'sub')), may hold values from -2.5 to 2.5, as said below
- panels: bfloat16 [1024, 256, 512], P(('leaf', 'sub')), may hold values from -0.125 to 0.125
- leaf_subtree: int32 [1024], P(('leaf', 'sub')), may hold values from 0 to 31, as said below
- panel_block: int32 [1024, 4], P(('leaf', 'sub')), may hold values from 0 to 63
- separator_right: bfloat16 [131072, 256], P(('leaf', 'sub')), may hold values from -6 to 6
- separator_inverse: bfloat16 [131072, 512], P(('leaf', 'sub')), may hold values from -2.5 to 2.5, as said below
- separator_factor: bfloat16 [131072, 4096], P(('leaf', 'sub')), may hold values from -1 to 1, as said below
Outputs:
- leaf_solution: bfloat16 [1024, 512, 256], P(('leaf', 'sub'))
- separator_solution: bfloat16 [131072, 256], P(('leaf', 'sub'))
Inputs may be any that keep to these rules, and one draw needn't show every extreme that they name: `leaf_subtree`: every leaf supernode held by section s of the leaf axis belongs to a subtree between s - (2) and s. Each device of section s holds, for every d from 0 to min(2, s), at least one leaf supernode of subtree s - d. `leaf_inverse`: each 512 x 512 block is lower triangular, with its diagonal between 0.6 and 1.4. `separator_inverse`: each 512 x 512 block is lower triangular, with its diagonal between 0.6 and 1.4. `separator_factor`: within each subtree's 4096 rows, the block of row block q and column block p (blocks of 512) is zero unless q > p.
All inputs are finite; a program needn't handle non-finite values.
Results may differ from a plain program's by a relative error of at most 0.024.
Values may be sent and summed in bfloat16 or wider, within the bound.
No kernel may reach another device: no remote copies, remote signals or barrier semaphores. Data moves between devices by JAX's collectives and lax.ppermute only.
A program may use at most 128 MiB of HBM per device.

v0:
```python
import jax
import jax.numpy as jnp
from jax import lax
from jax.sharding import PartitionSpec as P

WSN = 512
SA = 4096
R = 256
BLK = 64
KB = 4
SPAN = 3


exact_precision = lax.Precision.HIGHEST


def passed_along(block, axis, distance):
    devices = range(lax.axis_size(axis))
    route = [(i - distance, i) for i in devices if i - distance in devices]
    return lax.ppermute(block, axis, route)


def broadcast(shard, axis, root):
    mine = lax.axis_index(axis) == root
    return lax.psum(jnp.where(mine, shard, jnp.zeros_like(shard)), axis)


def route_forward(stacked):
    summed = stacked[0]
    for distance in range(1, SPAN):
        summed = summed + passed_along(stacked[distance], "leaf", -distance)
    return summed


def route_back(item):
    collected = [item] + [passed_along(item, "leaf", distance) for distance in range(1, SPAN)]
    return jnp.stack(collected)


def shards(
    leaf_right,
    leaf_inverse,
    panels,
    leaf_subtree,
    panel_block,
    separator_right,
    separator_inverse,
    separator_factor,
):
    section = lax.axis_index("leaf")
    member = lax.axis_index("sub")
    leaves_here = leaf_right.shape[0]
    row_blocks = SA // BLK
    share_rows = separator_right.shape[0]
    per_device = share_rows // WSN
    solved = jnp.einsum(
        "jab,jbr->jar", leaf_inverse, leaf_right, preferred_element_type=jnp.float32
    ).astype(jnp.bfloat16)
    updates = jnp.einsum(
        "jib,jbr->jir", panels, solved, preferred_element_type=jnp.float32
    ).reshape(leaves_here * KB, BLK * R)
    offsets = section - leaf_subtree
    slot_index = (offsets[:, None] * row_blocks + panel_block).reshape(-1)
    selector = (
        jnp.arange(SPAN * row_blocks, dtype=jnp.int32)[:, None] == slot_index[None, :]
    ).astype(jnp.float32)
    spilled = jnp.dot(
        selector, updates, precision=exact_precision, preferred_element_type=jnp.float32
    ).reshape(SPAN, SA, R)
    own_rows = lax.psum_scatter(route_forward(spilled), "sub", scatter_dimension=0, tiled=True)
    rhs_rows = (separator_right.astype(jnp.float32) - own_rows).astype(jnp.bfloat16)
    inverse_blocks = separator_inverse.reshape(per_device, WSN, WSN)
    running = rhs_rows.astype(jnp.float32).reshape(per_device, WSN, R)
    empty_block = jnp.zeros((WSN, R), jnp.bfloat16)
    forward_store = jnp.zeros((per_device, WSN, R), jnp.bfloat16)
    for column in range(SA // WSN):
        owner = column // per_device
        local_col = column % per_device
        is_owner = member == owner

        def solve_block():
            return jnp.dot(
                inverse_blocks[local_col].astype(jnp.float32),
                running[local_col],
                precision=exact_precision,
                preferred_element_type=jnp.float32,
            ).astype(jnp.bfloat16)

        own_block = lax.cond(is_owner, solve_block, lambda: empty_block)
        block_y = broadcast(own_block, "sub", owner)
        forward_store = forward_store.at[local_col].set(
            jnp.where(is_owner, block_y, forward_store[local_col])
        )
        column_panel = separator_factor[:, column * WSN : (column + 1) * WSN]
        running = running - jnp.dot(
            column_panel, block_y, preferred_element_type=jnp.float32
        ).reshape(per_device, WSN, R)
    backward_store = jnp.zeros((per_device, WSN, R), jnp.bfloat16)
    for column in reversed(range(SA // WSN)):
        owner = column // per_device
        local_col = column % per_device
        is_owner = member == owner
        column_panel = separator_factor[:, column * WSN : (column + 1) * WSN]
        partial_term = lax.dot_general(
            column_panel,
            backward_store.reshape(share_rows, R),
            (((0,), (0,)), ((), ())),
            preferred_element_type=jnp.float32,
        )
        summed_later = lax.psum(partial_term, "sub")

        def back_block():
            bracket = forward_store[local_col].astype(jnp.float32) - summed_later
            return lax.dot_general(
                inverse_blocks[local_col].astype(jnp.float32),
                bracket,
                (((0,), (0,)), ((), ())),
                precision=exact_precision,
                preferred_element_type=jnp.float32,
            ).astype(jnp.bfloat16)

        own_back = lax.cond(is_owner, back_block, lambda: empty_block)
        backward_store = backward_store.at[local_col].set(
            jnp.where(is_owner, own_back, backward_store[local_col])
        )
    separator_x = backward_store.reshape(share_rows, R)
    solution_table = route_back(lax.all_gather(separator_x, "sub", axis=0, tiled=True))
    pieces = jnp.take(solution_table.reshape(SPAN * row_blocks, BLK * R), slot_index, axis=0)
    pieces = pieces.reshape(leaves_here, KB * BLK, R)
    reduced = jnp.einsum("jib,jir->jbr", panels, pieces, preferred_element_type=jnp.float32)
    inner_rhs = (solved.astype(jnp.float32) - reduced).astype(jnp.bfloat16)
    leaf_x = jnp.einsum(
        "jab,jar->jbr", leaf_inverse, inner_rhs, preferred_element_type=jnp.float32
    ).astype(jnp.bfloat16)
    return (leaf_x, separator_x)


def solution(mesh):
    placed = (
        P(("leaf", "sub"), None, None),
        P(("leaf", "sub"), None, None),
        P(("leaf", "sub"), None, None),
        P(("leaf", "sub")),
        P(("leaf", "sub"), None),
        P(("leaf", "sub"), None),
        P(("leaf", "sub"), None),
        P(("leaf", "sub"), None),
    )
    return jax.shard_map(
        shards,
        mesh=mesh,
        in_specs=placed,
        out_specs=(P(("leaf", "sub"), None, None), P(("leaf", "sub"), None)),
        check_vma=False,
    )
```

profile of v0, /device:TPU:38, one launch (start us, length us, event | category | flops | bytes accessed | tf_op | source)
XLA Modules:
  0.0 1701.2 jit_solution(7460126840667194432)
XLA Ops:
  13.4 2.6 copy.45
  16.0 2.4 reshape.570
  18.4 9.1 fusion.50
  27.5 9.4 fusion.57
  36.9 4.9 squeeze.31
  41.8 5.7 copy.46
  49.4 5.0 squeeze.32
  54.4 5.6 copy.48
  60.1 8.5 collective-permute-start.1
  68.5 5.0 squeeze.29
  73.5 5.6 copy.47
  79.1 64.4 %collective-permute-done = f32[4096,256]{0,1:T(8,128)} collective-permute-done((f32[4096,256]{0,1:T(8,128)}, f32[4096,256]{0,1:T(8,128)}, u32[]{:S(2)}, u32[]{:S(2)}) %collective-permute-start) | collective-permute-done | bytes 4194336 | tf_op jit(solution)/shard_map/ppermute | solution.py:20
  143.6 91.8 %collective-permute-done.1 = f32[4096,256]{0,1:T(8,128)} collective-permute-done((f32[4096,256]{0,1:T(8,128)}, f32[4096,256]{0,1:T(8,128)}, u32[]{:S(2)}, u32[]{:S(2)}) %collective-permute-start.1) | collective-permute-done | bytes 4194336 | tf_op jit(solution)/shard_map/ppermute | solution.py:20
  235.4 7.8 add_add_fusion
  244.3 130.0 %reduce-scatter.2.cloned.1.call-done = f32[512,256]{0,1:T(8,128)} async-done(((f32[4096,256]{0,1:T(8,128)}), f32[512,256]{0,1:T(8,128)}) %reduce-scatter.2.cloned.1.call-update) | async-done | bytes 524304 | tf_op jit(solution)/shard_map/reduce_scatter | solution.py:70
  378.8 63.9 %all-reduce.17.cloned.1.call-done = bf16[512,256]{1,0:T(8,128)(2,1)} async-done(((bf16[512,256]{1,0:T(8,128)(2,1)}), bf16[512,256]{1,0:T(8,128)(2,1)}) %all-reduce.17.cloned.1.call-update) | async-done | bytes 262160 | tf_op jit(solution)/shard_map/psum | solution.py:25
  445.2 64.7 %all-reduce.19.cloned.1.call-done = bf16[512,256]{1,0:T(8,128)(2,1)} async-done(((bf16[512,256]{1,0:T(8,128)(2,1)}), bf16[512,256]{1,0:T(8,128)(2,1)}) %all-reduce.19.cloned.1.call-update) | async-done | bytes 262160 | tf_op jit(solution)/shard_map/psum | solution.py:25
  509.9 2.3 fusion.21
  513.0 64.3 %all-reduce.21.cloned.1.call-done = bf16[512,256]{1,0:T(8,128)(2,1)} async-done(((bf16[512,256]{1,0:T(8,128)(2,1)}), bf16[512,256]{1,0:T(8,128)(2,1)}) %all-reduce.21.cloned.1.call-update) | async-done | bytes 262160 | tf_op jit(solution)/shard_map/psum | solution.py:25
  580.1 64.4 %all-reduce.23.cloned.1.call-done = bf16[512,256]{1,0:T(8,128)(2,1)} async-done(((bf16[512,256]{1,0:T(8,128)(2,1)}), bf16[512,256]{1,0:T(8,128)(2,1)}) %all-reduce.23.cloned.1.call-update) | async-done | bytes 262160 | tf_op jit(solution)/shard_map/psum | solution.py:25
  644.4 2.3 fusion.23
  647.5 64.2 %all-reduce.25.cloned.1.call-done = bf16[512,256]{1,0:T(8,128)(2,1)} async-done(((bf16[512,256]{1,0:T(8,128)(2,1)}), bf16[512,256]{1,0:T(8,128)(2,1)}) %all-reduce.25.cloned.1.call-update) | async-done | bytes 262160 | tf_op jit(solution)/shard_map/psum | solution.py:25
  714.2 64.7 %all-reduce.27.cloned.1.call-done = bf16[512,256]{1,0:T(8,128)(2,1)} async-done(((bf16[512,256]{1,0:T(8,128)(2,1)}), bf16[512,256]{1,0:T(8,128)(2,1)}) %all-reduce.27.cloned.1.call-update) | async-done | bytes 262160 | tf_op jit(solution)/shard_map/psum | solution.py:25
  778.9 2.3 fusion.25
  782.1 65.5 %all-reduce.29.cloned.1.call-done = bf16[512,256]{1,0:T(8,128)(2,1)} async-done(((bf16[512,256]{1,0:T(8,128)(2,1)}), bf16[512,256]{1,0:T(8,128)(2,1)}) %all-reduce.29.cloned.1.call-update) | async-done | bytes 262160 | tf_op jit(solution)/shard_map/psum | solution.py:25
  847.6 2.3 convolution_bitcast_fusion.9
  853.6 70.1 %all-reduce.31.cloned.1.call-done = bf16[512,256]{1,0:T(8,128)(2,1)} async-done(((bf16[512,256]{1,0:T(8,128)(2,1)}), bf16[512,256]{1,0:T(8,128)(2,1)}) %all-reduce.31.cloned.1.call-update) | async-done | bytes 262160 | tf_op jit(solution)/shard_map/psum | solution.py:25
  923.9 67.1 %all-reduce.33.cloned.1.call-done = f32[512,256]{0,1:T(8,128)} async-done(((f32[512,256]{0,1:T(8,128)}), f32[512,256]{0,1:T(8,128)}) %all-reduce.33.cloned.1.call-update) | async-done | bytes 524304 | tf_op jit(solution)/shard_map/psum | solution.py:110
  994.0 69.0 %all-reduce.35.cloned.1.call-done = f32[512,256]{0,1:T(8,128)} async-done(((f32[512,256]{0,1:T(8,128)}), f32[512,256]{0,1:T(8,128)}) %all-reduce.35.cloned.1.call-update) | async-done | bytes 524304 | tf_op jit(solution)/shard_map/psum | solution.py:110
  1066.0 69.4 %all-reduce.37.cloned.1.call-done = f32[512,256]{0,1:T(8,128)} async-done(((f32[512,256]{0,1:T(8,128)}), f32[512,256]{0,1:T(8,128)}) %all-reduce.37.cloned.1.call-update) | async-done | bytes 524304 | tf_op jit(solution)/shard_map/psum | solution.py:110
  1135.4 2.3 convolution_bitcast_fusion.5
  1137.7 68.9 %all-reduce.39.cloned.1.call-done = f32[512,256]{0,1:T(8,128)} async-done(((f32[512,256]{0,1:T(8,128)}), f32[512,256]{0,1:T(8,128)}) %all-reduce.39.cloned.1.call-update) | async-done | bytes 524304 | tf_op jit(solution)/shard_map/psum | solution.py:110
  1209.7 69.8 %all-reduce.41.cloned.1.call-done = f32[512,256]{0,1:T(8,128)} async-done(((f32[512,256]{0,1:T(8,128)}), f32[512,256]{0,1:T(8,128)}) %all-reduce.41.cloned.1.call-update) | async-done | bytes 524304 | tf_op jit(solution)/shard_map/psum | solution.py:110
  1279.5 2.3 convolution_bitcast_fusion.3
  1281.9 66.4 %all-reduce.43.cloned.1.call-done = f32[512,256]{0,1:T(8,128)} async-done(((f32[512,256]{0,1:T(8,128)}), f32[512,256]{0,1:T(8,128)}) %all-reduce.43.cloned.1.call-update) | async-done | bytes 524304 | tf_op jit(solution)/shard_map/psum | solution.py:110
  1351.3 70.0 %all-reduce.45.cloned.1.call-done = f32[512,256]{0,1:T(8,128)} async-done(((f32[512,256]{0,1:T(8,128)}), f32[512,256]{0,1:T(8,128)}) %all-reduce.45.cloned.1.call-update) | async-done | bytes 524304 | tf_op jit(solution)/shard_map/psum | solution.py:110
  1423.6 67.7 %all-reduce.47.cloned.1.call-done = f32[512,256]{0,1:T(8,128)} async-done(((f32[512,256]{0,1:T(8,128)}), f32[512,256]{0,1:T(8,128)}) %all-reduce.47.cloned.1.call-update) | async-done | bytes 524304 | tf_op jit(solution)/shard_map/psum | solution.py:110
  1491.3 5.5 conditional.31
  1493.3 2.4 fusion.16
  1497.6 26.7 %all-gather.2.cloned.1.call-done = bf16[4096,256]{1,0:T(8,128)(2,1)} async-done(((bf16[512,256]{1,0:T(8,128)(2,1)}), bf16[4096,256]{1,0:T(8,128)(2,1)}) %all-gather.2.cloned.1.call-update) | async-done | bytes 2097168 | tf_op jit(solution)/shard_map/all_gather | solution.py:127
  1524.3 3.5 collective-permute-start.2
  1527.8 5.7 collective-permute-start.3
  1533.7 85.1 %collective-permute-done.2 = bf16[4096,256]{1,0:T(8,128)(2,1)} collective-permute-done((bf16[4096,256]{1,0:T(8,128)(2,1)}, bf16[4096,256]{1,0:T(8,128)(2,1)}, u32[]{:S(2)}, u32[]{:S(2)}) %collective-permute-start.2) | collective-permute-done | bytes 2097184 | tf_op jit(solution)/shard_map/ppermute | solution.py:20
  1618.8 47.4 %collective-permute-done.3 = bf16[4096,256]{1,0:T(8,128)(2,1)} collective-permute-done((bf16[4096,256]{1,0:T(8,128)(2,1)}, bf16[4096,256]{1,0:T(8,128)(2,1)}, u32[]{:S(2)}, u32[]{:S(2)}) %collective-permute-start.3) | collective-permute-done | bytes 2097184 | tf_op jit(solution)/shard_map/ppermute | solution.py:20
  1666.2 6.4 pad_maximum_fusion
  1672.6 10.5 reshape.571
  1683.1 4.9 gather_fusion
  1688.3 3.8 fusion.19
  (121 shorter events, 54.1 us)
Async XLA Ops:
  7.2 1.7 copy-start
  7.2 367.2 %reduce-scatter.2.cloned.1.call-start = ((), (), s32[]{:S(2)}) async-start(), calls=%async_computation.1 | async-start | bytes 4718592 | tf_op jit(solution)/shard_map/reduce_scatter | solution.py:70
  8.9 3.0 copy-start.4
  10.9 1.0 copy-start.5
  47.4 96.2 %collective-permute-start = (f32[4096,256]{0,1:T(8,128)}, f32[4096,256]{0,1:T(8,128)}, u32[]{:S(2)}, u32[]{:S(2)}) collective-permute-start(f32[4096,256]{0,1:T(8,128)} %copy.46), channel_id=1, source_target_pairs={{8,0},{16,8},{24,16},{32,24},{40,32},{48,40},{56,48},{64,56},{72,6... | collective-permute-start | bytes 12582920 | tf_op jit(solution)/shard_map/ppermute | solution.py:20
  60.1 175.3 %collective-permute-start.1 = (f32[4096,256]{0,1:T(8,128)}, f32[4096,256]{0,1:T(8,128)}, u32[]{:S(2)}, u32[]{:S(2)}) collective-permute-start(f32[4096,256]{0,1:T(8,128)} %copy.48), channel_id=1, source_target_pairs={{16,0},{24,8},{32,16},{40,24},{48,32},{56,40},{64,48},{72,56},{80,... | collective-permute-start | bytes 12582920 | tf_op jit(solution)/shard_map/ppermute | solution.py:20
  243.2 0.9 copy-start.7
  243.2 133.0 %copy-start.1 = (bf16[512,512]{1,0:T(8,128)(2,1)S(1)}, bf16[512,512]{1,0:T(8,128)(2,1)}, u32[]{:S(2)}) copy-start(bf16[512,512]{1,0:T(8,128)(2,1)} %param.78) | copy-start | bytes 1572868
  243.3 199.5 %all-reduce.17.cloned.1.call-start = ((), (), s32[]{:S(2)}) async-start(), calls=%async_computation.2 | async-start | bytes 524288 | tf_op jit(solution)/shard_map/psum | solution.py:25
  378.7 131.2 %all-reduce.19.cloned.1.call-start = ((), (), s32[]{:S(2)}) async-start(), calls=%async_computation.3 | async-start | bytes 524288 | tf_op jit(solution)/shard_map/psum | solution.py:25
  445.2 132.2 %all-reduce.21.cloned.1.call-start = ((), (), s32[]{:S(2)}) async-start(), calls=%async_computation.4 | async-start | bytes 524288 | tf_op jit(solution)/shard_map/psum | solution.py:25
  513.0 131.4 %all-reduce.23.cloned.1.call-start = ((), (), s32[]{:S(2)}) async-start(), calls=%async_computation.5 | async-start | bytes 524288 | tf_op jit(solution)/shard_map/psum | solution.py:25
  580.0 131.8 %all-reduce.25.cloned.1.call-start = ((), (), s32[]{:S(2)}) async-start(), calls=%async_computation.6 | async-start | bytes 524288 | tf_op jit(solution)/shard_map/psum | solution.py:25
  647.5 131.5 %all-reduce.27.cloned.1.call-start = ((), (), s32[]{:S(2)}) async-start(), calls=%async_computation.7 | async-start | bytes 524288 | tf_op jit(solution)/shard_map/psum | solution.py:25
  714.2 133.4 %all-reduce.29.cloned.1.call-start = ((), (), s32[]{:S(2)}) async-start(), calls=%async_computation.8 | async-start | bytes 524288 | tf_op jit(solution)/shard_map/psum | solution.py:25
  782.0 141.7 %all-reduce.31.cloned.1.call-start = ((), (), s32[]{:S(2)}) async-start(), calls=%async_computation.9 | async-start | bytes 524288 | tf_op jit(solution)/shard_map/psum | solution.py:25
  782.1 141.7 %copy-start.6 = (bf16[512,256]{1,0:T(8,128)(2,1)S(1)}, bf16[512,256]{1,0:T(8,128)(2,1)}, u32[]{:S(2)}) copy-start(bf16[512,256]{1,0:T(8,128)(2,1)} %all-reduce.17.cloned.1.call-done) | copy-start | bytes 786436
  851.3 139.6 %all-reduce.33.cloned.1.call-start = ((), (), s32[]{:S(2)}) async-start(), calls=%async_computation.10 | async-start | bytes 1048576 | tf_op jit(solution)/shard_map/psum | solution.py:110
  853.6 209.4 %all-reduce.35.cloned.1.call-start = ((), (), s32[]{:S(2)}) async-start(), calls=%async_computation.11 | async-start | bytes 1048576 | tf_op jit(solution)/shard_map/psum | solution.py:110
  993.9 141.4 %all-reduce.37.cloned.1.call-start = ((), (), s32[]{:S(2)}) async-start(), calls=%async_computation.12 | async-start | bytes 1048576 | tf_op jit(solution)/shard_map/psum | solution.py:110
  1065.9 140.7 %all-reduce.39.cloned.1.call-start = ((), (), s32[]{:S(2)}) async-start(), calls=%async_computation.13 | async-start | bytes 1048576 | tf_op jit(solution)/shard_map/psum | solution.py:110
  1135.4 72.0 %copy-start.2 = (bf16[512,256]{1,0:T(8,128)(2,1)}, bf16[512,256]{1,0:T(8,128)(2,1)S(1)}, u32[]{:S(2)}) copy-start(bf16[512,256]{1,0:T(8,128)(2,1)S(1)} %get-tuple-element.460) | copy-start | bytes 786436
  1137.7 141.8 %all-reduce.41.cloned.1.call-start = ((), (), s32[]{:S(2)}) async-start(), calls=%async_computation.14 | async-start | bytes 1048576 | tf_op jit(solution)/shard_map/psum | solution.py:110
  1209.6 138.6 %all-reduce.43.cloned.1.call-start = ((), (), s32[]{:S(2)}) async-start(), calls=%async_computation.15 | async-start | bytes 1048576 | tf_op jit(solution)/shard_map/psum | solution.py:110
  1279.5 69.5 %copy-start.3 = (bf16[512,256]{1,0:T(8,128)(2,1)}, bf16[512,256]{1,0:T(8,128)(2,1)S(1)}, u32[]{:S(2)}) copy-start(bf16[512,256]{1,0:T(8,128)(2,1)S(1)} %get-tuple-element.462) | copy-start | bytes 786436
  1281.8 139.4 %all-reduce.45.cloned.1.call-start = ((), (), s32[]{:S(2)}) async-start(), calls=%async_computation.16 | async-start | bytes 1048576 | tf_op jit(solution)/shard_map/psum | solution.py:110
  1351.2 140.1 %all-reduce.47.cloned.1.call-start = ((), (), s32[]{:S(2)}) async-start(), calls=%async_computation.17 | async-start | bytes 1048576 | tf_op jit(solution)/shard_map/psum | solution.py:110
  1423.5 100.8 %all-gather.2.cloned.1.call-start = ((), (), s32[]{:S(2)}) async-start(), calls=%async_computation.18 | async-start | bytes 2359296 | tf_op jit(solution)/shard_map/all_gather | solution.py:127
  1524.3 94.5 %collective-permute-start.2 = (bf16[4096,256]{1,0:T(8,128)(2,1)}, bf16[4096,256]{1,0:T(8,128)(2,1)}, u32[]{:S(2)}, u32[]{:S(2)}) collective-permute-start(bf16[4096,256]{1,0:T(8,128)(2,1)} %all-gather.2.cloned.1.call-done), channel_id=1, source_target_pairs={{0,8},{8,16},{16,24},{24,32},{32,40},{40,48},{48,56},{56,64},{64,7... | collective-permute-start | bytes 6291464 | tf_op jit(solution)/shard_map/ppermute | solution.py:20
  1527.8 138.4 %collective-permute-start.3 = (bf16[4096,256]{1,0:T(8,128)(2,1)}, bf16[4096,256]{1,0:T(8,128)(2,1)}, u32[]{:S(2)}, u32[]{:S(2)}) collective-permute-start(bf16[4096,256]{1,0:T(8,128)(2,1)} %all-gather.2.cloned.1.call-done), channel_id=1, source_target_pairs={{0,16},{8,24},{16,32},{24,40},{32,48},{40,56},{48,64},{56,72},{64,... | collective-permute-start | bytes 6291464 | tf_op jit(solution)/shard_map/ppermute | solution.py:20
Sparse Core Ops, SparseCore 0:
  243.4 130.9 reduce-scatter.1
  378.9 63.8 all-reduce.16
  445.7 64.1 all-reduce.18
  513.1 64.2 all-reduce.20
  580.2 64.1 all-reduce.22
  647.6 64.1 all-reduce.24
  714.8 64.1 all-reduce.26
  782.1 65.4 all-reduce.28
  851.5 72.2 all-reduce.30
  925.9 65.0 all-reduce.32
  994.0 68.8 all-reduce.34
  1066.0 69.2 all-reduce.36
  1137.8 68.7 all-reduce.38
  1209.7 69.6 all-reduce.40
  1281.9 66.2 all-reduce.42
  1351.3 69.8 all-reduce.44
  1423.6 67.6 all-reduce.46
  1497.7 26.5 all-gather.1
where the time goes:
time: 1700 us
  waiting for transfers between devices  1520 us (89%)
  local copies, waits for them, and re-layouts  73.3 us (4%)
  matrix products  52.2 us (3%)
  other arithmetic  24.6 us (1%)
  starting transfers between devices  20.3 us (1%)
    psum x8, waiting for transfers between devices, shards(): summed_later = lax.psum(partial_term, 'sub')  548 us
    psum x8, waiting for transfers between devices, broadcast(): return lax.psum(jnp.where(mine, shard, jnp.zeros_like(shard)), axis)  522 us
    ppermute x4, waiting for transfers between devices, passed_along(): return lax.ppermute(block, axis, route)  289 us
    reduce_scatter x1, waiting for transfers between devices, shards(): lax.psum_scatter(route_forward(spilled), 'sub', scatter_dimension=0, tile...  130 us
  transfers between devices with their start and end apart: 22, of which 22 were waited for; matrix products, arithmetic and copies ran while one was open for 1% of the time, Pallas kernels for 0%

commit v1 on v0

v1 whole, which is shorter than its diff:
```python
import jax
import jax.numpy as jnp
from jax import lax
from jax.experimental import pallas as pl
from jax.experimental.pallas import tpu as pltpu
from jax.sharding import PartitionSpec as P

W = 512
WSN = 512
SA = 4096
R = 256
BLK = 64
KB = 4
SPAN = 3
SN_DEV = 4
GROUP = 8
COLS = R // GROUP
CHUNKS = SA // 128
UPD = SN_DEV * KB * BLK
SEND = UPD + WSN
HUB = 3
bf16 = jnp.bfloat16
f32 = jnp.float32
NT = (((1,), (1,)), ((), ()))
NN = (((1,), (0,)), ((), ()))
MIB = 1 << 20


def dot(a, b, dims):
    return lax.dot_general(a, b, dims, preferred_element_type=f32)


def leaf_forward_kernel(right, inverse, panel, sep_right, y_out, send):
    j = pl.program_id(0)
    y = dot(right[0].T, inverse[0], NT).astype(bf16)
    y_out[0] = y
    send[:, pl.ds(pl.multiple_of(j * KB * BLK, 128), KB * BLK)] = dot(y, panel[0], NT).astype(bf16)

    @pl.when(j == 0)
    def _():
        send[:, UPD:] = sep_right[...].T


def leaf_forward(right, inverse, panels, sep_right):
    return pl.pallas_call(
        leaf_forward_kernel,
        grid=(SN_DEV,),
        in_specs=[
            pl.BlockSpec((1, W, R), lambda j: (j, 0, 0)),
            pl.BlockSpec((1, W, W), lambda j: (j, 0, 0)),
            pl.BlockSpec((1, KB * BLK, W), lambda j: (j, 0, 0)),
            pl.BlockSpec((WSN, R), lambda j: (0, 0)),
        ],
        out_specs=[
            pl.BlockSpec((1, R, W), lambda j: (j, 0, 0)),
            pl.BlockSpec((R, SEND), lambda j: (0, 0)),
        ],
        out_shape=[
            jax.ShapeDtypeStruct((SN_DEV, R, W), bf16),
            jax.ShapeDtypeStruct((R, SEND), bf16),
        ],
        compiler_params=pltpu.CompilerParams(dimension_semantics=("arbitrary",), vmem_limit_bytes=24 * MIB),
        name="leaf_forward",
    )(right, inverse, panels, sep_right)


def scatter_kernel(slots, received, base, near, far, table):
    table[...] = jnp.zeros_like(table)
    high = lax.broadcasted_iota(jnp.int32, (COLS, 128), 1) >= BLK

    def from_member(s, carry):
        for i in range(UPD // 128):
            pair = received[s, :, 128 * i : 128 * i + 128].astype(f32)
            turned = pltpu.roll(pair, BLK, 1)
            for h in range(2):
                slot = slots[16 * s + 2 * i + h]
                want_high = (slot & 1) == 1
                moved = jnp.where(want_high, turned if h == 0 else pair, pair if h == 0 else turned)
                row = slot >> 1
                table[row] = table[row] + jnp.where(high == want_high, moved, 0.0)
        return carry

    lax.fori_loop(0, GROUP, from_member, 0)
    for c in range(CHUNKS):
        first = UPD + 128 * (c % 4)
        base[c] = received[c // 4, :, first : first + 128].astype(f32) - table[c]
        near[c] = table[CHUNKS + c].astype(bf16)
        far[c] = table[2 * CHUNKS + c].astype(bf16)


def scatter(slots, received):
    share = (CHUNKS, COLS, 128)
    return pl.pallas_call(
        scatter_kernel,
        in_specs=[pl.BlockSpec(memory_space=pltpu.SMEM), pl.BlockSpec(memory_space=pltpu.VMEM)],
        out_specs=[pl.BlockSpec(memory_space=pltpu.VMEM)] * 3,
        out_shape=[
            jax.ShapeDtypeStruct(share, f32),
            jax.ShapeDtypeStruct(share, bf16),
            jax.ShapeDtypeStruct(share, bf16),
        ],
        scratch_shapes=[pltpu.VMEM((SPAN * CHUNKS, COLS, 128), f32)],
        compiler_params=pltpu.CompilerParams(vmem_limit_bytes=16 * MIB),
        name="scatter_updates",
    )(slots, received)


def sweep_kernel(where, *refs):
    rhs = refs[0:4]
    wide = refs[4:10]
    inverse = refs[10:18]
    beside = refs[18:26]
    outs = refs[26:30]
    lower, diagonal, state, lower_sem, diagonal_sem, beside_sem = refs[30:]
    core = where[1]

    def rows_of(k, same):
        q = 2 * k + (core if same else 1 - core)
        return pl.ds(pl.multiple_of(q * WSN, WSN), WSN)

    @pl.when(where[0] == HUB)
    def _():
        for k in range(4):
            for same in (0, 1):
                dst = diagonal.at[rows_of(k, same == 0)]
                pltpu.make_async_copy(inverse[2 * k + same], dst, diagonal_sem.at[k]).start()
            for same in (0, 1):

                @pl.when(core == 1 - same)
                def _():
                    dst = lower.at[(2 * k + 1) * WSN : (2 * k + 2) * WSN, 2 * k * WSN : (2 * k + 1) * WSN]
                    pltpu.make_async_copy(beside[2 * k + same], dst, beside_sem.at[k]).start()

            if k > 0:
                for same in (0, 1):
                    dst = lower.at[rows_of(k, same == 0), 0 : 2 * k * WSN]
                    pltpu.make_async_copy(wide[2 * (k - 1) + same], dst, lower_sem.at[k]).start()
        for k in range(4):
            for c in range(CHUNKS):
                state[COLS * k : COLS * k + COLS, 128 * c : 128 * c + 128] = rhs[k][c]
        for q in range(8):
            k = q // 2
            if q % 2 == 0:
                both = diagonal.at[2 * k * WSN : (2 * k + 2) * WSN]
                pltpu.make_async_copy(both, both, diagonal_sem.at[k]).wait()
                single = lower.at[(2 * k + 1) * WSN : (2 * k + 2) * WSN, 2 * k * WSN : (2 * k + 1) * WSN]
                pltpu.make_async_copy(single, single, beside_sem.at[k]).wait()
                if k > 0:
                    slab = lower.at[2 * k * WSN : (2 * k + 2) * WSN, 0 : 2 * k * WSN]
                    pltpu.make_async_copy(slab, slab, lower_sem.at[k]).wait()
            here = slice(q * WSN, (q + 1) * WSN)
            bracket = state[:, here].astype(f32)
            if q > 0:
                bracket = bracket - dot(state[:, : q * WSN], lower[here, : q * WSN], NT)
            state[:, here] = by_inverse(bracket, diagonal[here], NT)
        for q in reversed(range(8)):
            here = slice(q * WSN, (q + 1) * WSN)
            bracket = state[:, here].astype(f32)
            if q < 7:
                bracket = bracket - dot(state[:, (q + 1) * WSN :], lower[(q + 1) * WSN :, here], NN)
            solved = by_inverse(bracket, diagonal[here], NN)
            state[:, here] = solved
            for k in range(4):
                for t in range(4):
                    outs[k][4 * q + t] = solved[COLS * k : COLS * k + COLS, 128 * t : 128 * t + 128]


def by_inverse(bracket, block, dims):
    head = bracket.astype(bf16)
    tail = (bracket - head.astype(f32)).astype(bf16)
    return (dot(head, block, dims) + dot(tail, block, dims)).astype(bf16)


def sweeps(where, rhs, wide, inverse, beside):
    share = (CHUNKS, COLS, 128)
    anywhere = pl.BlockSpec(memory_space=pl.ANY)
    return pl.pallas_call(
        sweep_kernel,
        in_specs=[pl.BlockSpec(memory_space=pltpu.SMEM)]
        + [pl.BlockSpec(memory_space=pltpu.VMEM)] * 4
        + [anywhere] * 22,
        out_specs=[pl.BlockSpec(memory_space=pltpu.VMEM)] * 4,
        out_shape=[jax.ShapeDtypeStruct(share, bf16)] * 4,
        scratch_shapes=[
            pltpu.VMEM((SA, 7 * WSN), bf16),
            pltpu.VMEM((SA, WSN), bf16),
            pltpu.VMEM((4 * COLS, SA), bf16),
            pltpu.SemaphoreType.DMA((4,)),
            pltpu.SemaphoreType.DMA((4,)),
            pltpu.SemaphoreType.DMA((4,)),
        ],
        compiler_params=pltpu.CompilerParams(vmem_limit_bytes=48 * MIB),
        name="sweeps",
    )(where, *rhs, *wide, *inverse, *beside)


def extract_kernel(slots, own, near, far, send, table):
    for d, ref in enumerate((own, near, far)):
        for c in range(CHUNKS):
            table[d * CHUNKS + c] = ref[c].astype(f32)
    high = lax.broadcasted_iota(jnp.int32, (COLS, 128), 1) >= BLK

    def for_member(s, carry):
        for i in range(UPD // 128):
            halves = []
            for h in range(2):
                slot = slots[16 * s + 2 * i + h]
                pair = table[slot >> 1]
                halves.append(jnp.where((slot & 1) == h, pair, pltpu.roll(pair, BLK, 1)))
            send[s, :, 128 * i : 128 * i + 128] = jnp.where(high, halves[1], halves[0]).astype(bf16)
        for t in range(4):
            send[s, :, UPD + 128 * t : UPD + 128 * t + 128] = own[4 * s + t]
        return carry

    lax.fori_loop(0, GROUP, for_member, 0)


def extract(slots, own, near, far):
    return pl.pallas_call(
        extract_kernel,
        in_specs=[pl.BlockSpec(memory_space=pltpu.SMEM)] + [pl.BlockSpec(memory_space=pltpu.VMEM)] * 3,
        out_specs=pl.BlockSpec(memory_space=pltpu.VMEM),
        out_shape=jax.ShapeDtypeStruct((GROUP, COLS, SEND), bf16),
        scratch_shapes=[pltpu.VMEM((SPAN * CHUNKS, COLS, 128), f32)],
        compiler_params=pltpu.CompilerParams(vmem_limit_bytes=16 * MIB),
        name="extract_pieces",
    )(slots, own, near, far)


def leaf_backward_kernel(y, pieces, inverse, panel, rows, leaf_x, sep_x):
    inner = (y[0].astype(f32) - dot(pieces[...], panel[0], NN)).astype(bf16)
    leaf_x[0] = dot(inner, inverse[0], NN).astype(bf16).T

    @pl.when(pl.program_id(0) == 0)
    def _():
        sep_x[...] = rows[...].T


def leaf_backward(y, received, inverse, panels):
    return pl.pallas_call(
        leaf_backward_kernel,
        grid=(SN_DEV,),
        in_specs=[
            pl.BlockSpec((1, R, W), lambda j: (j, 0, 0)),
            pl.BlockSpec((R, KB * BLK), lambda j: (0, j)),
            pl.BlockSpec((1, W, W), lambda j: (j, 0, 0)),
            pl.BlockSpec((1, KB * BLK, W), lambda j: (j, 0, 0)),
            pl.BlockSpec((R, WSN), lambda j: (0, UPD // WSN)),
        ],
        out_specs=[
            pl.BlockSpec((1, W, R), lambda j: (j, 0, 0)),
            pl.BlockSpec((WSN, R), lambda j: (0, 0)),
        ],
        out_shape=[
            jax.ShapeDtypeStruct((SN_DEV, W, R), bf16),
            jax.ShapeDtypeStruct((WSN, R), bf16),
        ],
        compiler_params=pltpu.CompilerParams(dimension_semantics=("arbitrary",), vmem_limit_bytes=24 * MIB),
        name="leaf_backward",
    )(y, received, inverse, panels, received)


def along_leaf(block, distance):
    devices = range(lax.axis_size("leaf"))
    route = [(i - distance, i) for i in devices if i - distance in devices]
    return lax.ppermute(block, "leaf", route)


def hop(block, *chips, cores=(0, 1)):
    return lax.ppermute(block, "sub", [(2 * a + c, 2 * b + c) for a, b in chips for c in cores])


def swap(block, cores=(0, 1)):
    return lax.ppermute(block, "sub", [(2 * HUB + c, 2 * HUB + 1 - c) for c in cores])


def gather_factor(factor, inverse, chip):
    beside = lax.dynamic_slice(factor, (0, 2 * WSN * chip), (WSN, WSN))
    inv_near = hop(inverse, (0, 3), (1, 0))
    beside_near = hop(beside, (0, 3), (1, 0), cores=(1,))
    inv2 = hop(inverse, (2, 3))
    beside2 = hop(beside, (2, 3), cores=(1,))
    wide1_way = hop(factor[:, : 2 * WSN], (1, 0))
    wide2 = hop(factor[:, : 4 * WSN], (2, 3))
    inv1 = hop(inv_near, (0, 3))
    beside1 = hop(beside_near, (0, 3), cores=(1,))
    wide1 = hop(wide1_way, (0, 3))
    wide3 = factor[:, : 6 * WSN]
    inverses, besides, wides = [], [], []
    for block in (inv_near, inv1, inv2, inverse):
        inverses += [block, swap(block)]
    for block in (beside_near, beside1, beside2, beside):
        besides += [block, swap(block, cores=(1,))]
    for block in (wide1, wide2, wide3):
        wides += [block, swap(block)]
    return wides, inverses, besides


def shards(
    leaf_right,
    leaf_inverse,
    panels,
    leaf_subtree,
    panel_block,
    separator_right,
    separator_inverse,
    separator_factor,
):
    section = lax.axis_index("leaf")
    member = lax.axis_index("sub")
    chip, core = member // 2, member % 2
    row_blocks = SA // BLK
    own_slots = ((section - leaf_subtree)[:, None] * row_blocks + panel_block).reshape(-1)
    slots = lax.all_gather(own_slots, "sub", axis=0, tiled=True)
    wides, inverses, besides = gather_factor(separator_factor, separator_inverse, chip)
    y, send = leaf_forward(leaf_right, leaf_inverse, panels, separator_right)
    received = lax.all_to_all(send.reshape(GROUP, COLS, SEND), "sub", 0, 0, tiled=True)
    base, near, far = scatter(slots, received)
    near_sum = along_leaf(near, -1).astype(f32)
    far_sum = along_leaf(far, -2).astype(f32)
    rhs = (base - near_sum - far_sum).astype(bf16)
    to_hub = [hop(rhs, (k, HUB)) for k in range(3)] + [rhs]
    where = jnp.stack([chip, core]).astype(jnp.int32)
    shares = sweeps(where, to_hub, wides, inverses, besides)
    own = shares[3]
    back = [hop(shares[k], (HUB, k)) for k in range(3)]
    own = jnp.where(chip == 3, own, jnp.where(chip == 2, back[2], jnp.where(chip == 1, back[1], back[0])))
    pieces = extract(slots, own, along_leaf(own, 1), along_leaf(own, 2))
    pieces = lax.all_to_all(pieces, "sub", 0, 0, tiled=True).reshape(R, SEND)
    return tuple(leaf_backward(y, pieces, leaf_inverse, panels))


def solution(mesh):
    placed = (
        P(("leaf", "sub"), None, None),
        P(("leaf", "sub"), None, None),
        P(("leaf", "sub"), None, None),
        P(("leaf", "sub")),
        P(("leaf", "sub"), None),
        P(("leaf", "sub"), None),
        P(("leaf", "sub"), None),
        P(("leaf", "sub"), None),
    )
    return jax.shard_map(
        shards,
        mesh=mesh,
        in_specs=placed,
        out_specs=(P(("leaf", "sub"), None, None), P(("leaf", "sub"), None)),
        check_vma=False,
    )
```

time: 1700 us -> 264 us (0.16)
  the two profiles are of different devices: /device:TPU:38 before, /device:TPU:6 now
where the time goes in v1:
time: 264 us; the launch traced here: 262 us
  waiting for transfers between devices  94.4 us (36%)
  starting transfers between devices  67 us (25%)
  blocking collectives  62.2 us (24%)
  local copies, waits for them, and re-layouts  24.6 us (9%)
  Pallas kernels  11.1 us (4%)
    ppermute x15, waiting for transfers between devices, hop(): lax.ppermute(block, 'sub', [(2 * a + c, 2 * b + c) for a, b in chips for...  64.1 us
    unnamed x1, blocking collectives  44.7 us
    ppermute x4, waiting for transfers between devices, along_leaf(): return lax.ppermute(block, 'leaf', route)  30.3 us
    ppermute x15, starting transfers between devices, hop(): lax.ppermute(block, 'sub', [(2 * a + c, 2 * b + c) for a, b in chips for...  29.5 us
    ppermute x4, starting transfers between devices, along_leaf(): return lax.ppermute(block, 'leaf', route)  18.1 us
    all_to_all x1, blocking collectives, shards(): pieces = lax.all_to_all(pieces, 'sub', 0, 0, tiled=True).reshape(R, SEND)  17.5 us
    ppermute x11, starting transfers between devices, swap(): lax.ppermute(block, 'sub', [(2 * HUB + c, 2 * HUB + 1 - c) for c in cores])  14.6 us
    unnamed x49, local copies, waits for them, and re-layouts  13.4 us
  transfers between devices with their start and end apart: 31, of which 8 were waited for; matrix products, arithmetic and copies ran while one was open for 3% of the time, Pallas kernels for 2%

profile of v1, /device:TPU:6, one launch (start us, length us, event | category | flops | bytes accessed | tf_op | source)
XLA Modules:
  0.0 262.4 jit_solution(7295383518065924345)
XLA Ops:
  0.7 3.3 %slice.10 = bf16[512,2048]{1,0:T(8,128)(2,1)} slice(bf16[512,4096]{1,0:T(8,128)(2,1)} %param.15), slice={[0:512], [0:2048]} | slice | bytes 4194304 | tf_op jit(solution)/shard_map/slice | solution.py:284
  4.0 2.0 collective-permute-start.8
  6.0 4.2 %collective-permute-start.11 = (bf16[512,512]{1,0:T(8,128)(2,1)}, bf16[512,512]{1,0:T(8,128)(2,1)}, u32[]{:S(2)}, u32[]{:S(2)}) collective-permute-start(bf16[512,512]{1,0:T(8,128)(2,1)} %refs_16_.1), channel_id=1, source_target_pairs={{0,6},{1,7},{2,0},{3,1},{8,14},{9,15},{10,8},{11,9},{16,22},{17,23... | collective-permute-start | bytes 1572872 | tf_op jit(solution)/shard_map/ppermute | solution.py:270
  10.2 1.5 collective-permute-start.15
  11.7 1.5 collective-permute-start.17
  13.1 1.9 constant_dynamic-slice_fusion.refs_24_
  15.0 1.5 collective-permute-start.18
  16.5 1.2 copy-done.2
  17.7 2.2 leaf_forward.1
  19.9 1.0 copy-done.3
  21.7 4.9 %all-to-all-start = ((bf16[8,32,1536]{2,1,0:T(8,128)(2,1)}), bf16[8,32,1536]{2,1,0:T(8,128)(2,1)}, u32[]{:S(2)}, u32[]{:S(2)}) async-start(bf16[8,32,1536]{2,1,0:T(8,128)(2,1)} %bitcast.7), calls=%async_computation | async-start | bytes 1572864 | tf_op jit(solution)/shard_map/all_to_all | solution.py:317
  26.6 1.5 collective-permute-start.22
  28.1 2.2 slice.9
  30.3 3.8 %slice.11.refs_8_ = bf16[512,3072]{1,0:T(8,128)(2,1)} slice(bf16[512,4096]{1,0:T(8,128)(2,1)} %param.15), slice={[0:512], [0:3072]} | slice | bytes 6291456 | tf_op jit(solution)/shard_map/slice | solution.py:288
  34.1 1.5 collective-permute-start.24
  35.6 1.3 collective-permute-start.5
  36.9 2.3 collective-permute-start.10
  40.9 44.7 %all-reduce.slots = s32[128]{0:T(128)S(1)} all-reduce(s32[128]{0:T(128)S(1)} %dynamic-update-slice), channel_id=1, replica_groups=mesh['leaf'=32,'sub'=8] {'sub'}, use_global_device_ids=true, to_apply=%add | all-reduce | flops 128 | bytes 1024
  85.6 2.5 scatter_updates.1
  88.1 8.5 %collective-permute-start.1 = (bf16[32,32,128]{2,1,0:T(8,128)(2,1)S(1)}, bf16[32,32,128]{2,1,0:T(8,128)(2,1)S(1)}, u32[]{:S(2)}, u32[]{:S(2)}) collective-permute-start(bf16[32,32,128]{2,1,0:T(8,128)(2,1)S(1)} %get-tuple-element.15), channel_id=1, source_target_pairs={{16,0},{24,8},{32,16},{40,24},{48,32},{56,40},{64,48},{72,56},{80,... | collective-permute-start | bytes 786440 | tf_op jit(solution)/shard_map/ppermute | solution.py:266
  96.6 2.9 %collective-permute-start = (bf16[32,32,128]{2,1,0:T(8,128)(2,1)S(1)}, bf16[32,32,128]{2,1,0:T(8,128)(2,1)S(1)}, u32[]{:S(2)}, u32[]{:S(2)}) collective-permute-start(bf16[32,32,128]{2,1,0:T(8,128)(2,1)S(1)} %get-tuple-element.14), channel_id=1, source_target_pairs={{8,0},{16,8},{24,16},{32,24},{40,32},{48,40},{56,48},{64,56},{72,6... | collective-permute-start | bytes 786440 | tf_op jit(solution)/shard_map/ppermute | solution.py:266
  99.5 8.4 %collective-permute-done.1 = bf16[32,32,128]{2,1,0:T(8,128)(2,1)S(1)} collective-permute-done((bf16[32,32,128]{2,1,0:T(8,128)(2,1)S(1)}, bf16[32,32,128]{2,1,0:T(8,128)(2,1)S(1)}, u32[]{:S(2)}, u32[]{:S(2)}) %collective-permute-start.1) | collective-permute-done | bytes 262176 | tf_op jit(solution)/shard_map/ppermute | solution.py:266
  108.6 3.7 %collective-permute-done = bf16[32,32,128]{2,1,0:T(8,128)(2,1)S(1)} collective-permute-done((bf16[32,32,128]{2,1,0:T(8,128)(2,1)S(1)}, bf16[32,32,128]{2,1,0:T(8,128)(2,1)S(1)}, u32[]{:S(2)}, u32[]{:S(2)}) %collective-permute-start) | collective-permute-done | bytes 262176 | tf_op jit(solution)/shard_map/ppermute | solution.py:266
  112.3 2.1 collective-permute-start.13
  115.8 2.2 collective-permute-start.6
  118.1 2.0 collective-permute-start.9
  120.1 6.2 %collective-permute-done.13.refs_12_ = bf16[512,512]{1,0:T(8,128)(2,1)} collective-permute-done((bf16[512,512]{1,0:T(8,128)(2,1)}, bf16[512,512]{1,0:T(8,128)(2,1)}, u32[]{:S(2)}, u32[]{:S(2)}) %collective-permute-start.13) | collective-permute-done | bytes 524320 | tf_op jit(solution)/shard_map/ppermute | solution.py:270
  127.7 1.5 collective-permute-start.20
  130.2 7.1 %collective-permute-start.2 = (bf16[32,32,128]{2,1,0:T(8,128)(2,1)S(1)}, bf16[32,32,128]{2,1,0:T(8,128)(2,1)S(1)}, u32[]{:S(2)}, u32[]{:S(2)}) collective-permute-start(bf16[32,32,128]{2,1,0:T(8,128)(2,1)S(1)} %subtract_convert_fusion.refs_3_), channel_id=1, source_target_pairs={{0,6},{1,7},{8,14},{9,15},{16,22},{17,23},{24,30},{25,31},{32,38},... | collective-permute-start | bytes 786440 | tf_op jit(solution)/shard_map/ppermute | solution.py:270
  137.3 11.4 %collective-permute-done.6.refs_4_ = bf16[512,1024]{1,0:T(8,128)(2,1)} collective-permute-done((bf16[512,1024]{1,0:T(8,128)(2,1)}, bf16[512,1024]{1,0:T(8,128)(2,1)}, u32[]{:S(2)}, u32[]{:S(2)}) %collective-permute-start.6) | collective-permute-done | bytes 1048608 | tf_op jit(solution)/shard_map/ppermute | solution.py:270
  148.7 1.7 collective-permute-start.7
  151.1 3.1 %collective-permute-done.2.refs_0_ = bf16[32,32,128]{2,1,0:T(8,128)(2,1)S(1)} collective-permute-done((bf16[32,32,128]{2,1,0:T(8,128)(2,1)S(1)}, bf16[32,32,128]{2,1,0:T(8,128)(2,1)S(1)}, u32[]{:S(2)}, u32[]{:S(2)}) %collective-permute-start.2) | collective-permute-done | bytes 262176 | tf_op jit(solution)/shard_map/ppermute | solution.py:270
  156.3 1.4 collective-permute-start.14
  158.5 1.4 collective-permute-start.21
  160.1 1.0 copy-done.7
  161.1 1.0 copy-done.9
  165.0 1.7 sweeps.1
  168.1 1.4 collective-permute-start.26
  169.4 1.3 collective-permute-start.27
  170.8 43.3 %collective-permute-done.27 = bf16[32,32,128]{2,1,0:T(8,128)(2,1)} collective-permute-done((bf16[32,32,128]{2,1,0:T(8,128)(2,1)}, bf16[32,32,128]{2,1,0:T(8,128)(2,1)}, u32[]{:S(2)}, u32[]{:S(2)}) %collective-permute-start.27) | collective-permute-done | bytes 262176 | tf_op jit(solution)/shard_map/ppermute | solution.py:270
  214.1 1.0 select_select_fusion.own
  215.1 1.9 collective-permute-start.28
  217.0 4.8 %collective-permute-start.29 = (bf16[32,32,128]{2,1,0:T(8,128)(2,1)S(1)}, bf16[32,32,128]{2,1,0:T(8,128)(2,1)S(1)}, u32[]{:S(2)}, u32[]{:S(2)}) collective-permute-start(bf16[32,32,128]{2,1,0:T(8,128)(2,1)S(1)} %select_select_fusion.own), channel_id=1, source_target_pairs={{0,16},{8,24},{16,32},{24,40},{32,48},{40,56},{48,64},{56,72},{64,... | collective-permute-start | bytes 786440 | tf_op jit(solution)/shard_map/ppermute | solution.py:266
  221.9 7.1 %collective-permute-done.28.near = bf16[32,32,128]{2,1,0:T(8,128)(2,1)S(1)} collective-permute-done((bf16[32,32,128]{2,1,0:T(8,128)(2,1)S(1)}, bf16[32,32,128]{2,1,0:T(8,128)(2,1)S(1)}, u32[]{:S(2)}, u32[]{:S(2)}) %collective-permute-start.28) | collective-permute-done | bytes 262176 | tf_op jit(solution)/shard_map/ppermute | solution.py:266
  229.0 11.1 %collective-permute-done.29.far = bf16[32,32,128]{2,1,0:T(8,128)(2,1)S(1)} collective-permute-done((bf16[32,32,128]{2,1,0:T(8,128)(2,1)S(1)}, bf16[32,32,128]{2,1,0:T(8,128)(2,1)S(1)}, u32[]{:S(2)}, u32[]{:S(2)}) %collective-permute-start.29) | collective-permute-done | bytes 262176 | tf_op jit(solution)/shard_map/ppermute | solution.py:266
  240.1 1.5 extract_pieces.1
  241.6 17.5 %all_to_all.10 = bf16[8,32,1536]{2,1,0:T(8,128)(2,1)S(1)} all-to-all(bf16[8,32,1536]{2,1,0:T(8,128)(2,1)S(1)} %extract_pieces.1), channel_id=1, replica_groups=mesh['leaf'=32,'sub'=8] {'sub'}, dimensions={0} | all-to-all | bytes 1572864 | tf_op jit(solution)/shard_map/all_to_all | solution.py:329
  259.1 3.2 %leaf_backward.1 = (bf16[4,512,256]{2,1,0:T(8,128)(2,1)}, bf16[512,256]{1,0:T(8,128)(2,1)}) custom-call(bf16[4,256,512]{2,1,0:T(8,128)(2,1)S(1)} %copy-done.4, bf16[256,1536]{1,0:T(8,128)(2,1)S(1)} %bitcast.5, bf16[4,512,512]{2,1,0:T(8,128)(2,1)S(1)} %copy-done, bf16[4,256,512]{2,1,0:T(8,128)(2,1)S(1)} %copy-done.1, bf16[256,1536]{1,0:T(8,128)(2,1)S(1)} %bitcast.6), custom_call_target="tpu_custom_call" | custom-call | tf_op jit(solution)/shard_map/leaf_backward/pallas_call | solution.py:240
  (80 shorter events, 14.3 us)
Async XLA Ops:
  0.6 15.8 %copy-start = (bf16[4,512,512]{2,1,0:T(8,128)(2,1)S(1)}, bf16[4,512,512]{2,1,0:T(8,128)(2,1)}, u32[]{:S(2)}) copy-start(bf16[4,512,512]{2,1,0:T(8,128)(2,1)} %inverse.3) | copy-start | bytes 6291460
  0.6 15.8 %copy-start.1 = (bf16[4,256,512]{2,1,0:T(8,128)(2,1)S(1)}, bf16[4,256,512]{2,1,0:T(8,128)(2,1)}, u32[]{:S(2)}) copy-start(bf16[4,256,512]{2,1,0:T(8,128)(2,1)} %panel.3) | copy-start | bytes 3145732
  0.7 15.8 %copy-start.16 = (bf16[512,256]{1,0:T(8,128)(2,1)S(1)}, bf16[512,256]{1,0:T(8,128)(2,1)}, u32[]{:S(2)}) copy-start(bf16[512,256]{1,0:T(8,128)(2,1)} %sep_right.1) | copy-start | bytes 786436
  4.0 114.1 %collective-permute-start.8 = (bf16[512,2048]{1,0:T(8,128)(2,1)}, bf16[512,2048]{1,0:T(8,128)(2,1)}, u32[]{:S(2)}, u32[]{:S(2)}) collective-permute-start(bf16[512,2048]{1,0:T(8,128)(2,1)} %slice.10), channel_id=1, source_target_pairs={{4,6},{5,7},{12,14},{13,15},{20,22},{21,23},{28,30},{29,31},{36,38... | collective-permute-start | bytes 6291464 | tf_op jit(solution)/shard_map/ppermute | solution.py:270
  6.0 20.6 %collective-permute-start.11 = (bf16[512,512]{1,0:T(8,128)(2,1)}, bf16[512,512]{1,0:T(8,128)(2,1)}, u32[]{:S(2)}, u32[]{:S(2)}) collective-permute-start(bf16[512,512]{1,0:T(8,128)(2,1)} %refs_16_.1), channel_id=1, source_target_pairs={{0,6},{1,7},{2,0},{3,1},{8,14},{9,15},{10,8},{11,9},{16,22},{17,23... | collective-permute-start | bytes 1572872 | tf_op jit(solution)/shard_map/ppermute | solution.py:270
  10.2 23.9 %collective-permute-start.15 = (bf16[512,512]{1,0:T(8,128)(2,1)}, bf16[512,512]{1,0:T(8,128)(2,1)}, u32[]{:S(2)}, u32[]{:S(2)}) collective-permute-start(bf16[512,512]{1,0:T(8,128)(2,1)} %refs_16_.1), channel_id=1, source_target_pairs={{4,6},{5,7},{12,14},{13,15},{20,22},{21,23},{28,30},{29,31},{36,38... | collective-permute-start | bytes 1572872 | tf_op jit(solution)/shard_map/ppermute | solution.py:270
  11.7 23.9 %collective-permute-start.17 = (bf16[512,512]{1,0:T(8,128)(2,1)}, bf16[512,512]{1,0:T(8,128)(2,1)}, u32[]{:S(2)}, u32[]{:S(2)}) collective-permute-start(bf16[512,512]{1,0:T(8,128)(2,1)} %refs_16_.1), channel_id=1, source_target_pairs={{6,7},{7,6},{14,15},{15,14},{22,23},{23,22},{30,31},{31,30},{38,39... | collective-permute-start | bytes 1572872 | tf_op jit(solution)/shard_map/ppermute | solution.py:274
  15.0 21.9 %collective-permute-start.18 = (bf16[512,512]{1,0:T(8,128)(2,1)}, bf16[512,512]{1,0:T(8,128)(2,1)}, u32[]{:S(2)}, u32[]{:S(2)}) collective-permute-start(bf16[512,512]{1,0:T(8,128)(2,1)} %constant_dynamic-slice_fusion.refs_24_), channel_id=1, source_target_pairs={{1,7},{3,1},{9,15},{11,9},{17,23},{19,17},{25,31},{27,25},{33,39},... | collective-permute-start | bytes 1572872 | tf_op jit(solution)/shard_map/ppermute | solution.py:270
  16.4 1.2 copy-start.2
  19.8 1.0 copy-start.3
  20.8 0.9 copy-start.5
  21.7 63.8 %all-to-all-start = ((bf16[8,32,1536]{2,1,0:T(8,128)(2,1)}), bf16[8,32,1536]{2,1,0:T(8,128)(2,1)}, u32[]{:S(2)}, u32[]{:S(2)}) async-start(bf16[8,32,1536]{2,1,0:T(8,128)(2,1)} %bitcast.7), calls=%async_computation | async-start | bytes 1572864 | tf_op jit(solution)/shard_map/all_to_all | solution.py:317
  26.6 61.4 %collective-permute-start.22 = (bf16[512,512]{1,0:T(8,128)(2,1)}, bf16[512,512]{1,0:T(8,128)(2,1)}, u32[]{:S(2)}, u32[]{:S(2)}) collective-permute-start(bf16[512,512]{1,0:T(8,128)(2,1)} %constant_dynamic-slice_fusion.refs_24_), channel_id=1, source_target_pairs={{5,7},{13,15},{21,23},{29,31},{37,39},{45,47},{53,55},{61,63},{69,... | collective-permute-start | bytes 1572872 | tf_op jit(solution)/shard_map/ppermute | solution.py:270
  30.3 8.9 %copy-start.21 = (s32[4]{0:T(128)S(1)}, s32[4]{0:T(128)}, u32[]{:S(2)}) copy-start(s32[4]{0:T(128)} %param.11) | copy-start | bytes 52
  30.3 8.9 %copy-start.20 = (s32[4,4]{1,0:T(4,128)S(1)}, s32[4,4]{1,0:T(4,128)}, u32[]{:S(2)}) copy-start(s32[4,4]{1,0:T(4,128)} %param.12) | copy-start | bytes 196
  30.3 9.1 %copy-start.22 = (u32[256]{0:T(256)S(1)}, u32[256]{0:T(256)}, u32[]{:S(2)}) copy-start(u32[256]{0:T(256)} %constant.50) | copy-start | bytes 3076
  34.1 62.4 %collective-permute-start.24 = (bf16[512,512]{1,0:T(8,128)(2,1)}, bf16[512,512]{1,0:T(8,128)(2,1)}, u32[]{:S(2)}, u32[]{:S(2)}) collective-permute-start(bf16[512,512]{1,0:T(8,128)(2,1)} %constant_dynamic-slice_fusion.refs_24_), channel_id=1, source_target_pairs={{7,6},{15,14},{23,22},{31,30},{39,38},{47,46},{55,54},{63,62},{71,... | collective-permute-start | bytes 1572872 | tf_op jit(solution)/shard_map/ppermute | solution.py:274
  35.6 78.8 %collective-permute-start.5 = (bf16[512,1024]{1,0:T(8,128)(2,1)}, bf16[512,1024]{1,0:T(8,128)(2,1)}, u32[]{:S(2)}, u32[]{:S(2)}) collective-permute-start(bf16[512,1024]{1,0:T(8,128)(2,1)} %slice.9), channel_id=1, source_target_pairs={{2,0},{3,1},{10,8},{11,9},{18,16},{19,17},{26,24},{27,25},{34,32},... | collective-permute-start | bytes 3145736 | tf_op jit(solution)/shard_map/ppermute | solution.py:270
  36.9 123.2 %collective-permute-start.10 = (bf16[512,3072]{1,0:T(8,128)(2,1)}, bf16[512,3072]{1,0:T(8,128)(2,1)}, u32[]{:S(2)}, u32[]{:S(2)}) collective-permute-start(bf16[512,3072]{1,0:T(8,128)(2,1)} %slice.11.refs_8_), channel_id=1, source_target_pairs={{6,7},{7,6},{14,15},{15,14},{22,23},{23,22},{30,31},{31,30},{38,39... | collective-permute-start | bytes 9437192 | tf_op jit(solution)/shard_map/ppermute | solution.py:274
  88.1 19.8 %collective-permute-start.1 = (bf16[32,32,128]{2,1,0:T(8,128)(2,1)S(1)}, bf16[32,32,128]{2,1,0:T(8,128)(2,1)S(1)}, u32[]{:S(2)}, u32[]{:S(2)}) collective-permute-start(bf16[32,32,128]{2,1,0:T(8,128)(2,1)S(1)} %get-tuple-element.15), channel_id=1, source_target_pairs={{16,0},{24,8},{32,16},{40,24},{48,32},{56,40},{64,48},{72,56},{80,... | collective-permute-start | bytes 786440 | tf_op jit(solution)/shard_map/ppermute | solution.py:266
  96.6 15.7 %collective-permute-start = (bf16[32,32,128]{2,1,0:T(8,128)(2,1)S(1)}, bf16[32,32,128]{2,1,0:T(8,128)(2,1)S(1)}, u32[]{:S(2)}, u32[]{:S(2)}) collective-permute-start(bf16[32,32,128]{2,1,0:T(8,128)(2,1)S(1)} %get-tuple-element.14), channel_id=1, source_target_pairs={{8,0},{16,8},{24,16},{32,24},{40,32},{48,40},{56,48},{64,56},{72,6... | collective-permute-start | bytes 786440 | tf_op jit(solution)/shard_map/ppermute | solution.py:266
  107.9 7.2 %collective-permute-start.12 = (bf16[512,512]{1,0:T(8,128)(2,1)}, bf16[512,512]{1,0:T(8,128)(2,1)S(1)}, u32[]{:S(2)}, u32[]{:S(2)}) collective-permute-start(bf16[512,512]{1,0:T(8,128)(2,1)} %collective-permute-done.11.refs_10_), channel_id=1, source_target_pairs={{6,7},{7,6},{14,15},{15,14},{22,23},{23,22},{30,31},{31,30},{38,39... | collective-permute-start | bytes 1572872 | tf_op jit(solution)/shard_map/ppermute | solution.py:274
  112.3 14.0 %collective-permute-start.13 = (bf16[512,512]{1,0:T(8,128)(2,1)}, bf16[512,512]{1,0:T(8,128)(2,1)}, u32[]{:S(2)}, u32[]{:S(2)}) collective-permute-start(bf16[512,512]{1,0:T(8,128)(2,1)} %collective-permute-done.11.refs_10_), channel_id=1, source_target_pairs={{0,6},{1,7},{8,14},{9,15},{16,22},{17,23},{24,30},{25,31},{32,38},... | collective-permute-start | bytes 1572872 | tf_op jit(solution)/shard_map/ppermute | solution.py:270
  114.4 12.6 %collective-permute-start.16 = (bf16[512,512]{1,0:T(8,128)(2,1)}, bf16[512,512]{1,0:T(8,128)(2,1)S(1)}, u32[]{:S(2)}, u32[]{:S(2)}) collective-permute-start(bf16[512,512]{1,0:T(8,128)(2,1)} %collective-permute-done.15.refs_14_), channel_id=1, source_target_pairs={{6,7},{7,6},{14,15},{15,14},{22,23},{23,22},{30,31},{31,30},{38,39... | collective-permute-start | bytes 1572872 | tf_op jit(solution)/shard_map/ppermute | solution.py:274
  115.8 32.9 %collective-permute-start.6 = (bf16[512,1024]{1,0:T(8,128)(2,1)}, bf16[512,1024]{1,0:T(8,128)(2,1)}, u32[]{:S(2)}, u32[]{:S(2)}) collective-permute-start(bf16[512,1024]{1,0:T(8,128)(2,1)} %collective-permute-done.5), channel_id=1, source_target_pairs={{0,6},{1,7},{8,14},{9,15},{16,22},{17,23},{24,30},{25,31},{32,38},... | collective-permute-start | bytes 3145736 | tf_op jit(solution)/shard_map/ppermute | solution.py:270
  118.1 42.0 %collective-permute-start.9 = (bf16[512,2048]{1,0:T(8,128)(2,1)}, bf16[512,2048]{1,0:T(8,128)(2,1)}, u32[]{:S(2)}, u32[]{:S(2)}) collective-permute-start(bf16[512,2048]{1,0:T(8,128)(2,1)} %collective-permute-done.8.refs_6_), channel_id=1, source_target_pairs={{6,7},{7,6},{14,15},{15,14},{22,23},{23,22},{30,31},{31,30},{38,39... | collective-permute-start | bytes 6291464 | tf_op jit(solution)/shard_map/ppermute | solution.py:274
  126.2 3.0 %collective-permute-start.19 = (bf16[512,512]{1,0:T(8,128)(2,1)}, bf16[512,512]{1,0:T(8,128)(2,1)S(1)}, u32[]{:S(2)}, u32[]{:S(2)}) collective-permute-start(bf16[512,512]{1,0:T(8,128)(2,1)} %collective-permute-done.18.refs_18_), channel_id=1, source_target_pairs={{7,6},{15,14},{23,22},{31,30},{39,38},{47,46},{55,54},{63,62},{71,... | collective-permute-start | bytes 1572872 | tf_op jit(solution)/shard_map/ppermute | solution.py:274
  127.7 2.4 collective-permute-start.20
  129.2 0.8 copy-start.18
  129.2 21.2 %collective-permute-start.23 = (bf16[512,512]{1,0:T(8,128)(2,1)}, bf16[512,512]{1,0:T(8,128)(2,1)S(1)}, u32[]{:S(2)}, u32[]{:S(2)}) collective-permute-start(bf16[512,512]{1,0:T(8,128)(2,1)} %collective-permute-done.22.refs_22_), channel_id=1, source_target_pairs={{7,6},{15,14},{23,22},{31,30},{39,38},{47,46},{55,54},{63,62},{71,... | collective-permute-start | bytes 1572872 | tf_op jit(solution)/shard_map/ppermute | solution.py:274
  130.2 24.1 %collective-permute-start.2 = (bf16[32,32,128]{2,1,0:T(8,128)(2,1)S(1)}, bf16[32,32,128]{2,1,0:T(8,128)(2,1)S(1)}, u32[]{:S(2)}, u32[]{:S(2)}) collective-permute-start(bf16[32,32,128]{2,1,0:T(8,128)(2,1)S(1)} %subtract_convert_fusion.refs_3_), channel_id=1, source_target_pairs={{0,6},{1,7},{8,14},{9,15},{16,22},{17,23},{24,30},{25,31},{32,38},... | collective-permute-start | bytes 786440 | tf_op jit(solution)/shard_map/ppermute | solution.py:270
  148.7 11.3 %collective-permute-start.7 = (bf16[512,1024]{1,0:T(8,128)(2,1)}, bf16[512,1024]{1,0:T(8,128)(2,1)}, u32[]{:S(2)}, u32[]{:S(2)}) collective-permute-start(bf16[512,1024]{1,0:T(8,128)(2,1)} %collective-permute-done.6.refs_4_), channel_id=1, source_target_pairs={{6,7},{7,6},{14,15},{15,14},{22,23},{23,22},{30,31},{31,30},{38,39... | collective-permute-start | bytes 3145736 | tf_op jit(solution)/shard_map/ppermute | solution.py:274
  150.4 7.4 %copy-start.19 = (bf16[512,512]{1,0:T(8,128)(2,1)}, bf16[512,512]{1,0:T(8,128)(2,1)S(1)}, u32[]{:S(2)}) copy-start(bf16[512,512]{1,0:T(8,128)(2,1)S(1)} %collective-permute-done.23.refs_23_) | copy-start | bytes 1572868
  150.4 5.2 %collective-permute-start.3 = (bf16[32,32,128]{2,1,0:T(8,128)(2,1)S(1)}, bf16[32,32,128]{2,1,0:T(8,128)(2,1)S(1)}, u32[]{:S(2)}, u32[]{:S(2)}) collective-permute-start(bf16[32,32,128]{2,1,0:T(8,128)(2,1)S(1)} %subtract_convert_fusion.refs_3_), channel_id=1, source_target_pairs={{2,6},{3,7},{10,14},{11,15},{18,22},{19,23},{26,30},{27,31},{34,38... | collective-permute-start | bytes 786440 | tf_op jit(solution)/shard_map/ppermute | solution.py:270
  154.9 2.8 %collective-permute-start.4 = (bf16[32,32,128]{2,1,0:T(8,128)(2,1)S(1)}, bf16[32,32,128]{2,1,0:T(8,128)(2,1)S(1)}, u32[]{:S(2)}, u32[]{:S(2)}) collective-permute-start(bf16[32,32,128]{2,1,0:T(8,128)(2,1)S(1)} %subtract_convert_fusion.refs_3_), channel_id=1, source_target_pairs={{4,6},{5,7},{12,14},{13,15},{20,22},{21,23},{28,30},{29,31},{36,38... | collective-permute-start | bytes 786440 | tf_op jit(solution)/shard_map/ppermute | solution.py:270
  156.3 3.7 %collective-permute-start.14 = (bf16[512,512]{1,0:T(8,128)(2,1)}, bf16[512,512]{1,0:T(8,128)(2,1)}, u32[]{:S(2)}, u32[]{:S(2)}) collective-permute-start(bf16[512,512]{1,0:T(8,128)(2,1)} %collective-permute-done.13.refs_12_), channel_id=1, source_target_pairs={{6,7},{7,6},{14,15},{15,14},{22,23},{23,22},{30,31},{31,30},{38,39... | collective-permute-start | bytes 1572872 | tf_op jit(solution)/shard_map/ppermute | solution.py:274
  158.5 1.5 collective-permute-start.21
  160.1 1.0 copy-start.7
  161.1 1.0 copy-start.9
  162.1 0.9 copy-start.11
  163.1 0.9 copy-start.13
  164.0 0.9 copy-start.15
  167.4 3.4 %collective-permute-start.25 = (bf16[32,32,128]{2,1,0:T(8,128)(2,1)}, bf16[32,32,128]{2,1,0:T(8,128)(2,1)S(1)}, u32[]{:S(2)}, u32[]{:S(2)}) collective-permute-start(bf16[32,32,128]{2,1,0:T(8,128)(2,1)} %get-tuple-element.17), channel_id=1, source_target_pairs={{6,4},{7,5},{14,12},{15,13},{22,20},{23,21},{30,28},{31,29},{38,36... | collective-permute-start | bytes 786440 | tf_op jit(solution)/shard_map/ppermute | solution.py:270
  168.1 2.7 %collective-permute-start.26 = (bf16[32,32,128]{2,1,0:T(8,128)(2,1)}, bf16[32,32,128]{2,1,0:T(8,128)(2,1)}, u32[]{:S(2)}, u32[]{:S(2)}) collective-permute-start(bf16[32,32,128]{2,1,0:T(8,128)(2,1)} %get-tuple-element.18), channel_id=1, source_target_pairs={{6,2},{7,3},{14,10},{15,11},{22,18},{23,19},{30,26},{31,27},{38,34... | collective-permute-start | bytes 786440 | tf_op jit(solution)/shard_map/ppermute | solution.py:270
  169.4 44.6 %collective-permute-start.27 = (bf16[32,32,128]{2,1,0:T(8,128)(2,1)}, bf16[32,32,128]{2,1,0:T(8,128)(2,1)}, u32[]{:S(2)}, u32[]{:S(2)}) collective-permute-start(bf16[32,32,128]{2,1,0:T(8,128)(2,1)} %get-tuple-element.19), channel_id=1, source_target_pairs={{6,0},{7,1},{14,8},{15,9},{22,16},{23,17},{30,24},{31,25},{38,32},... | collective-permute-start | bytes 786440 | tf_op jit(solution)/shard_map/ppermute | solution.py:270
  170.7 88.4 %copy-start.4 = (bf16[4,256,512]{2,1,0:T(8,128)(2,1)S(1)}, bf16[4,256,512]{2,1,0:T(8,128)(2,1)}, u32[]{:S(2)}) copy-start(bf16[4,256,512]{2,1,0:T(8,128)(2,1)} %copy-done.3) | copy-start | bytes 3145732
  215.1 13.9 %collective-permute-start.28 = (bf16[32,32,128]{2,1,0:T(8,128)(2,1)S(1)}, bf16[32,32,128]{2,1,0:T(8,128)(2,1)S(1)}, u32[]{:S(2)}, u32[]{:S(2)}) collective-permute-start(bf16[32,32,128]{2,1,0:T(8,128)(2,1)S(1)} %select_select_fusion.own), channel_id=1, source_target_pairs={{0,8},{8,16},{16,24},{24,32},{32,40},{40,48},{48,56},{56,64},{64,7... | collective-permute-start | bytes 786440 | tf_op jit(solution)/shard_map/ppermute | solution.py:266
  217.0 23.0 %collective-permute-start.29 = (bf16[32,32,128]{2,1,0:T(8,128)(2,1)S(1)}, bf16[32,32,128]{2,1,0:T(8,128)(2,1)S(1)}, u32[]{:S(2)}, u32[]{:S(2)}) collective-permute-start(bf16[32,32,128]{2,1,0:T(8,128)(2,1)S(1)} %select_select_fusion.own), channel_id=1, source_target_pairs={{0,16},{8,24},{16,32},{24,40},{32,48},{40,56},{48,64},{56,72},{64,... | collective-permute-start | bytes 786440 | tf_op jit(solution)/shard_map/ppermute | solution.py:266
  (6 other events, 4.4 us)

commit v2 on v1

v2 whole, which is shorter than its diff:
```python
import jax
import jax.numpy as jnp
from jax import lax
from jax.experimental import pallas as pl
from jax.experimental.pallas import tpu as pltpu
from jax.sharding import PartitionSpec as P

W = 512
WSN = 512
SA = 4096
R = 256
BLK = 64
KB = 4
SPAN = 3
SN_DEV = 4
GROUP = 8
COLS = R // GROUP
CHUNKS = SA // 128
UPD = SN_DEV * KB * BLK
SLOT = UPD + WSN
SEND = SLOT + 128
HUB = 3
bf16 = jnp.bfloat16
f32 = jnp.float32
NT = (((1,), (1,)), ((), ()))
NN = (((1,), (0,)), ((), ()))
MIB = 1 << 20
WHOLE = 60 * MIB


def dot(a, b, dims):
    return lax.dot_general(a, b, dims, preferred_element_type=f32)


def for_each_source(where, visit):
    for chip, wide in ((2, 4 * WSN), (1, 2 * WSN), (0, WSN)):

        @pl.when(where[0] == chip)
        def _():
            visit(chip, wide)


def leaf_forward_kernel(
    where, slots, right, inverse, panel, sep_right, half, factor, sep_inverse, y_out, send, pack2, pack1, pack0, sems
):
    j = pl.program_id(0)
    packs = (pack0, pack1, pack2)

    def begin(chip, wide):
        rows = sep_inverse if chip == 0 else factor.at[:, 0:wide]
        pltpu.make_async_copy(rows, packs[chip].at[:, 0:wide], sems.at[0]).start()
        rest = packs[chip].at[:, wide : wide + WSN // 2]

        @pl.when(where[1] == 1)
        def _():
            beside = factor.at[:, 2 * WSN * chip : 2 * WSN * chip + WSN // 2]
            pltpu.make_async_copy(beside, rest, sems.at[1]).start()

        @pl.when(where[1] == 0)
        def _():
            pltpu.make_async_copy(half, rest, sems.at[1]).start()

    def end(chip, wide):
        whole, rest = packs[chip].at[:, 0:wide], packs[chip].at[:, wide : wide + WSN // 2]
        pltpu.make_async_copy(whole, whole, sems.at[0]).wait()
        pltpu.make_async_copy(rest, rest, sems.at[1]).wait()

    @pl.when(j == 0)
    def _():
        for_each_source(where, begin)
        send[:, UPD:SLOT] = sep_right[...].T
        send[:, SLOT:] = jnp.broadcast_to(slots[...], (R, 128)).astype(bf16)

    y = dot(right[0].T, inverse[0], NT).astype(bf16)
    y_out[0] = y
    send[:, pl.ds(pl.multiple_of(j * KB * BLK, 128), KB * BLK)] = dot(y, panel[0], NT).astype(bf16)

    @pl.when(j == SN_DEV - 1)
    def _():
        for_each_source(where, end)


def leaf_forward(where, slots, right, inverse, panels, sep_right, half, factor, sep_inverse):
    hbm = pl.BlockSpec(memory_space=pltpu.HBM)
    sizes = [(WSN, n * WSN + WSN // 2) for n in (4, 2, 1)]
    return pl.pallas_call(
        leaf_forward_kernel,
        grid=(SN_DEV,),
        in_specs=[
            pl.BlockSpec(memory_space=pltpu.SMEM),
            pl.BlockSpec((1, 128), lambda j: (0, 0)),
            pl.BlockSpec((1, W, R), lambda j: (j, 0, 0)),
            pl.BlockSpec((1, W, W), lambda j: (j, 0, 0)),
            pl.BlockSpec((1, KB * BLK, W), lambda j: (j, 0, 0)),
            pl.BlockSpec((WSN, R), lambda j: (0, 0)),
            hbm,
            hbm,
            hbm,
        ],
        out_specs=[
            pl.BlockSpec((1, R, W), lambda j: (j, 0, 0)),
            pl.BlockSpec((R, SEND), lambda j: (0, 0)),
        ]
        + [pl.BlockSpec(size, lambda j: (0, 0)) for size in sizes],
        out_shape=[
            jax.ShapeDtypeStruct((SN_DEV, R, W), bf16),
            jax.ShapeDtypeStruct((R, SEND), bf16),
        ]
        + [jax.ShapeDtypeStruct(size, bf16) for size in sizes],
        scratch_shapes=[pltpu.SemaphoreType.DMA((2,))],
        compiler_params=pltpu.CompilerParams(dimension_semantics=("arbitrary",), vmem_limit_bytes=WHOLE),
        name="leaf_forward",
    )(where, slots, right, inverse, panels, sep_right, half, factor, sep_inverse)


def scatter_kernel(received, base, near, far, slots_out, table, slots, sem):
    slots_out[...] = received[:, 0, SLOT:].astype(f32).astype(jnp.int32)
    to_scalars = pltpu.make_async_copy(slots_out, slots, sem)
    to_scalars.start()
    table[...] = jnp.zeros_like(table)
    high = lax.broadcasted_iota(jnp.int32, (COLS, 128), 1) >= BLK
    to_scalars.wait()

    def from_member(s, carry):
        for i in range(UPD // 128):
            pair = received[s, :, 128 * i : 128 * i + 128].astype(f32)
            turned = pltpu.roll(pair, BLK, 1)
            for h in range(2):
                slot = slots[s, 2 * i + h]
                want_high = (slot & 1) == 1
                moved = jnp.where(want_high, turned if h == 0 else pair, pair if h == 0 else turned)
                row = slot >> 1
                table[row] = table[row] + jnp.where(high == want_high, moved, 0.0)
        return carry

    lax.fori_loop(0, GROUP, from_member, 0)
    for c in range(CHUNKS):
        first = UPD + 128 * (c % 4)
        base[c] = received[c // 4, :, first : first + 128].astype(f32) - table[c]
        near[c] = table[CHUNKS + c].astype(bf16)
        far[c] = table[2 * CHUNKS + c].astype(bf16)


def scatter(received):
    share = (CHUNKS, COLS, 128)
    return pl.pallas_call(
        scatter_kernel,
        in_specs=[pl.BlockSpec(memory_space=pltpu.VMEM)],
        out_specs=[pl.BlockSpec(memory_space=pltpu.VMEM)] * 4,
        out_shape=[
            jax.ShapeDtypeStruct(share, f32),
            jax.ShapeDtypeStruct(share, bf16),
            jax.ShapeDtypeStruct(share, bf16),
            jax.ShapeDtypeStruct((GROUP, 128), jnp.int32),
        ],
        scratch_shapes=[
            pltpu.VMEM((SPAN * CHUNKS, COLS, 128), f32),
            pltpu.SMEM((GROUP, 128), jnp.int32),
            pltpu.SemaphoreType.DMA(()),
        ],
        compiler_params=pltpu.CompilerParams(vmem_limit_bytes=16 * MIB),
        name="scatter_updates",
    )(received)


def load_rows(core, k, blocks, lower, diagonal, sems):
    odd = slice((2 * k + 1) * WSN, (2 * k + 2) * WSN)
    width = 2 * k * WSN
    for other in (0, 1):
        q = 2 * k + (1 - core if other else core)
        rows = pl.ds(pl.multiple_of(q * WSN, WSN), WSN)
        wide, inverse = blocks[k][other]
        block = wide.at[:, 0:WSN] if k == 0 else inverse
        pltpu.make_async_copy(block, diagonal.at[rows], sems.at[0, k]).start()
        if k > 0:
            pltpu.make_async_copy(wide.at[:, 0:width], lower.at[rows, 0:width], sems.at[1, k]).start()
        for c in (0, 1):
            sender = 1 - c if other else c

            @pl.when(core == c)
            def _():
                if k == HUB:
                    if sender == 1:
                        block = wide.at[:, width : width + WSN]
                        dst = lower.at[odd, width : width + WSN]
                        pltpu.make_async_copy(block, dst, sems.at[2, k]).start()
                else:
                    first = WSN if k == 0 else width
                    block = wide.at[:, first : first + WSN // 2]
                    at = width + (1 - sender) * (WSN // 2)
                    dst = lower.at[odd, at : at + WSN // 2]
                    pltpu.make_async_copy(block, dst, sems.at[2, k]).start()


def await_rows(k, lower, diagonal, sems):
    pair = slice(2 * k * WSN, (2 * k + 2) * WSN)
    both = diagonal.at[pair]
    pltpu.make_async_copy(both, both, sems.at[0, k]).wait()
    if k > 0:
        slab = lower.at[pair, 0 : 2 * k * WSN]
        pltpu.make_async_copy(slab, slab, sems.at[1, k]).wait()
    single = lower.at[(2 * k + 1) * WSN : (2 * k + 2) * WSN, 2 * k * WSN : (2 * k + 1) * WSN]
    pltpu.make_async_copy(single, single, sems.at[2, k]).wait()


def forward_row(q, state, lower, diagonal):
    here = slice(q * WSN, (q + 1) * WSN)
    bracket = state[:, here].astype(f32)
    if q > 0:
        bracket = bracket - dot(state[:, : q * WSN], lower[here, : q * WSN], NT)
    state[:, here] = by_inverse(bracket, diagonal[here], NT)


def head_kernel(where, *refs):
    rhs = refs[0:4]
    blocks = {0: ((refs[4], None), (refs[5], None)), 1: ((refs[6], refs[8]), (refs[7], refs[9]))}
    state, lower, diagonal, shares, rhs_sem, sems = refs[10:]

    @pl.when(where[0] == HUB)
    def _():
        for k in range(4):
            pltpu.make_async_copy(rhs[k], shares.at[k], rhs_sem.at[k]).start()
        for k in (0, 1):
            load_rows(where[1], k, blocks, lower, diagonal, sems)
        for k in range(4):
            pltpu.make_async_copy(rhs[k], shares.at[k], rhs_sem.at[k]).wait()
            for c in range(CHUNKS):
                state[COLS * k : COLS * k + COLS, 128 * c : 128 * c + 128] = shares[k, c]
        for k in (0, 1):
            await_rows(k, lower, diagonal, sems)
            for q in (2 * k, 2 * k + 1):
                forward_row(q, state, lower, diagonal)


def rest_kernel(where, *refs):
    begun = refs[0]
    blocks = {
        0: ((refs[1], None), (refs[2], None)),
        1: ((refs[3], refs[5]), (refs[4], refs[6])),
        2: ((refs[7], refs[9]), (refs[8], refs[10])),
        3: ((refs[11], refs[13]), (refs[12], refs[14])),
    }
    outs = refs[15:19]
    lower, diagonal, state, state_sem, sems = refs[19:]

    @pl.when(where[0] == HUB)
    def _():
        pltpu.make_async_copy(begun, state, state_sem).start()
        for k in (2, 3, 1, 0):
            load_rows(where[1], k, blocks, lower, diagonal, sems)
        pltpu.make_async_copy(begun, state, state_sem).wait()
        for k in (2, 3):
            await_rows(k, lower, diagonal, sems)
            for q in (2 * k, 2 * k + 1):
                forward_row(q, state, lower, diagonal)
        for q in reversed(range(8)):
            if q in (1, 3):
                await_rows(q // 2, lower, diagonal, sems)
            here = slice(q * WSN, (q + 1) * WSN)
            bracket = state[:, here].astype(f32)
            if q < 7:
                bracket = bracket - dot(state[:, (q + 1) * WSN :], lower[(q + 1) * WSN :, here], NN)
            solved = by_inverse(bracket, diagonal[here], NN)
            state[:, here] = solved
            for k in range(4):
                for t in range(4):
                    outs[k][4 * q + t] = solved[COLS * k : COLS * k + COLS, 128 * t : 128 * t + 128]


def by_inverse(bracket, block, dims):
    head = bracket.astype(bf16)
    tail = (bracket - head.astype(f32)).astype(bf16)
    return (dot(head, block, dims) + dot(tail, block, dims)).astype(bf16)


def sweep_head(where, *blocks):
    share = (CHUNKS, COLS, 128)
    hbm = pl.BlockSpec(memory_space=pltpu.HBM)
    return pl.pallas_call(
        head_kernel,
        in_specs=[pl.BlockSpec(memory_space=pltpu.SMEM)] + [hbm] * len(blocks),
        out_specs=pl.BlockSpec(memory_space=pltpu.VMEM),
        out_shape=jax.ShapeDtypeStruct((4 * COLS, SA), bf16),
        scratch_shapes=[
            pltpu.VMEM((4 * WSN, 3 * WSN), bf16),
            pltpu.VMEM((4 * WSN, WSN), bf16),
            pltpu.VMEM((4, *share), bf16),
            pltpu.SemaphoreType.DMA((4,)),
            pltpu.SemaphoreType.DMA((3, 2)),
        ],
        compiler_params=pltpu.CompilerParams(vmem_limit_bytes=20 * MIB),
        name="sweep_head",
    )(where, *blocks)


def sweep_rest(where, *blocks):
    share = (CHUNKS, COLS, 128)
    hbm = pl.BlockSpec(memory_space=pltpu.HBM)
    return pl.pallas_call(
        rest_kernel,
        in_specs=[pl.BlockSpec(memory_space=pltpu.SMEM)] + [hbm] * len(blocks),
        out_specs=[pl.BlockSpec(memory_space=pltpu.VMEM)] * 4,
        out_shape=[jax.ShapeDtypeStruct(share, bf16)] * 4,
        scratch_shapes=[
            pltpu.VMEM((SA, 7 * WSN), bf16),
            pltpu.VMEM((SA, WSN), bf16),
            pltpu.VMEM((4 * COLS, SA), bf16),
            pltpu.SemaphoreType.DMA(()),
            pltpu.SemaphoreType.DMA((3, 4)),
        ],
        compiler_params=pltpu.CompilerParams(vmem_limit_bytes=42 * MIB),
        name="sweep_rest",
    )(where, *blocks)


def extract_kernel(slots, own, near, far, send, table):
    for d, ref in enumerate((own, near, far)):
        for c in range(CHUNKS):
            table[d * CHUNKS + c] = ref[c].astype(f32)
    high = lax.broadcasted_iota(jnp.int32, (COLS, 128), 1) >= BLK

    def for_member(s, carry):
        for i in range(UPD // 128):
            halves = []
            for h in range(2):
                slot = slots[s, 2 * i + h]
                pair = table[slot >> 1]
                halves.append(jnp.where((slot & 1) == h, pair, pltpu.roll(pair, BLK, 1)))
            send[s, :, 128 * i : 128 * i + 128] = jnp.where(high, halves[1], halves[0]).astype(bf16)
        return carry

    lax.fori_loop(0, GROUP, for_member, 0)


def extract(slots, own, near, far):
    return pl.pallas_call(
        extract_kernel,
        in_specs=[pl.BlockSpec(memory_space=pltpu.SMEM)] + [pl.BlockSpec(memory_space=pltpu.VMEM)] * 3,
        out_specs=pl.BlockSpec(memory_space=pltpu.VMEM),
        out_shape=jax.ShapeDtypeStruct((GROUP, COLS, UPD), bf16),
        scratch_shapes=[pltpu.VMEM((SPAN * CHUNKS, COLS, 128), f32)],
        compiler_params=pltpu.CompilerParams(vmem_limit_bytes=16 * MIB),
        name="extract_pieces",
    )(slots, own, near, far)


def leaf_backward_kernel(y, pieces, inverse, panel, rows, leaf_x, sep_x):
    inner = (y[0].astype(f32) - dot(pieces[...], panel[0], NN)).astype(bf16)
    leaf_x[0] = dot(inner, inverse[0], NN).astype(bf16).T

    @pl.when(pl.program_id(0) == 0)
    def _():
        for m in range(GROUP):
            for t in range(WSN // 128):
                sep_x[128 * t : 128 * t + 128, COLS * m : COLS * m + COLS] = rows[m, t].T


def leaf_backward(y, pieces, inverse, panels, rows):
    return pl.pallas_call(
        leaf_backward_kernel,
        grid=(SN_DEV,),
        in_specs=[
            pl.BlockSpec((1, R, W), lambda j: (j, 0, 0)),
            pl.BlockSpec((R, KB * BLK), lambda j: (0, j)),
            pl.BlockSpec((1, W, W), lambda j: (j, 0, 0)),
            pl.BlockSpec((1, KB * BLK, W), lambda j: (j, 0, 0)),
            pl.BlockSpec((GROUP, WSN // 128, COLS, 128), lambda j: (0, 0, 0, 0)),
        ],
        out_specs=[
            pl.BlockSpec((1, W, R), lambda j: (j, 0, 0)),
            pl.BlockSpec((WSN, R), lambda j: (0, 0)),
        ],
        out_shape=[
            jax.ShapeDtypeStruct((SN_DEV, W, R), bf16),
            jax.ShapeDtypeStruct((WSN, R), bf16),
        ],
        compiler_params=pltpu.CompilerParams(dimension_semantics=("arbitrary",), vmem_limit_bytes=WHOLE),
        name="leaf_backward",
    )(y, pieces, inverse, panels, rows)


def along_leaf(block, distance):
    devices = range(lax.axis_size("leaf"))
    route = [(i - distance, i) for i in devices if i - distance in devices]
    return lax.ppermute(block, "leaf", route)


def hop(block, *chips, cores=(0, 1)):
    return lax.ppermute(block, "sub", [(2 * a + c, 2 * b + c) for a, b in chips for c in cores])


def swap(block, cores=(0, 1)):
    return lax.ppermute(block, "sub", [(2 * HUB + c, 2 * HUB + 1 - c) for c in cores])


def shards(
    leaf_right,
    leaf_inverse,
    panels,
    leaf_subtree,
    panel_block,
    separator_right,
    separator_inverse,
    separator_factor,
):
    section = lax.axis_index("leaf")
    member = lax.axis_index("sub")
    chip, core = member // 2, member % 2
    where = jnp.stack([chip, core]).astype(jnp.int32)
    row_blocks = SA // BLK
    own_slots = ((section - leaf_subtree)[:, None] * row_blocks + panel_block).reshape(1, -1)
    own_slots = jnp.pad(own_slots.astype(f32), ((0, 0), (0, 128 - SN_DEV * KB)))
    inverse2, inverse1 = hop(separator_inverse, (2, HUB)), hop(separator_inverse, (1, HUB))
    factors = (separator_factor, swap(separator_factor))
    inverses = (separator_inverse, swap(separator_inverse))
    half = lax.dynamic_slice(separator_factor, (0, 2 * WSN * chip + WSN // 2), (WSN, WSN // 2))
    half = lax.ppermute(half, "sub", [(2 * k + 1, 2 * k) for k in range(3)])
    y, send, *packs = leaf_forward(
        where, own_slots, leaf_right, leaf_inverse, panels, separator_right, half, separator_factor, separator_inverse
    )
    received = lax.all_to_all(send.reshape(GROUP, COLS, SEND), "sub", 0, 0, tiled=True)
    inverse1, inverse2 = (inverse1, swap(inverse1)), (inverse2, swap(inverse2))
    received, packs, factors, inverses, inverse1, inverse2 = lax.optimization_barrier(
        (received, packs, factors, inverses, inverse1, inverse2)
    )
    pack2, pack1, pack0 = (hop(block, (k, HUB)) for block, k in zip(packs, (2, 1, 0)))
    base, near, far, slots = scatter(received)
    near_sum = along_leaf(near, -1).astype(f32)
    far_sum = along_leaf(far, -2).astype(f32)
    rhs = (base - near_sum - far_sum).astype(bf16)
    to_hub = [None, hop(rhs, (1, HUB)), hop(rhs, (2, HUB)), rhs]
    rhs, pack0 = lax.optimization_barrier((rhs, pack0))
    to_hub[0] = hop(rhs, (0, HUB))
    pack0, pack1 = lax.optimization_barrier((pack0, pack1, to_hub[0]))[:2]
    pack0, pack1 = (pack0, swap(pack0)), (pack1, swap(pack1))
    pack2 = lax.optimization_barrier((pack2, *to_hub[:3], pack0, pack1))[0]
    pack2 = (pack2, swap(pack2))
    begun = sweep_head(where, *to_hub, *pack0, *pack1, *inverse1)
    shares = sweep_rest(where, begun, *pack0, *pack1, *inverse1, *pack2, *inverse2, *factors, *inverses)
    back = [hop(shares[k], (HUB, k)) for k in range(3)] + [shares[HUB]]
    own = jnp.where(chip == 3, back[3], jnp.where(chip == 2, back[2], jnp.where(chip == 1, back[1], back[0])))
    pieces = extract(slots, own, along_leaf(own, 1), along_leaf(own, 2))
    rows = lax.all_to_all(own.reshape(GROUP, WSN // 128, COLS, 128), "sub", 0, 0, tiled=True)
    pieces = lax.all_to_all(pieces, "sub", 0, 0, tiled=True).reshape(R, UPD)
    return tuple(leaf_backward(y, pieces, leaf_inverse, panels, rows))


def solution(mesh):
    placed = (
        P(("leaf", "sub"), None, None),
        P(("leaf", "sub"), None, None),
        P(("leaf", "sub"), None, None),
        P(("leaf", "sub")),
        P(("leaf", "sub"), None),
        P(("leaf", "sub"), None),
        P(("leaf", "sub"), None),
        P(("leaf", "sub"), None),
    )
    return jax.shard_map(
        shards,
        mesh=mesh,
        in_specs=placed,
        out_specs=(P(("leaf", "sub"), None, None), P(("leaf", "sub"), None)),
        check_vma=False,
    )
```

time: 264 us -> 201 us (0.76)
  the two profiles are of different devices: /device:TPU:6 before, /device:TPU:38 now
where the time goes in v2:
time: 201 us; the launch traced here: 200 us
  waiting for transfers between devices  98.7 us (49%)
  starting transfers between devices  59 us (29%)
  Pallas kernels  18.9 us (9%)
  blocking collectives  15.6 us (8%)
  local copies, waits for them, and re-layouts  3.79 us (2%)
  other arithmetic  2.88 us (1%)
    ppermute x11, waiting for transfers between devices, hop(): lax.ppermute(block, 'sub', [(2 * a + c, 2 * b + c) for a, b in chips for...  66.3 us
    ppermute x4, waiting for transfers between devices, along_leaf(): return lax.ppermute(block, 'leaf', route)  21.5 us
    ppermute x4, starting transfers between devices, along_leaf(): return lax.ppermute(block, 'leaf', route)  20.7 us
    ppermute x11, starting transfers between devices, hop(): lax.ppermute(block, 'sub', [(2 * a + c, 2 * b + c) for a, b in chips for...  16.1 us
    all_to_all x1, blocking collectives, shards(): pieces = lax.all_to_all(pieces, 'sub', 0, 0, tiled=True).reshape(R, UPD)  15.6 us
    all_to_all x1, waiting for transfers between devices, shards(): lax.all_to_all(send.reshape(GROUP, COLS, SEND), 'sub', 0, 0, tiled=True)  10.9 us
    ppermute x7, starting transfers between devices, swap(): lax.ppermute(block, 'sub', [(2 * HUB + c, 2 * HUB + 1 - c) for c in cores])  7.76 us
    all_to_all x1, starting transfers between devices, shards(): lax.all_to_all(send.reshape(GROUP, COLS, SEND), 'sub', 0, 0, tiled=True)  7.76 us
  transfers between devices with their start and end apart: 25, of which 7 were waited for; matrix products, arithmetic and copies ran while one was open for 2% of the time, Pallas kernels for 6%

profile of v2, /device:TPU:38, one launch (start us, length us, event | category | flops | bytes accessed | tf_op | source)
XLA Modules:
  0.0 199.9 jit_solution(11764589332294424882)
XLA Ops:
  0.6 2.6 %collective-permute-start.1 = (bf16[512,4096]{1,0:T(8,128)(2,1)}, bf16[512,4096]{1,0:T(8,128)(2,1)}, u32[]{:S(2)}, u32[]{:S(2)}) collective-permute-start(bf16[512,4096]{1,0:T(8,128)(2,1)} %refs_11_), channel_id=1, source_target_pairs={{6,7},{7,6},{14,15},{15,14},{22,23},{23,22},{30,31},{31,30},{38,39... | collective-permute-start | bytes 12582920 | tf_op jit(solution)/shard_map/ppermute | solution.py:393
  3.3 0.7 collective-permute-start.3
  3.9 0.7 collective-permute-start.5
  4.7 1.0 constant_dynamic-slice_fusion
  5.6 1.3 collective-permute-start
  7.0 0.7 subtract_multiply_fusion
  7.6 0.8 add_convert_fusion
  8.5 0.6 pad.4.slots
  9.1 0.6 pad_add_fusion.where
  9.6 0.7 copy-done.4
  10.3 7.1 %leaf_forward.1 = (bf16[4,256,512]{2,1,0:T(8,128)(2,1)}, bf16[256,1664]{1,0:T(8,128)(2,1)}, bf16[512,2304]{1,0:T(8,128)(2,1)}, bf16[512,1280]{1,0:T(8,128)(2,1)}, bf16[512,768]{1,0:T(8,128)(2,1)}) custom-call(s32[2]{0:T(128)} %pad_add_fusion.where, f32[1,128]{1,0:T(1,128)} %pad.4.slots, bf16[4,512,256]{2,1,0:T(8,128)(2,1)} %right.1, ...), custom_call_target="tpu_custom_call" | custom-call | tf_op jit(solution)/shard_map/leaf_forward/pallas_call | solution.py:86
  17.4 7.8 %all-to-all-start = ((bf16[8,32,1664]{2,1,0:T(8,128)(2,1)}), bf16[8,32,1664]{2,1,0:T(8,128)(2,1)S(1)}, u32[]{:S(2)}, u32[]{:S(2)}) async-start(bf16[8,32,1664]{2,1,0:T(8,128)(2,1)} %bitcast.6), calls=%async_computation | async-start | bytes 1703936 | tf_op jit(solution)/shard_map/all_to_all | solution.py:421
  25.2 0.7 collective-permute-start.2
  25.9 0.7 collective-permute-start.4
  26.6 1.5 collective-permute-start.6
  28.1 10.9 %all-to-all-done.received = bf16[8,32,1664]{2,1,0:T(8,128)(2,1)S(1)} async-done(((bf16[8,32,1664]{2,1,0:T(8,128)(2,1)}), bf16[8,32,1664]{2,1,0:T(8,128)(2,1)S(1)}, u32[]{:S(2)}, u32[]{:S(2)}) %all-to-all-start) | async-done | bytes 852000 | tf_op jit(solution)/shard_map/all_to_all | solution.py:421
  39.1 0.7 collective-permute-start.13
  39.8 3.7 %collective-permute-start.9 = (bf16[512,768]{1,0:T(8,128)(2,1)}, bf16[512,768]{1,0:T(8,128)(2,1)S(1)}, u32[]{:S(2)}, u32[]{:S(2)}) collective-permute-start(bf16[512,768]{1,0:T(8,128)(2,1)} %get-tuple-element.42), channel_id=1, source_target_pairs={{0,6},{1,7},{8,14},{9,15},{16,22},{17,23},{24,30},{25,31},{32,38},... | collective-permute-start | bytes 2359304 | tf_op jit(solution)/shard_map/ppermute | solution.py:389
  43.5 0.8 collective-permute-start.16
  44.3 1.9 scatter_updates.1
  46.3 7.6 %collective-permute-start.8 = (bf16[32,32,128]{2,1,0:T(8,128)(2,1)S(1)}, bf16[32,32,128]{2,1,0:T(8,128)(2,1)S(1)}, u32[]{:S(2)}, u32[]{:S(2)}) collective-permute-start(bf16[32,32,128]{2,1,0:T(8,128)(2,1)S(1)} %get-tuple-element.41), channel_id=1, source_target_pairs={{16,0},{24,8},{32,16},{40,24},{48,32},{56,40},{64,48},{72,56},{80,... | collective-permute-start | bytes 786440 | tf_op jit(solution)/shard_map/ppermute | solution.py:385
  53.9 2.9 %collective-permute-start.7 = (bf16[32,32,128]{2,1,0:T(8,128)(2,1)S(1)}, bf16[32,32,128]{2,1,0:T(8,128)(2,1)S(1)}, u32[]{:S(2)}, u32[]{:S(2)}) collective-permute-start(bf16[32,32,128]{2,1,0:T(8,128)(2,1)S(1)} %get-tuple-element.40), channel_id=1, source_target_pairs={{8,0},{16,8},{24,16},{32,24},{40,32},{48,40},{56,48},{64,56},{72,6... | collective-permute-start | bytes 786440 | tf_op jit(solution)/shard_map/ppermute | solution.py:385
  56.8 7.1 %collective-permute-done.8 = bf16[32,32,128]{2,1,0:T(8,128)(2,1)S(1)} collective-permute-done((bf16[32,32,128]{2,1,0:T(8,128)(2,1)S(1)}, bf16[32,32,128]{2,1,0:T(8,128)(2,1)S(1)}, u32[]{:S(2)}, u32[]{:S(2)}) %collective-permute-start.8) | collective-permute-done | bytes 262176 | tf_op jit(solution)/shard_map/ppermute | solution.py:385
  63.9 4.8 %collective-permute-done.7 = bf16[32,32,128]{2,1,0:T(8,128)(2,1)S(1)} collective-permute-done((bf16[32,32,128]{2,1,0:T(8,128)(2,1)S(1)}, bf16[32,32,128]{2,1,0:T(8,128)(2,1)S(1)}, u32[]{:S(2)}, u32[]{:S(2)}) %collective-permute-start.7) | collective-permute-done | bytes 262176 | tf_op jit(solution)/shard_map/ppermute | solution.py:385
  68.7 0.1 subtract_convert_fusion.refs_3_
  68.8 18.6 %collective-permute-done.9.refs_4_.refs_1_ = bf16[512,768]{1,0:T(8,128)(2,1)S(1)} collective-permute-done((bf16[512,768]{1,0:T(8,128)(2,1)}, bf16[512,768]{1,0:T(8,128)(2,1)S(1)}, u32[]{:S(2)}, u32[]{:S(2)}) %collective-permute-start.9) | collective-permute-done | bytes 786464 | tf_op jit(solution)/shard_map/ppermute | solution.py:389
  87.4 5.5 %collective-permute-start.10 = (bf16[32,32,128]{2,1,0:T(8,128)(2,1)S(1)}, bf16[32,32,128]{2,1,0:T(8,128)(2,1)S(1)}, u32[]{:S(2)}, u32[]{:S(2)}) collective-permute-start(bf16[32,32,128]{2,1,0:T(8,128)(2,1)S(1)} %subtract_convert_fusion.refs_3_), channel_id=1, source_target_pairs={{0,6},{1,7},{8,14},{9,15},{16,22},{17,23},{24,30},{25,31},{32,38},... | collective-permute-start | bytes 786440 | tf_op jit(solution)/shard_map/ppermute | solution.py:389
  92.9 5.7 %collective-permute-done.10.refs_0_ = bf16[32,32,128]{2,1,0:T(8,128)(2,1)S(1)} collective-permute-done((bf16[32,32,128]{2,1,0:T(8,128)(2,1)S(1)}, bf16[32,32,128]{2,1,0:T(8,128)(2,1)S(1)}, u32[]{:S(2)}, u32[]{:S(2)}) %collective-permute-start.10) | collective-permute-done | bytes 262176 | tf_op jit(solution)/shard_map/ppermute | solution.py:389
  98.7 0.7 collective-permute-start.15
  99.4 0.7 collective-permute-start.14
  100.1 0.7 collective-permute-start.11
  100.8 0.7 collective-permute-start.12
  101.5 0.8 collective-permute-start.17
  102.4 0.6 sweep_head.1.refs_0_
  103.0 1.4 copy-done.2
  104.5 1.4 sweep_rest.1
  105.8 0.7 collective-permute-start.18
  106.5 0.7 collective-permute-start.19
  107.2 1.3 collective-permute-start.20
  108.5 41.9 %collective-permute-done.20 = bf16[32,32,128]{2,1,0:T(8,128)(2,1)S(1)} collective-permute-done((bf16[32,32,128]{2,1,0:T(8,128)(2,1)S(1)}, bf16[32,32,128]{2,1,0:T(8,128)(2,1)S(1)}, u32[]{:S(2)}, u32[]{:S(2)}) %collective-permute-start.20) | collective-permute-done | bytes 262176 | tf_op jit(solution)/shard_map/ppermute | solution.py:389
  150.5 0.8 select_select_fusion.own
  151.2 3.8 %collective-permute-start.21 = (bf16[32,32,128]{2,1,0:T(8,128)(2,1)}, bf16[32,32,128]{2,1,0:T(8,128)(2,1)S(1)}, u32[]{:S(2)}, u32[]{:S(2)}) collective-permute-start(bf16[32,32,128]{2,1,0:T(8,128)(2,1)} %select_select_fusion.own), channel_id=1, source_target_pairs={{0,8},{8,16},{16,24},{24,32},{32,40},{40,48},{48,56},{56,64},{64,7... | collective-permute-start | bytes 786440 | tf_op jit(solution)/shard_map/ppermute | solution.py:385
  155.1 6.4 %collective-permute-start.22 = (bf16[32,32,128]{2,1,0:T(8,128)(2,1)}, bf16[32,32,128]{2,1,0:T(8,128)(2,1)S(1)}, u32[]{:S(2)}, u32[]{:S(2)}) collective-permute-start(bf16[32,32,128]{2,1,0:T(8,128)(2,1)} %select_select_fusion.own), channel_id=1, source_target_pairs={{0,16},{8,24},{16,32},{24,40},{32,48},{40,56},{48,64},{56,72},{64,... | collective-permute-start | bytes 786440 | tf_op jit(solution)/shard_map/ppermute | solution.py:385
  161.5 5.4 %all-to-all-start.2 = ((bf16[8,4,32,128]{3,2,1,0:T(8,128)(2,1)}), bf16[8,4,32,128]{3,2,1,0:T(8,128)(2,1)S(1)}, u32[]{:S(2)}, u32[]{:S(2)}) async-start(bf16[8,4,32,128]{3,2,1,0:T(8,128)(2,1)} %bitcast.4), calls=%async_computation.2 | async-start | bytes 524288 | tf_op jit(solution)/shard_map/all_to_all | solution.py:443
  166.8 9.5 %collective-permute-done.22.far = bf16[32,32,128]{2,1,0:T(8,128)(2,1)S(1)} collective-permute-done((bf16[32,32,128]{2,1,0:T(8,128)(2,1)}, bf16[32,32,128]{2,1,0:T(8,128)(2,1)S(1)}, u32[]{:S(2)}, u32[]{:S(2)}) %collective-permute-start.22) | collective-permute-done | bytes 262176 | tf_op jit(solution)/shard_map/ppermute | solution.py:385
  176.4 1.9 extract_pieces.1
  178.3 15.6 %all_to_all.15 = bf16[8,32,1024]{2,1,0:T(8,128)(2,1)} all-to-all(bf16[8,32,1024]{2,1,0:T(8,128)(2,1)S(1)} %extract_pieces.1), channel_id=1, replica_groups=mesh['leaf'=32,'sub'=8] {'sub'}, dimensions={0} | all-to-all | bytes 1048576 | tf_op jit(solution)/shard_map/all_to_all | solution.py:444
  193.9 6.0 %leaf_backward.1 = (bf16[4,512,256]{2,1,0:T(8,128)(2,1)}, bf16[512,256]{1,0:T(8,128)(2,1)}) custom-call(bf16[4,256,512]{2,1,0:T(8,128)(2,1)} %get-tuple-element.32.y, bf16[256,1024]{1,0:T(8,128)(2,1)} %bitcast.5, bf16[4,512,512]{2,1,0:T(8,128)(2,1)} %inverse.3, bf16[4,256,512]{2,1,0:T(8,128)(2,1)} %panel.3, bf16[8,4,32,128]{3,2,1,0:T(8,128)(2,1)} %copy-done.3), custom_call_target="tpu_custom_call" | custom-call | tf_op jit(solution)/shard_map/leaf_backward/pallas_call | solution.py:359
  (27 shorter events, 0.1 us)
Async XLA Ops:
  0.6 38.4 %collective-permute-start.1 = (bf16[512,4096]{1,0:T(8,128)(2,1)}, bf16[512,4096]{1,0:T(8,128)(2,1)}, u32[]{:S(2)}, u32[]{:S(2)}) collective-permute-start(bf16[512,4096]{1,0:T(8,128)(2,1)} %refs_11_), channel_id=1, source_target_pairs={{6,7},{7,6},{14,15},{15,14},{22,23},{23,22},{30,31},{31,30},{38,39... | collective-permute-start | bytes 12582920 | tf_op jit(solution)/shard_map/ppermute | solution.py:393
  3.3 22.7 %collective-permute-start.3 = (bf16[512,512]{1,0:T(8,128)(2,1)}, bf16[512,512]{1,0:T(8,128)(2,1)S(1)}, u32[]{:S(2)}, u32[]{:S(2)}) collective-permute-start(bf16[512,512]{1,0:T(8,128)(2,1)} %refs_13_), channel_id=1, source_target_pairs={{2,6},{3,7},{10,14},{11,15},{18,22},{19,23},{26,30},{27,31},{34,38... | collective-permute-start | bytes 1572872 | tf_op jit(solution)/shard_map/ppermute | solution.py:389
  3.9 22.7 %collective-permute-start.5 = (bf16[512,512]{1,0:T(8,128)(2,1)}, bf16[512,512]{1,0:T(8,128)(2,1)S(1)}, u32[]{:S(2)}, u32[]{:S(2)}) collective-permute-start(bf16[512,512]{1,0:T(8,128)(2,1)} %refs_13_), channel_id=1, source_target_pairs={{4,6},{5,7},{12,14},{13,15},{20,22},{21,23},{28,30},{29,31},{36,38... | collective-permute-start | bytes 1572872 | tf_op jit(solution)/shard_map/ppermute | solution.py:389
  5.6 4.0 %collective-permute-start = (bf16[512,256]{1,0:T(8,128)(2,1)S(1)}, bf16[512,256]{1,0:T(8,128)(2,1)S(1)}, u32[]{:S(2)}, u32[]{:S(2)}) collective-permute-start(bf16[512,256]{1,0:T(8,128)(2,1)S(1)} %constant_dynamic-slice_fusion), channel_id=1, source_target_pairs={{1,0},{3,2},{5,4},{9,8},{11,10},{13,12},{17,16},{19,18},{21,20},{2... | collective-permute-start | bytes 786440 | tf_op jit(solution)/shard_map/ppermute | solution.py:417
  9.6 15.6 %copy-start = (bf16[512,512]{1,0:T(8,128)(2,1)S(1)}, bf16[512,512]{1,0:T(8,128)(2,1)}, u32[]{:S(2)}) copy-start(bf16[512,512]{1,0:T(8,128)(2,1)} %refs_13_) | copy-start | bytes 1572868
  9.6 0.7 copy-start.4
  17.4 84.9 %copy-start.1 = (s32[2]{0:T(128)S(1)}, s32[2]{0:T(128)}, u32[]{:S(2)}) copy-start(s32[2]{0:T(128)} %pad_add_fusion.where) | copy-start | bytes 28
  17.4 21.6 %all-to-all-start = ((bf16[8,32,1664]{2,1,0:T(8,128)(2,1)}), bf16[8,32,1664]{2,1,0:T(8,128)(2,1)S(1)}, u32[]{:S(2)}, u32[]{:S(2)}) async-start(bf16[8,32,1664]{2,1,0:T(8,128)(2,1)} %bitcast.6), calls=%async_computation | async-start | bytes 1703936 | tf_op jit(solution)/shard_map/all_to_all | solution.py:421
  25.2 2.9 %collective-permute-start.2 = (bf16[512,512]{1,0:T(8,128)(2,1)S(1)}, bf16[512,512]{1,0:T(8,128)(2,1)S(1)}, u32[]{:S(2)}, u32[]{:S(2)}) collective-permute-start(bf16[512,512]{1,0:T(8,128)(2,1)S(1)} %copy-done), channel_id=1, source_target_pairs={{6,7},{7,6},{14,15},{15,14},{22,23},{23,22},{30,31},{31,30},{38,39... | collective-permute-start | bytes 1572872 | tf_op jit(solution)/shard_map/ppermute | solution.py:393
  25.9 13.1 %collective-permute-start.4 = (bf16[512,512]{1,0:T(8,128)(2,1)S(1)}, bf16[512,512]{1,0:T(8,128)(2,1)S(1)}, u32[]{:S(2)}, u32[]{:S(2)}) collective-permute-start(bf16[512,512]{1,0:T(8,128)(2,1)S(1)} %collective-permute-done.3.refs_8_.refs_5_), channel_id=1, source_target_pairs={{6,7},{7,6},{14,15},{15,14},{22,23},{23,22},{30,31},{31,30},{38,39... | collective-permute-start | bytes 1572872 | tf_op jit(solution)/shard_map/ppermute | solution.py:393
  26.6 12.4 %collective-permute-start.6 = (bf16[512,512]{1,0:T(8,128)(2,1)S(1)}, bf16[512,512]{1,0:T(8,128)(2,1)}, u32[]{:S(2)}, u32[]{:S(2)}) collective-permute-start(bf16[512,512]{1,0:T(8,128)(2,1)S(1)} %collective-permute-done.5.refs_9_), channel_id=1, source_target_pairs={{6,7},{7,6},{14,15},{15,14},{22,23},{23,22},{30,31},{31,30},{38,39... | collective-permute-start | bytes 1572872 | tf_op jit(solution)/shard_map/ppermute | solution.py:393
  39.1 59.6 %collective-permute-start.13 = (bf16[512,1280]{1,0:T(8,128)(2,1)}, bf16[512,1280]{1,0:T(8,128)(2,1)S(1)}, u32[]{:S(2)}, u32[]{:S(2)}) collective-permute-start(bf16[512,1280]{1,0:T(8,128)(2,1)} %get-tuple-element.45), channel_id=1, source_target_pairs={{2,6},{3,7},{10,14},{11,15},{18,22},{19,23},{26,30},{27,31},{34,38... | collective-permute-start | bytes 3932168 | tf_op jit(solution)/shard_map/ppermute | solution.py:389
  39.8 47.6 %collective-permute-start.9 = (bf16[512,768]{1,0:T(8,128)(2,1)}, bf16[512,768]{1,0:T(8,128)(2,1)S(1)}, u32[]{:S(2)}, u32[]{:S(2)}) collective-permute-start(bf16[512,768]{1,0:T(8,128)(2,1)} %get-tuple-element.42), channel_id=1, source_target_pairs={{0,6},{1,7},{8,14},{9,15},{16,22},{17,23},{24,30},{25,31},{32,38},... | collective-permute-start | bytes 2359304 | tf_op jit(solution)/shard_map/ppermute | solution.py:389
  43.5 58.0 %collective-permute-start.16 = (bf16[512,2304]{1,0:T(8,128)(2,1)}, bf16[512,2304]{1,0:T(8,128)(2,1)S(1)}, u32[]{:S(2)}, u32[]{:S(2)}) collective-permute-start(bf16[512,2304]{1,0:T(8,128)(2,1)} %get-tuple-element.50), channel_id=1, source_target_pairs={{4,6},{5,7},{12,14},{13,15},{20,22},{21,23},{28,30},{29,31},{36,38... | collective-permute-start | bytes 7077896 | tf_op jit(solution)/shard_map/ppermute | solution.py:389
  46.3 17.6 %collective-permute-start.8 = (bf16[32,32,128]{2,1,0:T(8,128)(2,1)S(1)}, bf16[32,32,128]{2,1,0:T(8,128)(2,1)S(1)}, u32[]{:S(2)}, u32[]{:S(2)}) collective-permute-start(bf16[32,32,128]{2,1,0:T(8,128)(2,1)S(1)} %get-tuple-element.41), channel_id=1, source_target_pairs={{16,0},{24,8},{32,16},{40,24},{48,32},{56,40},{64,48},{72,56},{80,... | collective-permute-start | bytes 786440 | tf_op jit(solution)/shard_map/ppermute | solution.py:385
  53.9 14.8 %collective-permute-start.7 = (bf16[32,32,128]{2,1,0:T(8,128)(2,1)S(1)}, bf16[32,32,128]{2,1,0:T(8,128)(2,1)S(1)}, u32[]{:S(2)}, u32[]{:S(2)}) collective-permute-start(bf16[32,32,128]{2,1,0:T(8,128)(2,1)S(1)} %get-tuple-element.40), channel_id=1, source_target_pairs={{8,0},{16,8},{24,16},{32,24},{40,32},{48,40},{56,48},{64,56},{72,6... | collective-permute-start | bytes 786440 | tf_op jit(solution)/shard_map/ppermute | solution.py:385
  87.4 11.2 %collective-permute-start.10 = (bf16[32,32,128]{2,1,0:T(8,128)(2,1)S(1)}, bf16[32,32,128]{2,1,0:T(8,128)(2,1)S(1)}, u32[]{:S(2)}, u32[]{:S(2)}) collective-permute-start(bf16[32,32,128]{2,1,0:T(8,128)(2,1)S(1)} %subtract_convert_fusion.refs_3_), channel_id=1, source_target_pairs={{0,6},{1,7},{8,14},{9,15},{16,22},{17,23},{24,30},{25,31},{32,38},... | collective-permute-start | bytes 786440 | tf_op jit(solution)/shard_map/ppermute | solution.py:389
  98.7 2.9 %collective-permute-start.15 = (bf16[512,1280]{1,0:T(8,128)(2,1)S(1)}, bf16[512,1280]{1,0:T(8,128)(2,1)S(1)}, u32[]{:S(2)}, u32[]{:S(2)}) collective-permute-start(bf16[512,1280]{1,0:T(8,128)(2,1)S(1)} %collective-permute-done.13.refs_6_.refs_3_), channel_id=1, source_target_pairs={{6,7},{7,6},{14,15},{15,14},{22,23},{23,22},{30,31},{31,30},{38,39... | collective-permute-start | bytes 3932168 | tf_op jit(solution)/shard_map/ppermute | solution.py:393
  99.4 2.1 %collective-permute-start.14 = (bf16[512,768]{1,0:T(8,128)(2,1)S(1)}, bf16[512,768]{1,0:T(8,128)(2,1)S(1)}, u32[]{:S(2)}, u32[]{:S(2)}) collective-permute-start(bf16[512,768]{1,0:T(8,128)(2,1)S(1)} %collective-permute-done.9.refs_4_.refs_1_), channel_id=1, source_target_pairs={{6,7},{7,6},{14,15},{15,14},{22,23},{23,22},{30,31},{31,30},{38,39... | collective-permute-start | bytes 2359304 | tf_op jit(solution)/shard_map/ppermute | solution.py:393
  100.1 1.4 collective-permute-start.11
  100.8 0.7 collective-permute-start.12
  101.5 1.5 collective-permute-start.17
  103.0 1.4 copy-start.2
  105.8 2.7 %collective-permute-start.18 = (bf16[32,32,128]{2,1,0:T(8,128)(2,1)}, bf16[32,32,128]{2,1,0:T(8,128)(2,1)S(1)}, u32[]{:S(2)}, u32[]{:S(2)}) collective-permute-start(bf16[32,32,128]{2,1,0:T(8,128)(2,1)} %get-tuple-element.59), channel_id=1, source_target_pairs={{6,4},{7,5},{14,12},{15,13},{22,20},{23,21},{30,28},{31,29},{38,36... | collective-permute-start | bytes 786440 | tf_op jit(solution)/shard_map/ppermute | solution.py:389
  106.5 2.0 %collective-permute-start.19 = (bf16[32,32,128]{2,1,0:T(8,128)(2,1)S(1)}, bf16[32,32,128]{2,1,0:T(8,128)(2,1)S(1)}, u32[]{:S(2)}, u32[]{:S(2)}) collective-permute-start(bf16[32,32,128]{2,1,0:T(8,128)(2,1)S(1)} %get-tuple-element.60), channel_id=1, source_target_pairs={{6,2},{7,3},{14,10},{15,11},{22,18},{23,19},{30,26},{31,27},{38,34... | collective-permute-start | bytes 786440 | tf_op jit(solution)/shard_map/ppermute | solution.py:389
  107.2 43.2 %collective-permute-start.20 = (bf16[32,32,128]{2,1,0:T(8,128)(2,1)S(1)}, bf16[32,32,128]{2,1,0:T(8,128)(2,1)S(1)}, u32[]{:S(2)}, u32[]{:S(2)}) collective-permute-start(bf16[32,32,128]{2,1,0:T(8,128)(2,1)S(1)} %get-tuple-element.61), channel_id=1, source_target_pairs={{6,0},{7,1},{14,8},{15,9},{22,16},{23,17},{30,24},{31,25},{38,32},... | collective-permute-start | bytes 786440 | tf_op jit(solution)/shard_map/ppermute | solution.py:389
  151.2 15.6 %collective-permute-start.21 = (bf16[32,32,128]{2,1,0:T(8,128)(2,1)}, bf16[32,32,128]{2,1,0:T(8,128)(2,1)S(1)}, u32[]{:S(2)}, u32[]{:S(2)}) collective-permute-start(bf16[32,32,128]{2,1,0:T(8,128)(2,1)} %select_select_fusion.own), channel_id=1, source_target_pairs={{0,8},{8,16},{16,24},{24,32},{32,40},{40,48},{48,56},{56,64},{64,7... | collective-permute-start | bytes 786440 | tf_op jit(solution)/shard_map/ppermute | solution.py:385
  155.1 21.3 %collective-permute-start.22 = (bf16[32,32,128]{2,1,0:T(8,128)(2,1)}, bf16[32,32,128]{2,1,0:T(8,128)(2,1)S(1)}, u32[]{:S(2)}, u32[]{:S(2)}) collective-permute-start(bf16[32,32,128]{2,1,0:T(8,128)(2,1)} %select_select_fusion.own), channel_id=1, source_target_pairs={{0,16},{8,24},{16,32},{24,40},{32,48},{40,56},{48,64},{56,72},{64,... | collective-permute-start | bytes 786440 | tf_op jit(solution)/shard_map/ppermute | solution.py:385
  161.5 16.8 %all-to-all-start.2 = ((bf16[8,4,32,128]{3,2,1,0:T(8,128)(2,1)}), bf16[8,4,32,128]{3,2,1,0:T(8,128)(2,1)S(1)}, u32[]{:S(2)}, u32[]{:S(2)}) async-start(bf16[8,4,32,128]{3,2,1,0:T(8,128)(2,1)} %bitcast.4), calls=%async_computation.2 | async-start | bytes 524288 | tf_op jit(solution)/shard_map/all_to_all | solution.py:443
  178.3 15.7 %copy-start.3 = (bf16[8,4,32,128]{3,2,1,0:T(8,128)(2,1)}, bf16[8,4,32,128]{3,2,1,0:T(8,128)(2,1)S(1)}, u32[]{:S(2)}) copy-start(bf16[8,4,32,128]{3,2,1,0:T(8,128)(2,1)S(1)} %all-to-all-done.2.rows) | copy-start | bytes 786436

commit v3 on v2

--- a/solution.py
+++ b/solution.py
@@ -33,7 +33,7 @@
 
 
 def for_each_source(where, visit):
-    for chip, wide in ((2, 4 * WSN), (1, 2 * WSN), (0, WSN)):
+    for chip, wide in ((2, 4 * WSN), (1, 2 * WSN), (0, 0)):
 
         @pl.when(where[0] == chip)
         def _():
@@ -41,14 +41,14 @@
 
 
 def leaf_forward_kernel(
-    where, slots, right, inverse, panel, sep_right, half, factor, sep_inverse, y_out, send, pack2, pack1, pack0, sems
+    where, subtree, block, right, inverse, panel, sep_right, half, factor, y_out, send, pack2, pack1, pack0, sems
 ):
     j = pl.program_id(0)
     packs = (pack0, pack1, pack2)
 
     def begin(chip, wide):
-        rows = sep_inverse if chip == 0 else factor.at[:, 0:wide]
-        pltpu.make_async_copy(rows, packs[chip].at[:, 0:wide], sems.at[0]).start()
+        if wide:
+            pltpu.make_async_copy(factor.at[:, 0:wide], packs[chip].at[:, 0:wide], sems.at[0]).start()
         rest = packs[chip].at[:, wide : wide + WSN // 2]
 
         @pl.when(where[1] == 1)
@@ -61,15 +61,23 @@
             pltpu.make_async_copy(half, rest, sems.at[1]).start()
 
     def end(chip, wide):
-        whole, rest = packs[chip].at[:, 0:wide], packs[chip].at[:, wide : wide + WSN // 2]
-        pltpu.make_async_copy(whole, whole, sems.at[0]).wait()
+        if wide:
+            whole = packs[chip].at[:, 0:wide]
+            pltpu.make_async_copy(whole, whole, sems.at[0]).wait()
+        rest = packs[chip].at[:, wide : wide + WSN // 2]
         pltpu.make_async_copy(rest, rest, sems.at[1]).wait()
 
     @pl.when(j == 0)
     def _():
         for_each_source(where, begin)
         send[:, UPD:SLOT] = sep_right[...].T
-        send[:, SLOT:] = jnp.broadcast_to(slots[...], (R, 128)).astype(bf16)
+        lane = lax.broadcasted_iota(jnp.int32, (R, 128), 1)
+        slots = jnp.zeros((R, 128), jnp.int32)
+        for leaf in range(SN_DEV):
+            for k in range(KB):
+                slot = (where[2] - subtree[leaf]) * (SA // BLK) + block[leaf, k]
+                slots = jnp.where(lane == leaf * KB + k, slot, slots)
+        send[:, SLOT:] = slots.astype(f32).astype(bf16)
 
     y = dot(right[0].T, inverse[0], NT).astype(bf16)
     y_out[0] = y
@@ -80,20 +88,20 @@
         for_each_source(where, end)
 
 
-def leaf_forward(where, slots, right, inverse, panels, sep_right, half, factor, sep_inverse):
+def leaf_forward(where, subtree, block, right, inverse, panels, sep_right, half, factor):
     hbm = pl.BlockSpec(memory_space=pltpu.HBM)
-    sizes = [(WSN, n * WSN + WSN // 2) for n in (4, 2, 1)]
+    sizes = [(WSN, n * WSN + WSN // 2) for n in (4, 2, 0)]
     return pl.pallas_call(
         leaf_forward_kernel,
         grid=(SN_DEV,),
         in_specs=[
             pl.BlockSpec(memory_space=pltpu.SMEM),
-            pl.BlockSpec((1, 128), lambda j: (0, 0)),
+            pl.BlockSpec(memory_space=pltpu.SMEM),
+            pl.BlockSpec(memory_space=pltpu.SMEM),
             pl.BlockSpec((1, W, R), lambda j: (j, 0, 0)),
             pl.BlockSpec((1, W, W), lambda j: (j, 0, 0)),
             pl.BlockSpec((1, KB * BLK, W), lambda j: (j, 0, 0)),
             pl.BlockSpec((WSN, R), lambda j: (0, 0)),
-            hbm,
             hbm,
             hbm,
         ],
@@ -110,7 +118,7 @@
         scratch_shapes=[pltpu.SemaphoreType.DMA((2,))],
         compiler_params=pltpu.CompilerParams(dimension_semantics=("arbitrary",), vmem_limit_bytes=WHOLE),
         name="leaf_forward",
-    )(where, slots, right, inverse, panels, sep_right, half, factor, sep_inverse)
+    )(where, subtree, block, right, inverse, panels, sep_right, half, factor)
 
 
 def scatter_kernel(received, base, near, far, slots_out, table, slots, sem):
@@ -170,8 +178,7 @@
         q = 2 * k + (1 - core if other else core)
         rows = pl.ds(pl.multiple_of(q * WSN, WSN), WSN)
         wide, inverse = blocks[k][other]
-        block = wide.at[:, 0:WSN] if k == 0 else inverse
-        pltpu.make_async_copy(block, diagonal.at[rows], sems.at[0, k]).start()
+        pltpu.make_async_copy(inverse, diagonal.at[rows], sems.at[0, k]).start()
         if k > 0:
             pltpu.make_async_copy(wide.at[:, 0:width], lower.at[rows, 0:width], sems.at[1, k]).start()
         for c in (0, 1):
@@ -185,7 +192,7 @@
                         dst = lower.at[odd, width : width + WSN]
                         pltpu.make_async_copy(block, dst, sems.at[2, k]).start()
                 else:
-                    first = WSN if k == 0 else width
+                    first = width
                     block = wide.at[:, first : first + WSN // 2]
                     at = width + (1 - sender) * (WSN // 2)
                     dst = lower.at[odd, at : at + WSN // 2]
@@ -213,8 +220,8 @@
 
 def head_kernel(where, *refs):
     rhs = refs[0:4]
-    blocks = {0: ((refs[4], None), (refs[5], None)), 1: ((refs[6], refs[8]), (refs[7], refs[9]))}
-    state, lower, diagonal, shares, rhs_sem, sems = refs[10:]
+    blocks = {0: ((refs[4], refs[6]), (refs[5], refs[7])), 1: ((refs[8], refs[10]), (refs[9], refs[11]))}
+    state, lower, diagonal, shares, rhs_sem, sems = refs[12:]
 
     @pl.when(where[0] == HUB)
     def _():
@@ -235,13 +242,13 @@
 def rest_kernel(where, *refs):
     begun = refs[0]
     blocks = {
-        0: ((refs[1], None), (refs[2], None)),
-        1: ((refs[3], refs[5]), (refs[4], refs[6])),
-        2: ((refs[7], refs[9]), (refs[8], refs[10])),
-        3: ((refs[11], refs[13]), (refs[12], refs[14])),
+        0: ((refs[1], refs[3]), (refs[2], refs[4])),
+        1: ((refs[5], refs[7]), (refs[6], refs[8])),
+        2: ((refs[9], refs[11]), (refs[10], refs[12])),
+        3: ((refs[13], refs[15]), (refs[14], refs[16])),
     }
-    outs = refs[15:19]
-    lower, diagonal, state, state_sem, sems = refs[19:]
+    outs = refs[17:21]
+    lower, diagonal, state, state_sem, sems = refs[21:]
 
     @pl.when(where[0] == HUB)
     def _():
@@ -374,7 +381,7 @@
             jax.ShapeDtypeStruct((SN_DEV, W, R), bf16),
             jax.ShapeDtypeStruct((WSN, R), bf16),
         ],
-        compiler_params=pltpu.CompilerParams(dimension_semantics=("arbitrary",), vmem_limit_bytes=WHOLE),
+        compiler_params=pltpu.CompilerParams(dimension_semantics=("arbitrary",), vmem_limit_bytes=24 * MIB),
         name="leaf_backward",
     )(y, pieces, inverse, panels, rows)
 
@@ -406,37 +413,43 @@
     section = lax.axis_index("leaf")
     member = lax.axis_index("sub")
     chip, core = member // 2, member % 2
-    where = jnp.stack([chip, core]).astype(jnp.int32)
-    row_blocks = SA // BLK
-    own_slots = ((section - leaf_subtree)[:, None] * row_blocks + panel_block).reshape(1, -1)
-    own_slots = jnp.pad(own_slots.astype(f32), ((0, 0), (0, 128 - SN_DEV * KB)))
-    inverse2, inverse1 = hop(separator_inverse, (2, HUB)), hop(separator_inverse, (1, HUB))
+    where = jnp.stack([chip, core, section]).astype(jnp.int32)
+    early = [hop(separator_inverse, (k, HUB)) for k in range(3)]
     factors = (separator_factor, swap(separator_factor))
     inverses = (separator_inverse, swap(separator_inverse))
     half = lax.dynamic_slice(separator_factor, (0, 2 * WSN * chip + WSN // 2), (WSN, WSN // 2))
     half = lax.ppermute(half, "sub", [(2 * k + 1, 2 * k) for k in range(3)])
     y, send, *packs = leaf_forward(
-        where, own_slots, leaf_right, leaf_inverse, panels, separator_right, half, separator_factor, separator_inverse
+        where,
+        leaf_subtree,
+        panel_block,
+        leaf_right,
+        leaf_inverse,
+        panels,
+        separator_right,
+        half,
+        separator_factor,
     )
     received = lax.all_to_all(send.reshape(GROUP, COLS, SEND), "sub", 0, 0, tiled=True)
-    inverse1, inverse2 = (inverse1, swap(inverse1)), (inverse2, swap(inverse2))
-    received, packs, factors, inverses, inverse1, inverse2 = lax.optimization_barrier(
-        (received, packs, factors, inverses, inverse1, inverse2)
+    early = [(block, swap(block)) for block in early]
+    received, packs, factors, inverses, early = lax.optimization_barrier(
+        (received, packs, factors, inverses, early)
     )
     pack2, pack1, pack0 = (hop(block, (k, HUB)) for block, k in zip(packs, (2, 1, 0)))
     base, near, far, slots = scatter(received)
-    near_sum = along_leaf(near, -1).astype(f32)
-    far_sum = along_leaf(far, -2).astype(f32)
-    rhs = (base - near_sum - far_sum).astype(bf16)
-    to_hub = [None, hop(rhs, (1, HUB)), hop(rhs, (2, HUB)), rhs]
-    rhs, pack0 = lax.optimization_barrier((rhs, pack0))
-    to_hub[0] = hop(rhs, (0, HUB))
-    pack0, pack1 = lax.optimization_barrier((pack0, pack1, to_hub[0]))[:2]
-    pack0, pack1 = (pack0, swap(pack0)), (pack1, swap(pack1))
-    pack2 = lax.optimization_barrier((pack2, *to_hub[:3], pack0, pack1))[0]
+    near, far = along_leaf(near, -1), along_leaf(far, -2)
+    pack1 = lax.optimization_barrier((pack1, near, far))[0]
+    pack1 = (pack1, swap(pack1))
+    near, far, pack0, pack1 = lax.optimization_barrier((near, far, pack0, pack1))
+    rhs = (base - near.astype(f32) - far.astype(f32)).astype(bf16)
+    pack0 = (pack0, swap(pack0))
+    to_hub = [hop(rhs, (k, HUB)) for k in range(3)] + [rhs]
+    pack2 = lax.optimization_barrier((pack2, *to_hub[:3], pack0))[0]
     pack2 = (pack2, swap(pack2))
-    begun = sweep_head(where, *to_hub, *pack0, *pack1, *inverse1)
-    shares = sweep_rest(where, begun, *pack0, *pack1, *inverse1, *pack2, *inverse2, *factors, *inverses)
+    begun = sweep_head(where, *to_hub, *pack0, *early[0], *pack1, *early[1])
+    shares = sweep_rest(
+        where, begun, *pack0, *early[0], *pack1, *early[1], *pack2, *early[2], *factors, *inverses
+    )
     back = [hop(shares[k], (HUB, k)) for k in range(3)] + [shares[HUB]]
     own = jnp.where(chip == 3, back[3], jnp.where(chip == 2, back[2], jnp.where(chip == 1, back[1], back[0])))
     pieces = extract(slots, own, along_leaf(own, 1), along_leaf(own, 2))

time: 201 us -> 195 us (0.970)
  waiting for transfers between devices: 98.7 us -> 75.1 us
  starting transfers between devices: 59 us -> 76.8 us
  local copies, waits for them, and re-layouts: 3.79 us -> 6.62 us
    ppermute x11 -> x12, starting transfers between devices: 16.1 us -> 37.9 us  [hop(): lax.ppermute(block, 'sub', [(2 * a + c, 2 * b + c) for a, b in chips for...]
    ppermute x11 -> x12, waiting for transfers between devices: 66.3 us -> 50.5 us  [hop(): lax.ppermute(block, 'sub', [(2 * a + c, 2 * b + c) for a, b in chips for...]
    all_to_all x1, waiting for transfers between devices: 10.9 us -> 3.89 us  [shards(): lax.all_to_all(send.reshape(GROUP, COLS, SEND), 'sub', 0, 0, tiled=True)]
    all_to_all x1, starting transfers between devices: 7.76 us -> 4.07 us  [shards(): lax.all_to_all(send.reshape(GROUP, COLS, SEND), 'sub', 0, 0, tiled=True)]
    unnamed x10 -> x22, local copies, waits for them, and re-layouts: 2.14 us -> 5.65 us
    ppermute x4, waiting for transfers between devices: 21.5 us -> 19.1 us  [along_leaf(): return lax.ppermute(block, 'leaf', route)]
    pallas_call x1, Pallas kernels: 5.98 us -> 3.86 us  [leaf_backward(): pl.pallas_call(leaf_backward_kernel, grid=(SN_DEV,), in_specs=[pl.BlockSp...]
    ppermute x7 -> x8, starting transfers between devices: 7.76 us -> 8.42 us  [swap(): lax.ppermute(block, 'sub', [(2 * HUB + c, 2 * HUB + 1 - c) for c in cores])]
  transfers between devices with their start and end apart: 25 -> 27, of which waited for: 7 -> 9; matrix products, arithmetic and copies ran while one was open for 2% -> 1% of each run, Pallas kernels for 6% -> 6%
where the time goes in v3:
time: 195 us; the launch traced here: 194 us
  starting transfers between devices  76.8 us (39%)
  waiting for transfers between devices  75.1 us (39%)
  Pallas kernels  16.9 us (9%)
  blocking collectives  14.8 us (8%)
  local copies, waits for them, and re-layouts  6.62 us (3%)
  other arithmetic  2.42 us (1%)
    ppermute x12, waiting for transfers between devices, hop(): lax.ppermute(block, 'sub', [(2 * a + c, 2 * b + c) for a, b in chips for...  50.5 us
    ppermute x12, starting transfers between devices, hop(): lax.ppermute(block, 'sub', [(2 * a + c, 2 * b + c) for a, b in chips for...  37.9 us
    ppermute x4, starting transfers between devices, along_leaf(): return lax.ppermute(block, 'leaf', route)  20.7 us
    ppermute x4, waiting for transfers between devices, along_leaf(): return lax.ppermute(block, 'leaf', route)  19.1 us
    all_to_all x1, blocking collectives, shards(): pieces = lax.all_to_all(pieces, 'sub', 0, 0, tiled=True).reshape(R, UPD)  14.8 us
    ppermute x8, starting transfers between devices, swap(): lax.ppermute(block, 'sub', [(2 * HUB + c, 2 * HUB + 1 - c) for c in cores])  8.42 us
    pallas_call x1, Pallas kernels, leaf_forward(): pl.pallas_call(leaf_forward_kernel, grid=(SN_DEV,), in_specs=[pl.BlockSpe...  6.9 us
    unnamed x22, local copies, waits for them, and re-layouts  5.65 us
  transfers between devices with their start and end apart: 27, of which 9 were waited for; matrix products, arithmetic and copies ran while one was open for 1% of the time, Pallas kernels for 6%

profile of v3, /device:TPU:38, one launch (start us, length us, event | category | flops | bytes accessed | tf_op | source)
XLA Modules:
  0.0 193.7 jit_solution(12161247729838501039)
XLA Ops:
  0.6 2.7 %collective-permute-start.1 = (bf16[512,4096]{1,0:T(8,128)(2,1)}, bf16[512,4096]{1,0:T(8,128)(2,1)}, u32[]{:S(2)}, u32[]{:S(2)}) collective-permute-start(bf16[512,4096]{1,0:T(8,128)(2,1)} %refs_13_), channel_id=1, source_target_pairs={{6,7},{7,6},{14,15},{15,14},{22,23},{23,22},{30,31},{31,30},{38,39... | collective-permute-start | bytes 12582920 | tf_op jit(solution)/shard_map/ppermute | solution.py:400
  3.3 4.2 %collective-permute-start.3 = (bf16[512,512]{1,0:T(8,128)(2,1)}, bf16[512,512]{1,0:T(8,128)(2,1)S(1)}, u32[]{:S(2)}, u32[]{:S(2)}) collective-permute-start(bf16[512,512]{1,0:T(8,128)(2,1)} %refs_15_), channel_id=1, source_target_pairs={{0,6},{1,7},{8,14},{9,15},{16,22},{17,23},{24,30},{25,31},{32,38},... | collective-permute-start | bytes 1572872 | tf_op jit(solution)/shard_map/ppermute | solution.py:396
  7.5 0.7 collective-permute-start.5
  8.2 1.5 collective-permute-start.7
  9.7 1.0 constant_dynamic-slice_fusion
  10.7 1.3 collective-permute-start
  12.6 1.5 collective-permute-done.half
  14.1 0.7 copy-done.10
  14.8 6.9 %leaf_forward.1 = (bf16[4,256,512]{2,1,0:T(8,128)(2,1)}, bf16[256,1664]{1,0:T(8,128)(2,1)}, bf16[512,2304]{1,0:T(8,128)(2,1)}, bf16[512,1280]{1,0:T(8,128)(2,1)}, bf16[512,256]{1,0:T(8,128)(2,1)}) custom-call(s32[3]{0:T(128)} %pad_add_fusion.where, s32[4]{0:T(128)} %subtree.1, s32[4,4]{1,0:T(4,128)} %block.1, bf16[4,512,256]{2,1,0:T(8,128)(2,1)} %right.1, ...), custom_call_target="tpu_custom_call" | custom-call | tf_op jit(solution)/shard_map/leaf_forward/pallas_call | solution.py:94
  21.7 4.1 %all-to-all-start = ((bf16[8,32,1664]{2,1,0:T(8,128)(2,1)}), bf16[8,32,1664]{2,1,0:T(8,128)(2,1)S(1)}, u32[]{:S(2)}, u32[]{:S(2)}) async-start(bf16[8,32,1664]{2,1,0:T(8,128)(2,1)} %bitcast.7), calls=%async_computation | async-start | bytes 1703936 | tf_op jit(solution)/shard_map/all_to_all | solution.py:433
  25.8 0.7 collective-permute-start.2
  26.5 5.9 %collective-permute-done.3.refs_6_.refs_3_ = bf16[512,512]{1,0:T(8,128)(2,1)S(1)} collective-permute-done((bf16[512,512]{1,0:T(8,128)(2,1)}, bf16[512,512]{1,0:T(8,128)(2,1)S(1)}, u32[]{:S(2)}, u32[]{:S(2)}) %collective-permute-start.3) | collective-permute-done | bytes 524320 | tf_op jit(solution)/shard_map/ppermute | solution.py:396
  32.4 0.7 collective-permute-start.4
  33.1 0.7 collective-permute-start.6
  33.8 1.5 collective-permute-start.8
  35.3 0.8 copy-done.5
  36.1 3.9 %all-to-all-done.received = bf16[8,32,1664]{2,1,0:T(8,128)(2,1)S(1)} async-done(((bf16[8,32,1664]{2,1,0:T(8,128)(2,1)}), bf16[8,32,1664]{2,1,0:T(8,128)(2,1)S(1)}, u32[]{:S(2)}, u32[]{:S(2)}) %all-to-all-start) | async-done | bytes 852000 | tf_op jit(solution)/shard_map/all_to_all | solution.py:433
  40.0 0.7 collective-permute-start.12
  40.8 0.8 collective-permute-start.18
  41.6 1.9 scatter_updates.1
  43.5 2.0 %collective-permute-start.9 = (bf16[32,32,128]{2,1,0:T(8,128)(2,1)S(1)}, bf16[32,32,128]{2,1,0:T(8,128)(2,1)S(1)}, u32[]{:S(2)}, u32[]{:S(2)}) collective-permute-start(bf16[32,32,128]{2,1,0:T(8,128)(2,1)S(1)} %get-tuple-element.44), channel_id=1, source_target_pairs={{8,0},{16,8},{24,16},{32,24},{40,32},{48,40},{56,48},{64,56},{72,6... | collective-permute-start | bytes 786440 | tf_op jit(solution)/shard_map/ppermute | solution.py:392
  45.6 8.5 %collective-permute-start.10 = (bf16[32,32,128]{2,1,0:T(8,128)(2,1)S(1)}, bf16[32,32,128]{2,1,0:T(8,128)(2,1)S(1)}, u32[]{:S(2)}, u32[]{:S(2)}) collective-permute-start(bf16[32,32,128]{2,1,0:T(8,128)(2,1)S(1)} %get-tuple-element.45), channel_id=1, source_target_pairs={{16,0},{24,8},{32,16},{40,24},{48,32},{56,40},{64,48},{72,56},{80,... | collective-permute-start | bytes 786440 | tf_op jit(solution)/shard_map/ppermute | solution.py:392
  54.0 8.6 %collective-permute-done.10 = bf16[32,32,128]{2,1,0:T(8,128)(2,1)S(1)} collective-permute-done((bf16[32,32,128]{2,1,0:T(8,128)(2,1)S(1)}, bf16[32,32,128]{2,1,0:T(8,128)(2,1)S(1)}, u32[]{:S(2)}, u32[]{:S(2)}) %collective-permute-start.10) | collective-permute-done | bytes 262176 | tf_op jit(solution)/shard_map/ppermute | solution.py:392
  62.6 0.7 collective-permute-start.13
  63.4 19.4 %collective-permute-start.11 = (bf16[512,256]{1,0:T(8,128)(2,1)}, bf16[512,256]{1,0:T(8,128)(2,1)S(1)}, u32[]{:S(2)}, u32[]{:S(2)}) collective-permute-start(bf16[512,256]{1,0:T(8,128)(2,1)} %get-tuple-element.46), channel_id=1, source_target_pairs={{0,6},{1,7},{8,14},{9,15},{16,22},{17,23},{24,30},{25,31},{32,38},... | collective-permute-start | bytes 786440 | tf_op jit(solution)/shard_map/ppermute | solution.py:396
  82.8 6.5 %collective-permute-done.11.refs_4_.refs_1_ = bf16[512,256]{1,0:T(8,128)(2,1)S(1)} collective-permute-done((bf16[512,256]{1,0:T(8,128)(2,1)}, bf16[512,256]{1,0:T(8,128)(2,1)S(1)}, u32[]{:S(2)}, u32[]{:S(2)}) %collective-permute-start.11) | collective-permute-done | bytes 262176 | tf_op jit(solution)/shard_map/ppermute | solution.py:396
  89.4 5.6 %collective-permute-start.14 = (bf16[32,32,128]{2,1,0:T(8,128)(2,1)S(1)}, bf16[32,32,128]{2,1,0:T(8,128)(2,1)S(1)}, u32[]{:S(2)}, u32[]{:S(2)}) collective-permute-start(bf16[32,32,128]{2,1,0:T(8,128)(2,1)S(1)} %subtract_convert_fusion.refs_3_), channel_id=1, source_target_pairs={{0,6},{1,7},{8,14},{9,15},{16,22},{17,23},{24,30},{25,31},{32,38},... | collective-permute-start | bytes 786440 | tf_op jit(solution)/shard_map/ppermute | solution.py:396
  95.0 0.7 collective-permute-start.15
  95.7 0.7 collective-permute-start.16
  97.1 9.0 %collective-permute-done.14.refs_0_ = bf16[32,32,128]{2,1,0:T(8,128)(2,1)S(1)} collective-permute-done((bf16[32,32,128]{2,1,0:T(8,128)(2,1)S(1)}, bf16[32,32,128]{2,1,0:T(8,128)(2,1)S(1)}, u32[]{:S(2)}, u32[]{:S(2)}) %collective-permute-start.14) | collective-permute-done | bytes 262176 | tf_op jit(solution)/shard_map/ppermute | solution.py:396
  106.1 0.8 collective-permute-start.19
  107.6 1.4 copy-done.9
  109.0 1.5 sweep_rest.1
  110.5 0.7 copy-done.7
  111.2 0.8 collective-permute-start.20
  112.0 1.5 collective-permute-start.21
  113.5 1.3 collective-permute-start.22
  114.8 29.1 %collective-permute-done.22 = bf16[32,32,128]{2,1,0:T(8,128)(2,1)} collective-permute-done((bf16[32,32,128]{2,1,0:T(8,128)(2,1)}, bf16[32,32,128]{2,1,0:T(8,128)(2,1)}, u32[]{:S(2)}, u32[]{:S(2)}) %collective-permute-start.22) | collective-permute-done | bytes 262176 | tf_op jit(solution)/shard_map/ppermute | solution.py:396
  144.0 1.7 select_select_fusion.own
  145.7 3.8 %collective-permute-start.23 = (bf16[32,32,128]{2,1,0:T(8,128)(2,1)}, bf16[32,32,128]{2,1,0:T(8,128)(2,1)}, u32[]{:S(2)}, u32[]{:S(2)}) collective-permute-start(bf16[32,32,128]{2,1,0:T(8,128)(2,1)} %select_select_fusion.own), channel_id=1, source_target_pairs={{0,8},{8,16},{16,24},{24,32},{32,40},{40,48},{48,56},{56,64},{64,7... | collective-permute-start | bytes 786440 | tf_op jit(solution)/shard_map/ppermute | solution.py:392
  149.5 6.4 %collective-permute-start.24 = (bf16[32,32,128]{2,1,0:T(8,128)(2,1)}, bf16[32,32,128]{2,1,0:T(8,128)(2,1)}, u32[]{:S(2)}, u32[]{:S(2)}) collective-permute-start(bf16[32,32,128]{2,1,0:T(8,128)(2,1)} %select_select_fusion.own), channel_id=1, source_target_pairs={{0,16},{8,24},{16,32},{24,40},{32,48},{40,56},{48,64},{56,72},{64,... | collective-permute-start | bytes 786440 | tf_op jit(solution)/shard_map/ppermute | solution.py:392
  155.9 4.5 %all-to-all-start.2 = ((bf16[8,4,32,128]{3,2,1,0:T(8,128)(2,1)}), bf16[8,4,32,128]{3,2,1,0:T(8,128)(2,1)S(1)}, u32[]{:S(2)}, u32[]{:S(2)}) async-start(bf16[8,4,32,128]{3,2,1,0:T(8,128)(2,1)} %bitcast.5), calls=%async_computation.2 | async-start | bytes 524288 | tf_op jit(solution)/shard_map/all_to_all | solution.py:456
  160.9 10.0 %collective-permute-done.24.far = bf16[32,32,128]{2,1,0:T(8,128)(2,1)} collective-permute-done((bf16[32,32,128]{2,1,0:T(8,128)(2,1)}, bf16[32,32,128]{2,1,0:T(8,128)(2,1)}, u32[]{:S(2)}, u32[]{:S(2)}) %collective-permute-start.24) | collective-permute-done | bytes 262176 | tf_op jit(solution)/shard_map/ppermute | solution.py:392
  170.9 2.1 %extract_pieces.1 = bf16[8,32,1024]{2,1,0:T(8,128)(2,1)S(1)} custom-call(s32[8,128]{1,0:T(8,128)S(1)} %get-tuple-element.42.slots, bf16[32,32,128]{2,1,0:T(8,128)(2,1)} %select_select_fusion.own, bf16[32,32,128]{2,1,0:T(8,128)(2,1)} %collective-permute-done.23.near, bf16[32,32,128]{2,1,0:T(8,128)(2,1)} %collective-permute-done.24.far), custom_call_target="tpu_custom_call" | custom-call | tf_op jit(solution)/shard_map/extract_pieces/pallas_call | solution.py:343
  173.0 0.8 copy-done.2
  173.8 14.8 %all_to_all.15 = bf16[8,32,1024]{2,1,0:T(8,128)(2,1)S(1)} all-to-all(bf16[8,32,1024]{2,1,0:T(8,128)(2,1)} %copy-done.2), channel_id=1, replica_groups=mesh['leaf'=32,'sub'=8] {'sub'}, dimensions={0} | all-to-all | bytes 1048576 | tf_op jit(solution)/shard_map/all_to_all | solution.py:457
  188.6 1.2 copy-done.3
  189.8 3.9 %leaf_backward.1 = (bf16[4,512,256]{2,1,0:T(8,128)(2,1)}, bf16[512,256]{1,0:T(8,128)(2,1)}) custom-call(bf16[4,256,512]{2,1,0:T(8,128)(2,1)S(1)} %copy-done.3, bf16[256,1024]{1,0:T(8,128)(2,1)S(1)} %bitcast.6, bf16[4,512,512]{2,1,0:T(8,128)(2,1)S(1)} %copy-done, bf16[4,256,512]{2,1,0:T(8,128)(2,1)S(1)} %copy-done.1, ...), custom_call_target="tpu_custom_call" | custom-call | tf_op jit(solution)/shard_map/leaf_backward/pallas_call | solution.py:366
  (39 shorter events, 2.7 us)
Async XLA Ops:
  0.6 39.4 %collective-permute-start.1 = (bf16[512,4096]{1,0:T(8,128)(2,1)}, bf16[512,4096]{1,0:T(8,128)(2,1)}, u32[]{:S(2)}, u32[]{:S(2)}) collective-permute-start(bf16[512,4096]{1,0:T(8,128)(2,1)} %refs_13_), channel_id=1, source_target_pairs={{6,7},{7,6},{14,15},{15,14},{22,23},{23,22},{30,31},{31,30},{38,39... | collective-permute-start | bytes 12582920 | tf_op jit(solution)/shard_map/ppermute | solution.py:400
  3.3 29.1 %collective-permute-start.3 = (bf16[512,512]{1,0:T(8,128)(2,1)}, bf16[512,512]{1,0:T(8,128)(2,1)S(1)}, u32[]{:S(2)}, u32[]{:S(2)}) collective-permute-start(bf16[512,512]{1,0:T(8,128)(2,1)} %refs_15_), channel_id=1, source_target_pairs={{0,6},{1,7},{8,14},{9,15},{16,22},{17,23},{24,30},{25,31},{32,38},... | collective-permute-start | bytes 1572872 | tf_op jit(solution)/shard_map/ppermute | solution.py:396
  7.5 25.6 %collective-permute-start.5 = (bf16[512,512]{1,0:T(8,128)(2,1)}, bf16[512,512]{1,0:T(8,128)(2,1)S(1)}, u32[]{:S(2)}, u32[]{:S(2)}) collective-permute-start(bf16[512,512]{1,0:T(8,128)(2,1)} %refs_15_), channel_id=1, source_target_pairs={{2,6},{3,7},{10,14},{11,15},{18,22},{19,23},{26,30},{27,31},{34,38... | collective-permute-start | bytes 1572872 | tf_op jit(solution)/shard_map/ppermute | solution.py:396
  8.2 25.6 %collective-permute-start.7 = (bf16[512,512]{1,0:T(8,128)(2,1)}, bf16[512,512]{1,0:T(8,128)(2,1)}, u32[]{:S(2)}, u32[]{:S(2)}) collective-permute-start(bf16[512,512]{1,0:T(8,128)(2,1)} %refs_15_), channel_id=1, source_target_pairs={{4,6},{5,7},{12,14},{13,15},{20,22},{21,23},{28,30},{29,31},{36,38... | collective-permute-start | bytes 1572872 | tf_op jit(solution)/shard_map/ppermute | solution.py:396
  10.7 3.4 %collective-permute-start = (bf16[512,256]{1,0:T(8,128)(2,1)S(1)}, bf16[512,256]{1,0:T(8,128)(2,1)S(1)}, u32[]{:S(2)}, u32[]{:S(2)}) collective-permute-start(bf16[512,256]{1,0:T(8,128)(2,1)S(1)} %constant_dynamic-slice_fusion), channel_id=1, source_target_pairs={{1,0},{3,2},{5,4},{9,8},{11,10},{13,12},{17,16},{19,18},{21,20},{2... | collective-permute-start | bytes 786440 | tf_op jit(solution)/shard_map/ppermute | solution.py:421
  12.6 13.2 %copy-start.4 = (bf16[512,512]{1,0:T(8,128)(2,1)S(1)}, bf16[512,512]{1,0:T(8,128)(2,1)}, u32[]{:S(2)}) copy-start(bf16[512,512]{1,0:T(8,128)(2,1)} %refs_15_) | copy-start | bytes 1572868
  14.1 0.7 copy-start.10
  21.7 85.2 %copy-start.8 = (s32[3]{0:T(128)S(1)}, s32[3]{0:T(128)}, u32[]{:S(2)}) copy-start(s32[3]{0:T(128)} %pad_add_fusion.where) | copy-start | bytes 40
  21.7 18.3 %all-to-all-start = ((bf16[8,32,1664]{2,1,0:T(8,128)(2,1)}), bf16[8,32,1664]{2,1,0:T(8,128)(2,1)S(1)}, u32[]{:S(2)}, u32[]{:S(2)}) async-start(bf16[8,32,1664]{2,1,0:T(8,128)(2,1)} %bitcast.7), calls=%async_computation | async-start | bytes 1703936 | tf_op jit(solution)/shard_map/all_to_all | solution.py:433
  25.8 9.5 %collective-permute-start.2 = (bf16[512,512]{1,0:T(8,128)(2,1)S(1)}, bf16[512,512]{1,0:T(8,128)(2,1)S(1)}, u32[]{:S(2)}, u32[]{:S(2)}) collective-permute-start(bf16[512,512]{1,0:T(8,128)(2,1)S(1)} %copy-done.4), channel_id=1, source_target_pairs={{6,7},{7,6},{14,15},{15,14},{22,23},{23,22},{30,31},{31,30},{38,39... | collective-permute-start | bytes 1572872 | tf_op jit(solution)/shard_map/ppermute | solution.py:400
  32.4 7.6 %collective-permute-start.4 = (bf16[512,512]{1,0:T(8,128)(2,1)S(1)}, bf16[512,512]{1,0:T(8,128)(2,1)S(1)}, u32[]{:S(2)}, u32[]{:S(2)}) collective-permute-start(bf16[512,512]{1,0:T(8,128)(2,1)S(1)} %collective-permute-done.3.refs_6_.refs_3_), channel_id=1, source_target_pairs={{6,7},{7,6},{14,15},{15,14},{22,23},{23,22},{30,31},{31,30},{38,39... | collective-permute-start | bytes 1572872 | tf_op jit(solution)/shard_map/ppermute | solution.py:400
  33.1 6.9 %collective-permute-start.6 = (bf16[512,512]{1,0:T(8,128)(2,1)S(1)}, bf16[512,512]{1,0:T(8,128)(2,1)S(1)}, u32[]{:S(2)}, u32[]{:S(2)}) collective-permute-start(bf16[512,512]{1,0:T(8,128)(2,1)S(1)} %collective-permute-done.5.refs_10_.refs_7_), channel_id=1, source_target_pairs={{6,7},{7,6},{14,15},{15,14},{22,23},{23,22},{30,31},{31,30},{38,39... | collective-permute-start | bytes 1572872 | tf_op jit(solution)/shard_map/ppermute | solution.py:400
  33.8 6.2 %collective-permute-start.8 = (bf16[512,512]{1,0:T(8,128)(2,1)}, bf16[512,512]{1,0:T(8,128)(2,1)}, u32[]{:S(2)}, u32[]{:S(2)}) collective-permute-start(bf16[512,512]{1,0:T(8,128)(2,1)} %collective-permute-done.7.refs_11_), channel_id=1, source_target_pairs={{6,7},{7,6},{14,15},{15,14},{22,23},{23,22},{30,31},{31,30},{38,39... | collective-permute-start | bytes 1572872 | tf_op jit(solution)/shard_map/ppermute | solution.py:400
  35.3 0.8 copy-start.5
  40.0 22.6 %collective-permute-start.12 = (bf16[512,1280]{1,0:T(8,128)(2,1)}, bf16[512,1280]{1,0:T(8,128)(2,1)S(1)}, u32[]{:S(2)}, u32[]{:S(2)}) collective-permute-start(bf16[512,1280]{1,0:T(8,128)(2,1)} %get-tuple-element.47), channel_id=1, source_target_pairs={{2,6},{3,7},{10,14},{11,15},{18,22},{19,23},{26,30},{27,31},{34,38... | collective-permute-start | bytes 3932168 | tf_op jit(solution)/shard_map/ppermute | solution.py:396
  40.8 56.3 %collective-permute-start.18 = (bf16[512,2304]{1,0:T(8,128)(2,1)}, bf16[512,2304]{1,0:T(8,128)(2,1)S(1)}, u32[]{:S(2)}, u32[]{:S(2)}) collective-permute-start(bf16[512,2304]{1,0:T(8,128)(2,1)} %get-tuple-element.58), channel_id=1, source_target_pairs={{4,6},{5,7},{12,14},{13,15},{20,22},{21,23},{28,30},{29,31},{36,38... | collective-permute-start | bytes 7077896 | tf_op jit(solution)/shard_map/ppermute | solution.py:396
  43.5 10.5 %collective-permute-start.9 = (bf16[32,32,128]{2,1,0:T(8,128)(2,1)S(1)}, bf16[32,32,128]{2,1,0:T(8,128)(2,1)S(1)}, u32[]{:S(2)}, u32[]{:S(2)}) collective-permute-start(bf16[32,32,128]{2,1,0:T(8,128)(2,1)S(1)} %get-tuple-element.44), channel_id=1, source_target_pairs={{8,0},{16,8},{24,16},{32,24},{40,32},{48,40},{56,48},{64,56},{72,6... | collective-permute-start | bytes 786440 | tf_op jit(solution)/shard_map/ppermute | solution.py:392
  45.6 17.1 %collective-permute-start.10 = (bf16[32,32,128]{2,1,0:T(8,128)(2,1)S(1)}, bf16[32,32,128]{2,1,0:T(8,128)(2,1)S(1)}, u32[]{:S(2)}, u32[]{:S(2)}) collective-permute-start(bf16[32,32,128]{2,1,0:T(8,128)(2,1)S(1)} %get-tuple-element.45), channel_id=1, source_target_pairs={{16,0},{24,8},{32,16},{40,24},{48,32},{56,40},{64,48},{72,56},{80,... | collective-permute-start | bytes 786440 | tf_op jit(solution)/shard_map/ppermute | solution.py:392
  62.6 26.6 %collective-permute-start.13 = (bf16[512,1280]{1,0:T(8,128)(2,1)S(1)}, bf16[512,1280]{1,0:T(8,128)(2,1)S(1)}, u32[]{:S(2)}, u32[]{:S(2)}) collective-permute-start(bf16[512,1280]{1,0:T(8,128)(2,1)S(1)} %collective-permute-done.12.refs_8_.refs_5_), channel_id=1, source_target_pairs={{6,7},{7,6},{14,15},{15,14},{22,23},{23,22},{30,31},{31,30},{38,39... | collective-permute-start | bytes 3932168 | tf_op jit(solution)/shard_map/ppermute | solution.py:400
  63.4 25.9 %collective-permute-start.11 = (bf16[512,256]{1,0:T(8,128)(2,1)}, bf16[512,256]{1,0:T(8,128)(2,1)S(1)}, u32[]{:S(2)}, u32[]{:S(2)}) collective-permute-start(bf16[512,256]{1,0:T(8,128)(2,1)} %get-tuple-element.46), channel_id=1, source_target_pairs={{0,6},{1,7},{8,14},{9,15},{16,22},{17,23},{24,30},{25,31},{32,38},... | collective-permute-start | bytes 786440 | tf_op jit(solution)/shard_map/ppermute | solution.py:396
  89.4 19.6 %copy-start.6 = (bf16[512,512]{1,0:T(8,128)(2,1)S(1)}, bf16[512,512]{1,0:T(8,128)(2,1)}, u32[]{:S(2)}) copy-start(bf16[512,512]{1,0:T(8,128)(2,1)} %copy-done.5) | copy-start | bytes 1572868
  89.4 16.7 %collective-permute-start.14 = (bf16[32,32,128]{2,1,0:T(8,128)(2,1)S(1)}, bf16[32,32,128]{2,1,0:T(8,128)(2,1)S(1)}, u32[]{:S(2)}, u32[]{:S(2)}) collective-permute-start(bf16[32,32,128]{2,1,0:T(8,128)(2,1)S(1)} %subtract_convert_fusion.refs_3_), channel_id=1, source_target_pairs={{0,6},{1,7},{8,14},{9,15},{16,22},{17,23},{24,30},{25,31},{32,38},... | collective-permute-start | bytes 786440 | tf_op jit(solution)/shard_map/ppermute | solution.py:396
  95.0 11.0 %collective-permute-start.15 = (bf16[32,32,128]{2,1,0:T(8,128)(2,1)S(1)}, bf16[32,32,128]{2,1,0:T(8,128)(2,1)S(1)}, u32[]{:S(2)}, u32[]{:S(2)}) collective-permute-start(bf16[32,32,128]{2,1,0:T(8,128)(2,1)S(1)} %subtract_convert_fusion.refs_3_), channel_id=1, source_target_pairs={{2,6},{3,7},{10,14},{11,15},{18,22},{19,23},{26,30},{27,31},{34,38... | collective-permute-start | bytes 786440 | tf_op jit(solution)/shard_map/ppermute | solution.py:396
  95.7 10.3 %collective-permute-start.16 = (bf16[32,32,128]{2,1,0:T(8,128)(2,1)S(1)}, bf16[32,32,128]{2,1,0:T(8,128)(2,1)S(1)}, u32[]{:S(2)}, u32[]{:S(2)}) collective-permute-start(bf16[32,32,128]{2,1,0:T(8,128)(2,1)S(1)} %subtract_convert_fusion.refs_3_), channel_id=1, source_target_pairs={{4,6},{5,7},{12,14},{13,15},{20,22},{21,23},{28,30},{29,31},{36,38... | collective-permute-start | bytes 786440 | tf_op jit(solution)/shard_map/ppermute | solution.py:396
  96.4 9.7 %collective-permute-start.17 = (bf16[512,256]{1,0:T(8,128)(2,1)S(1)}, bf16[512,256]{1,0:T(8,128)(2,1)S(1)}, u32[]{:S(2)}, u32[]{:S(2)}) collective-permute-start(bf16[512,256]{1,0:T(8,128)(2,1)S(1)} %collective-permute-done.11.refs_4_.refs_1_), channel_id=1, source_target_pairs={{6,7},{7,6},{14,15},{15,14},{22,23},{23,22},{30,31},{31,30},{38,39... | collective-permute-start | bytes 786440 | tf_op jit(solution)/shard_map/ppermute | solution.py:400
  106.1 1.5 collective-permute-start.19
  107.6 1.4 copy-start.9
  110.5 0.7 copy-start.7
  111.2 77.4 %copy-start = (bf16[4,512,512]{2,1,0:T(8,128)(2,1)S(1)}, bf16[4,512,512]{2,1,0:T(8,128)(2,1)}, u32[]{:S(2)}) copy-start(bf16[4,512,512]{2,1,0:T(8,128)(2,1)} %inverse.3) | copy-start | bytes 6291460
  111.2 77.4 %copy-start.1 = (bf16[4,256,512]{2,1,0:T(8,128)(2,1)S(1)}, bf16[4,256,512]{2,1,0:T(8,128)(2,1)}, u32[]{:S(2)}) copy-start(bf16[4,256,512]{2,1,0:T(8,128)(2,1)} %panel.3) | copy-start | bytes 3145732
  111.2 3.6 %collective-permute-start.20 = (bf16[32,32,128]{2,1,0:T(8,128)(2,1)}, bf16[32,32,128]{2,1,0:T(8,128)(2,1)S(1)}, u32[]{:S(2)}, u32[]{:S(2)}) collective-permute-start(bf16[32,32,128]{2,1,0:T(8,128)(2,1)} %get-tuple-element.67), channel_id=1, source_target_pairs={{6,4},{7,5},{14,12},{15,13},{22,20},{23,21},{30,28},{31,29},{38,36... | collective-permute-start | bytes 786440 | tf_op jit(solution)/shard_map/ppermute | solution.py:396
  112.0 2.8 %collective-permute-start.21 = (bf16[32,32,128]{2,1,0:T(8,128)(2,1)}, bf16[32,32,128]{2,1,0:T(8,128)(2,1)}, u32[]{:S(2)}, u32[]{:S(2)}) collective-permute-start(bf16[32,32,128]{2,1,0:T(8,128)(2,1)} %get-tuple-element.68), channel_id=1, source_target_pairs={{6,2},{7,3},{14,10},{15,11},{22,18},{23,19},{30,26},{31,27},{38,34... | collective-permute-start | bytes 786440 | tf_op jit(solution)/shard_map/ppermute | solution.py:396
  113.5 30.4 %collective-permute-start.22 = (bf16[32,32,128]{2,1,0:T(8,128)(2,1)}, bf16[32,32,128]{2,1,0:T(8,128)(2,1)}, u32[]{:S(2)}, u32[]{:S(2)}) collective-permute-start(bf16[32,32,128]{2,1,0:T(8,128)(2,1)} %get-tuple-element.69), channel_id=1, source_target_pairs={{6,0},{7,1},{14,8},{15,9},{22,16},{23,17},{30,24},{31,25},{38,32},... | collective-permute-start | bytes 786440 | tf_op jit(solution)/shard_map/ppermute | solution.py:396
  145.7 15.3 %collective-permute-start.23 = (bf16[32,32,128]{2,1,0:T(8,128)(2,1)}, bf16[32,32,128]{2,1,0:T(8,128)(2,1)}, u32[]{:S(2)}, u32[]{:S(2)}) collective-permute-start(bf16[32,32,128]{2,1,0:T(8,128)(2,1)} %select_select_fusion.own), channel_id=1, source_target_pairs={{0,8},{8,16},{16,24},{24,32},{32,40},{40,48},{48,56},{56,64},{64,7... | collective-permute-start | bytes 786440 | tf_op jit(solution)/shard_map/ppermute | solution.py:392
  149.5 21.4 %collective-permute-start.24 = (bf16[32,32,128]{2,1,0:T(8,128)(2,1)}, bf16[32,32,128]{2,1,0:T(8,128)(2,1)}, u32[]{:S(2)}, u32[]{:S(2)}) collective-permute-start(bf16[32,32,128]{2,1,0:T(8,128)(2,1)} %select_select_fusion.own), channel_id=1, source_target_pairs={{0,16},{8,24},{16,32},{24,40},{32,48},{40,56},{48,64},{56,72},{64,... | collective-permute-start | bytes 786440 | tf_op jit(solution)/shard_map/ppermute | solution.py:392
  155.9 17.9 %all-to-all-start.2 = ((bf16[8,4,32,128]{3,2,1,0:T(8,128)(2,1)}), bf16[8,4,32,128]{3,2,1,0:T(8,128)(2,1)S(1)}, u32[]{:S(2)}, u32[]{:S(2)}) async-start(bf16[8,4,32,128]{3,2,1,0:T(8,128)(2,1)} %bitcast.5), calls=%async_computation.2 | async-start | bytes 524288 | tf_op jit(solution)/shard_map/all_to_all | solution.py:456
  173.0 0.8 copy-start.2
  188.6 1.2 copy-start.3

commit v4 on v3

--- a/solution.py
+++ b/solution.py
@@ -277,7 +277,9 @@
 def by_inverse(bracket, block, dims):
     head = bracket.astype(bf16)
     tail = (bracket - head.astype(f32)).astype(bf16)
-    return (dot(head, block, dims) + dot(tail, block, dims)).astype(bf16)
+    both = dot(jnp.concatenate([head, tail], axis=0), block, dims)
+    rows = bracket.shape[0]
+    return (both[:rows] + both[rows:]).astype(bf16)
 
 
 def sweep_head(where, *blocks):
@@ -381,7 +383,7 @@
             jax.ShapeDtypeStruct((SN_DEV, W, R), bf16),
             jax.ShapeDtypeStruct((WSN, R), bf16),
         ],
-        compiler_params=pltpu.CompilerParams(dimension_semantics=("arbitrary",), vmem_limit_bytes=24 * MIB),
+        compiler_params=pltpu.CompilerParams(dimension_semantics=("arbitrary",), vmem_limit_bytes=WHOLE),
         name="leaf_backward",
     )(y, pieces, inverse, panels, rows)
 

time: 195 us -> 192 us (0.985)
  local copies, waits for them, and re-layouts: 6.62 us -> 3.94 us
  waiting for transfers between devices: 75.1 us -> 72.9 us
    unnamed x22 -> x14, local copies, waits for them, and re-layouts: 5.65 us -> 2.97 us
    pallas_call x1, Pallas kernels: 3.86 us -> 5.98 us  [leaf_backward(): pl.pallas_call(leaf_backward_kernel, grid=(SN_DEV,), in_specs=[pl.BlockSp...]
  transfers between devices with their start and end apart: 27 -> 27, of which waited for: 9 -> 8; matrix products, arithmetic and copies ran while one was open for 1% -> 1% of each run, Pallas kernels for 6% -> 6%
where the time goes in v4:
time: 192 us; the launch traced here: 191 us
  starting transfers between devices  76.7 us (40%)
  waiting for transfers between devices  72.9 us (38%)
  Pallas kernels  18.7 us (10%)
  blocking collectives  15.6 us (8%)
  local copies, waits for them, and re-layouts  3.94 us (2%)
    ppermute x12, waiting for transfers between devices, hop(): lax.ppermute(block, 'sub', [(2 * a + c, 2 * b + c) for a, b in chips for...  49.5 us
    ppermute x12, starting transfers between devices, hop(): lax.ppermute(block, 'sub', [(2 * a + c, 2 * b + c) for a, b in chips for...  37 us
    ppermute x4, starting transfers between devices, along_leaf(): return lax.ppermute(block, 'leaf', route)  20.7 us
    ppermute x4, waiting for transfers between devices, along_leaf(): return lax.ppermute(block, 'leaf', route)  18.1 us
    all_to_all x1, blocking collectives, shards(): pieces = lax.all_to_all(pieces, 'sub', 0, 0, tiled=True).reshape(R, UPD)  15.6 us
    ppermute x8, starting transfers between devices, swap(): lax.ppermute(block, 'sub', [(2 * HUB + c, 2 * HUB + 1 - c) for c in cores])  8.39 us
    pallas_call x1, Pallas kernels, leaf_forward(): pl.pallas_call(leaf_forward_kernel, grid=(SN_DEV,), in_specs=[pl.BlockSpe...  6.91 us
    pallas_call x1, Pallas kernels, leaf_backward(): pl.pallas_call(leaf_backward_kernel, grid=(SN_DEV,), in_specs=[pl.BlockSp...  5.98 us
  transfers between devices with their start and end apart: 27, of which 8 were waited for; matrix products, arithmetic and copies ran while one was open for 1% of the time, Pallas kernels for 6%

profile of v4, /device:TPU:38, one launch (start us, length us, event | category | flops | bytes accessed | tf_op | source)
XLA Modules:
  0.0 190.5 jit_solution(16914227667893092361)
XLA Ops:
  0.6 2.6 %collective-permute-start.1 = (bf16[512,4096]{1,0:T(8,128)(2,1)}, bf16[512,4096]{1,0:T(8,128)(2,1)}, u32[]{:S(2)}, u32[]{:S(2)}) collective-permute-start(bf16[512,4096]{1,0:T(8,128)(2,1)} %refs_13_), channel_id=1, source_target_pairs={{6,7},{7,6},{14,15},{15,14},{22,23},{23,22},{30,31},{31,30},{38,39... | collective-permute-start | bytes 12582920 | tf_op jit(solution)/shard_map/ppermute | solution.py:402
  3.3 4.2 %collective-permute-start.3 = (bf16[512,512]{1,0:T(8,128)(2,1)}, bf16[512,512]{1,0:T(8,128)(2,1)S(1)}, u32[]{:S(2)}, u32[]{:S(2)}) collective-permute-start(bf16[512,512]{1,0:T(8,128)(2,1)} %refs_15_), channel_id=1, source_target_pairs={{0,6},{1,7},{8,14},{9,15},{16,22},{17,23},{24,30},{25,31},{32,38},... | collective-permute-start | bytes 1572872 | tf_op jit(solution)/shard_map/ppermute | solution.py:398
  7.5 0.7 collective-permute-start.5
  8.2 1.5 collective-permute-start.7
  9.7 1.0 constant_dynamic-slice_fusion
  10.7 1.3 collective-permute-start
  12.0 0.7 pad_add_fusion.where
  12.6 1.4 collective-permute-done.half
  14.1 0.7 copy-done.6
  14.8 6.9 %leaf_forward.1 = (bf16[4,256,512]{2,1,0:T(8,128)(2,1)}, bf16[256,1664]{1,0:T(8,128)(2,1)}, bf16[512,2304]{1,0:T(8,128)(2,1)}, bf16[512,1280]{1,0:T(8,128)(2,1)}, bf16[512,256]{1,0:T(8,128)(2,1)}) custom-call(s32[3]{0:T(128)} %pad_add_fusion.where, s32[4]{0:T(128)} %subtree.1, s32[4,4]{1,0:T(4,128)} %block.1, bf16[4,512,256]{2,1,0:T(8,128)(2,1)} %right.1, ...), custom_call_target="tpu_custom_call" | custom-call | tf_op jit(solution)/shard_map/leaf_forward/pallas_call | solution.py:94
  21.7 4.0 %all-to-all-start = ((bf16[8,32,1664]{2,1,0:T(8,128)(2,1)}), bf16[8,32,1664]{2,1,0:T(8,128)(2,1)S(1)}, u32[]{:S(2)}, u32[]{:S(2)}) async-start(bf16[8,32,1664]{2,1,0:T(8,128)(2,1)} %bitcast.7), calls=%async_computation | async-start | bytes 1703936 | tf_op jit(solution)/shard_map/all_to_all | solution.py:435
  25.8 0.7 collective-permute-start.2
  26.5 5.9 %collective-permute-done.3.refs_6_.refs_3_ = bf16[512,512]{1,0:T(8,128)(2,1)S(1)} collective-permute-done((bf16[512,512]{1,0:T(8,128)(2,1)}, bf16[512,512]{1,0:T(8,128)(2,1)S(1)}, u32[]{:S(2)}, u32[]{:S(2)}) %collective-permute-start.3) | collective-permute-done | bytes 524320 | tf_op jit(solution)/shard_map/ppermute | solution.py:398
  32.4 0.7 collective-permute-start.4
  33.1 0.7 collective-permute-start.6
  33.8 1.5 collective-permute-start.8
  35.3 0.8 copy-done.1
  36.1 3.9 %all-to-all-done.received = bf16[8,32,1664]{2,1,0:T(8,128)(2,1)S(1)} async-done(((bf16[8,32,1664]{2,1,0:T(8,128)(2,1)}), bf16[8,32,1664]{2,1,0:T(8,128)(2,1)S(1)}, u32[]{:S(2)}, u32[]{:S(2)}) %all-to-all-start) | async-done | bytes 852000 | tf_op jit(solution)/shard_map/all_to_all | solution.py:435
  40.0 0.7 collective-permute-start.12
  40.8 0.8 collective-permute-start.18
  41.6 1.9 %scatter_updates.1 = (f32[32,32,128]{2,1,0:T(8,128)S(1)}, bf16[32,32,128]{2,1,0:T(8,128)(2,1)S(1)}, bf16[32,32,128]{2,1,0:T(8,128)(2,1)S(1)}, s32[8,128]{1,0:T(8,128)S(1)}) custom-call(bf16[8,32,1664]{2,1,0:T(8,128)(2,1)S(1)} %all-to-all-done.received), custom_call_target="tpu_custom_call" | custom-call | tf_op jit(solution)/shard_map/scatter_updates/pallas_call | solution.py:154
  43.5 2.0 %collective-permute-start.9 = (bf16[32,32,128]{2,1,0:T(8,128)(2,1)S(1)}, bf16[32,32,128]{2,1,0:T(8,128)(2,1)S(1)}, u32[]{:S(2)}, u32[]{:S(2)}) collective-permute-start(bf16[32,32,128]{2,1,0:T(8,128)(2,1)S(1)} %get-tuple-element.44), channel_id=1, source_target_pairs={{8,0},{16,8},{24,16},{32,24},{40,32},{48,40},{56,48},{64,56},{72,6... | collective-permute-start | bytes 786440 | tf_op jit(solution)/shard_map/ppermute | solution.py:394
  45.6 8.5 %collective-permute-start.10 = (bf16[32,32,128]{2,1,0:T(8,128)(2,1)S(1)}, bf16[32,32,128]{2,1,0:T(8,128)(2,1)S(1)}, u32[]{:S(2)}, u32[]{:S(2)}) collective-permute-start(bf16[32,32,128]{2,1,0:T(8,128)(2,1)S(1)} %get-tuple-element.45), channel_id=1, source_target_pairs={{16,0},{24,8},{32,16},{40,24},{48,32},{56,40},{64,48},{72,56},{80,... | collective-permute-start | bytes 786440 | tf_op jit(solution)/shard_map/ppermute | solution.py:394
  54.1 8.6 %collective-permute-done.10 = bf16[32,32,128]{2,1,0:T(8,128)(2,1)S(1)} collective-permute-done((bf16[32,32,128]{2,1,0:T(8,128)(2,1)S(1)}, bf16[32,32,128]{2,1,0:T(8,128)(2,1)S(1)}, u32[]{:S(2)}, u32[]{:S(2)}) %collective-permute-start.10) | collective-permute-done | bytes 262176 | tf_op jit(solution)/shard_map/ppermute | solution.py:394
  62.7 0.7 collective-permute-start.13
  63.4 19.4 %collective-permute-start.11 = (bf16[512,256]{1,0:T(8,128)(2,1)}, bf16[512,256]{1,0:T(8,128)(2,1)S(1)}, u32[]{:S(2)}, u32[]{:S(2)}) collective-permute-start(bf16[512,256]{1,0:T(8,128)(2,1)} %get-tuple-element.46), channel_id=1, source_target_pairs={{0,6},{1,7},{8,14},{9,15},{16,22},{17,23},{24,30},{25,31},{32,38},... | collective-permute-start | bytes 786440 | tf_op jit(solution)/shard_map/ppermute | solution.py:398
  82.8 6.5 %collective-permute-done.11.refs_4_.refs_1_ = bf16[512,256]{1,0:T(8,128)(2,1)S(1)} collective-permute-done((bf16[512,256]{1,0:T(8,128)(2,1)}, bf16[512,256]{1,0:T(8,128)(2,1)S(1)}, u32[]{:S(2)}, u32[]{:S(2)}) %collective-permute-start.11) | collective-permute-done | bytes 262176 | tf_op jit(solution)/shard_map/ppermute | solution.py:398
  89.4 5.6 %collective-permute-start.14 = (bf16[32,32,128]{2,1,0:T(8,128)(2,1)S(1)}, bf16[32,32,128]{2,1,0:T(8,128)(2,1)S(1)}, u32[]{:S(2)}, u32[]{:S(2)}) collective-permute-start(bf16[32,32,128]{2,1,0:T(8,128)(2,1)S(1)} %subtract_convert_fusion.refs_3_), channel_id=1, source_target_pairs={{0,6},{1,7},{8,14},{9,15},{16,22},{17,23},{24,30},{25,31},{32,38},... | collective-permute-start | bytes 786440 | tf_op jit(solution)/shard_map/ppermute | solution.py:398
  95.0 0.7 collective-permute-start.15
  95.7 0.7 collective-permute-start.16
  96.4 0.7 collective-permute-start.17
  97.1 9.0 %collective-permute-done.14.refs_0_ = bf16[32,32,128]{2,1,0:T(8,128)(2,1)S(1)} collective-permute-done((bf16[32,32,128]{2,1,0:T(8,128)(2,1)S(1)}, bf16[32,32,128]{2,1,0:T(8,128)(2,1)S(1)}, u32[]{:S(2)}, u32[]{:S(2)}) %collective-permute-start.14) | collective-permute-done | bytes 262176 | tf_op jit(solution)/shard_map/ppermute | solution.py:398
  106.1 0.8 collective-permute-start.19
  106.9 0.6 sweep_head.1.refs_0_
  107.6 1.4 copy-done.4
  109.0 1.4 sweep_rest.1
  110.4 0.7 collective-permute-start.20
  111.1 0.7 collective-permute-start.21
  111.7 1.3 collective-permute-start.22
  113.1 28.1 %collective-permute-done.22 = bf16[32,32,128]{2,1,0:T(8,128)(2,1)S(1)} collective-permute-done((bf16[32,32,128]{2,1,0:T(8,128)(2,1)S(1)}, bf16[32,32,128]{2,1,0:T(8,128)(2,1)S(1)}, u32[]{:S(2)}, u32[]{:S(2)}) %collective-permute-start.22) | collective-permute-done | bytes 262176 | tf_op jit(solution)/shard_map/ppermute | solution.py:398
  141.1 0.8 select_select_fusion.own
  141.9 3.8 %collective-permute-start.23 = (bf16[32,32,128]{2,1,0:T(8,128)(2,1)}, bf16[32,32,128]{2,1,0:T(8,128)(2,1)S(1)}, u32[]{:S(2)}, u32[]{:S(2)}) collective-permute-start(bf16[32,32,128]{2,1,0:T(8,128)(2,1)} %select_select_fusion.own), channel_id=1, source_target_pairs={{0,8},{8,16},{16,24},{24,32},{32,40},{40,48},{48,56},{56,64},{64,7... | collective-permute-start | bytes 786440 | tf_op jit(solution)/shard_map/ppermute | solution.py:394
  145.7 6.4 %collective-permute-start.24 = (bf16[32,32,128]{2,1,0:T(8,128)(2,1)}, bf16[32,32,128]{2,1,0:T(8,128)(2,1)S(1)}, u32[]{:S(2)}, u32[]{:S(2)}) collective-permute-start(bf16[32,32,128]{2,1,0:T(8,128)(2,1)} %select_select_fusion.own), channel_id=1, source_target_pairs={{0,16},{8,24},{16,32},{24,40},{32,48},{40,56},{48,64},{56,72},{64,... | collective-permute-start | bytes 786440 | tf_op jit(solution)/shard_map/ppermute | solution.py:394
  152.1 5.4 %all-to-all-start.2 = ((bf16[8,4,32,128]{3,2,1,0:T(8,128)(2,1)}), bf16[8,4,32,128]{3,2,1,0:T(8,128)(2,1)S(1)}, u32[]{:S(2)}, u32[]{:S(2)}) async-start(bf16[8,4,32,128]{3,2,1,0:T(8,128)(2,1)} %bitcast.5), calls=%async_computation.2 | async-start | bytes 524288 | tf_op jit(solution)/shard_map/all_to_all | solution.py:458
  157.5 9.5 %collective-permute-done.24.far = bf16[32,32,128]{2,1,0:T(8,128)(2,1)S(1)} collective-permute-done((bf16[32,32,128]{2,1,0:T(8,128)(2,1)}, bf16[32,32,128]{2,1,0:T(8,128)(2,1)S(1)}, u32[]{:S(2)}, u32[]{:S(2)}) %collective-permute-start.24) | collective-permute-done | bytes 262176 | tf_op jit(solution)/shard_map/ppermute | solution.py:394
  167.0 1.9 %extract_pieces.1 = bf16[8,32,1024]{2,1,0:T(8,128)(2,1)S(1)} custom-call(s32[8,128]{1,0:T(8,128)S(1)} %get-tuple-element.42.slots, bf16[32,32,128]{2,1,0:T(8,128)(2,1)} %select_select_fusion.own, bf16[32,32,128]{2,1,0:T(8,128)(2,1)S(1)} %collective-permute-done.23.near, bf16[32,32,128]{2,1,0:T(8,128)(2,1)S(1)} %collective-permute-done.24.far), custom_call_target="tpu_custom_call" | custom-call | tf_op jit(solution)/shard_map/extract_pieces/pallas_call | solution.py:345
  168.9 15.6 %all_to_all.15 = bf16[8,32,1024]{2,1,0:T(8,128)(2,1)} all-to-all(bf16[8,32,1024]{2,1,0:T(8,128)(2,1)S(1)} %extract_pieces.1), channel_id=1, replica_groups=mesh['leaf'=32,'sub'=8] {'sub'}, dimensions={0} | all-to-all | bytes 1048576 | tf_op jit(solution)/shard_map/all_to_all | solution.py:459
  184.6 6.0 %leaf_backward.1 = (bf16[4,512,256]{2,1,0:T(8,128)(2,1)}, bf16[512,256]{1,0:T(8,128)(2,1)}) custom-call(bf16[4,256,512]{2,1,0:T(8,128)(2,1)} %get-tuple-element.36.y, bf16[256,1024]{1,0:T(8,128)(2,1)} %bitcast.6, bf16[4,512,512]{2,1,0:T(8,128)(2,1)} %inverse.3, bf16[4,256,512]{2,1,0:T(8,128)(2,1)} %panel.3, bf16[8,4,32,128]{3,2,1,0:T(8,128)(2,1)} %copy-done.5), custom_call_target="tpu_custom_call" | custom-call | tf_op jit(solution)/shard_map/leaf_backward/pallas_call | solution.py:368
  (31 shorter events, 0.2 us)
Async XLA Ops:
  0.6 39.4 %collective-permute-start.1 = (bf16[512,4096]{1,0:T(8,128)(2,1)}, bf16[512,4096]{1,0:T(8,128)(2,1)}, u32[]{:S(2)}, u32[]{:S(2)}) collective-permute-start(bf16[512,4096]{1,0:T(8,128)(2,1)} %refs_13_), channel_id=1, source_target_pairs={{6,7},{7,6},{14,15},{15,14},{22,23},{23,22},{30,31},{31,30},{38,39... | collective-permute-start | bytes 12582920 | tf_op jit(solution)/shard_map/ppermute | solution.py:402
  3.3 29.1 %collective-permute-start.3 = (bf16[512,512]{1,0:T(8,128)(2,1)}, bf16[512,512]{1,0:T(8,128)(2,1)S(1)}, u32[]{:S(2)}, u32[]{:S(2)}) collective-permute-start(bf16[512,512]{1,0:T(8,128)(2,1)} %refs_15_), channel_id=1, source_target_pairs={{0,6},{1,7},{8,14},{9,15},{16,22},{17,23},{24,30},{25,31},{32,38},... | collective-permute-start | bytes 1572872 | tf_op jit(solution)/shard_map/ppermute | solution.py:398
  7.5 25.6 %collective-permute-start.5 = (bf16[512,512]{1,0:T(8,128)(2,1)}, bf16[512,512]{1,0:T(8,128)(2,1)S(1)}, u32[]{:S(2)}, u32[]{:S(2)}) collective-permute-start(bf16[512,512]{1,0:T(8,128)(2,1)} %refs_15_), channel_id=1, source_target_pairs={{2,6},{3,7},{10,14},{11,15},{18,22},{19,23},{26,30},{27,31},{34,38... | collective-permute-start | bytes 1572872 | tf_op jit(solution)/shard_map/ppermute | solution.py:398
  8.2 25.6 %collective-permute-start.7 = (bf16[512,512]{1,0:T(8,128)(2,1)}, bf16[512,512]{1,0:T(8,128)(2,1)}, u32[]{:S(2)}, u32[]{:S(2)}) collective-permute-start(bf16[512,512]{1,0:T(8,128)(2,1)} %refs_15_), channel_id=1, source_target_pairs={{4,6},{5,7},{12,14},{13,15},{20,22},{21,23},{28,30},{29,31},{36,38... | collective-permute-start | bytes 1572872 | tf_op jit(solution)/shard_map/ppermute | solution.py:398
  10.7 3.4 %collective-permute-start = (bf16[512,256]{1,0:T(8,128)(2,1)S(1)}, bf16[512,256]{1,0:T(8,128)(2,1)S(1)}, u32[]{:S(2)}, u32[]{:S(2)}) collective-permute-start(bf16[512,256]{1,0:T(8,128)(2,1)S(1)} %constant_dynamic-slice_fusion), channel_id=1, source_target_pairs={{1,0},{3,2},{5,4},{9,8},{11,10},{13,12},{17,16},{19,18},{21,20},{2... | collective-permute-start | bytes 786440 | tf_op jit(solution)/shard_map/ppermute | solution.py:423
  12.6 13.1 %copy-start = (bf16[512,512]{1,0:T(8,128)(2,1)S(1)}, bf16[512,512]{1,0:T(8,128)(2,1)}, u32[]{:S(2)}) copy-start(bf16[512,512]{1,0:T(8,128)(2,1)} %refs_15_) | copy-start | bytes 1572868
  14.1 0.7 copy-start.6
  21.7 85.2 %copy-start.3 = (s32[3]{0:T(128)S(1)}, s32[3]{0:T(128)}, u32[]{:S(2)}) copy-start(s32[3]{0:T(128)} %pad_add_fusion.where) | copy-start | bytes 40
  21.7 18.3 %all-to-all-start = ((bf16[8,32,1664]{2,1,0:T(8,128)(2,1)}), bf16[8,32,1664]{2,1,0:T(8,128)(2,1)S(1)}, u32[]{:S(2)}, u32[]{:S(2)}) async-start(bf16[8,32,1664]{2,1,0:T(8,128)(2,1)} %bitcast.7), calls=%async_computation | async-start | bytes 1703936 | tf_op jit(solution)/shard_map/all_to_all | solution.py:435
  25.8 9.5 %collective-permute-start.2 = (bf16[512,512]{1,0:T(8,128)(2,1)S(1)}, bf16[512,512]{1,0:T(8,128)(2,1)S(1)}, u32[]{:S(2)}, u32[]{:S(2)}) collective-permute-start(bf16[512,512]{1,0:T(8,128)(2,1)S(1)} %copy-done), channel_id=1, source_target_pairs={{6,7},{7,6},{14,15},{15,14},{22,23},{23,22},{30,31},{31,30},{38,39... | collective-permute-start | bytes 1572872 | tf_op jit(solution)/shard_map/ppermute | solution.py:402
  32.4 7.6 %collective-permute-start.4 = (bf16[512,512]{1,0:T(8,128)(2,1)S(1)}, bf16[512,512]{1,0:T(8,128)(2,1)S(1)}, u32[]{:S(2)}, u32[]{:S(2)}) collective-permute-start(bf16[512,512]{1,0:T(8,128)(2,1)S(1)} %collective-permute-done.3.refs_6_.refs_3_), channel_id=1, source_target_pairs={{6,7},{7,6},{14,15},{15,14},{22,23},{23,22},{30,31},{31,30},{38,39... | collective-permute-start | bytes 1572872 | tf_op jit(solution)/shard_map/ppermute | solution.py:402
  33.1 6.9 %collective-permute-start.6 = (bf16[512,512]{1,0:T(8,128)(2,1)S(1)}, bf16[512,512]{1,0:T(8,128)(2,1)S(1)}, u32[]{:S(2)}, u32[]{:S(2)}) collective-permute-start(bf16[512,512]{1,0:T(8,128)(2,1)S(1)} %collective-permute-done.5.refs_10_.refs_7_), channel_id=1, source_target_pairs={{6,7},{7,6},{14,15},{15,14},{22,23},{23,22},{30,31},{31,30},{38,39... | collective-permute-start | bytes 1572872 | tf_op jit(solution)/shard_map/ppermute | solution.py:402
  33.8 6.2 %collective-permute-start.8 = (bf16[512,512]{1,0:T(8,128)(2,1)}, bf16[512,512]{1,0:T(8,128)(2,1)}, u32[]{:S(2)}, u32[]{:S(2)}) collective-permute-start(bf16[512,512]{1,0:T(8,128)(2,1)} %collective-permute-done.7.refs_11_), channel_id=1, source_target_pairs={{6,7},{7,6},{14,15},{15,14},{22,23},{23,22},{30,31},{31,30},{38,39... | collective-permute-start | bytes 1572872 | tf_op jit(solution)/shard_map/ppermute | solution.py:402
  35.3 0.8 copy-start.1
  40.0 22.6 %collective-permute-start.12 = (bf16[512,1280]{1,0:T(8,128)(2,1)}, bf16[512,1280]{1,0:T(8,128)(2,1)S(1)}, u32[]{:S(2)}, u32[]{:S(2)}) collective-permute-start(bf16[512,1280]{1,0:T(8,128)(2,1)} %get-tuple-element.47), channel_id=1, source_target_pairs={{2,6},{3,7},{10,14},{11,15},{18,22},{19,23},{26,30},{27,31},{34,38... | collective-permute-start | bytes 3932168 | tf_op jit(solution)/shard_map/ppermute | solution.py:398
  40.8 56.3 %collective-permute-start.18 = (bf16[512,2304]{1,0:T(8,128)(2,1)}, bf16[512,2304]{1,0:T(8,128)(2,1)S(1)}, u32[]{:S(2)}, u32[]{:S(2)}) collective-permute-start(bf16[512,2304]{1,0:T(8,128)(2,1)} %get-tuple-element.58), channel_id=1, source_target_pairs={{4,6},{5,7},{12,14},{13,15},{20,22},{21,23},{28,30},{29,31},{36,38... | collective-permute-start | bytes 7077896 | tf_op jit(solution)/shard_map/ppermute | solution.py:398
  43.5 10.5 %collective-permute-start.9 = (bf16[32,32,128]{2,1,0:T(8,128)(2,1)S(1)}, bf16[32,32,128]{2,1,0:T(8,128)(2,1)S(1)}, u32[]{:S(2)}, u32[]{:S(2)}) collective-permute-start(bf16[32,32,128]{2,1,0:T(8,128)(2,1)S(1)} %get-tuple-element.44), channel_id=1, source_target_pairs={{8,0},{16,8},{24,16},{32,24},{40,32},{48,40},{56,48},{64,56},{72,6... | collective-permute-start | bytes 786440 | tf_op jit(solution)/shard_map/ppermute | solution.py:394
  45.6 17.1 %collective-permute-start.10 = (bf16[32,32,128]{2,1,0:T(8,128)(2,1)S(1)}, bf16[32,32,128]{2,1,0:T(8,128)(2,1)S(1)}, u32[]{:S(2)}, u32[]{:S(2)}) collective-permute-start(bf16[32,32,128]{2,1,0:T(8,128)(2,1)S(1)} %get-tuple-element.45), channel_id=1, source_target_pairs={{16,0},{24,8},{32,16},{40,24},{48,32},{56,40},{64,48},{72,56},{80,... | collective-permute-start | bytes 786440 | tf_op jit(solution)/shard_map/ppermute | solution.py:394
  62.7 26.6 %collective-permute-start.13 = (bf16[512,1280]{1,0:T(8,128)(2,1)S(1)}, bf16[512,1280]{1,0:T(8,128)(2,1)S(1)}, u32[]{:S(2)}, u32[]{:S(2)}) collective-permute-start(bf16[512,1280]{1,0:T(8,128)(2,1)S(1)} %collective-permute-done.12.refs_8_.refs_5_), channel_id=1, source_target_pairs={{6,7},{7,6},{14,15},{15,14},{22,23},{23,22},{30,31},{31,30},{38,39... | collective-permute-start | bytes 3932168 | tf_op jit(solution)/shard_map/ppermute | solution.py:402
  63.4 25.9 %collective-permute-start.11 = (bf16[512,256]{1,0:T(8,128)(2,1)}, bf16[512,256]{1,0:T(8,128)(2,1)S(1)}, u32[]{:S(2)}, u32[]{:S(2)}) collective-permute-start(bf16[512,256]{1,0:T(8,128)(2,1)} %get-tuple-element.46), channel_id=1, source_target_pairs={{0,6},{1,7},{8,14},{9,15},{16,22},{17,23},{24,30},{25,31},{32,38},... | collective-permute-start | bytes 786440 | tf_op jit(solution)/shard_map/ppermute | solution.py:398
  89.4 19.6 %copy-start.2 = (bf16[512,512]{1,0:T(8,128)(2,1)S(1)}, bf16[512,512]{1,0:T(8,128)(2,1)}, u32[]{:S(2)}) copy-start(bf16[512,512]{1,0:T(8,128)(2,1)} %copy-done.1) | copy-start | bytes 1572868
  89.4 16.7 %collective-permute-start.14 = (bf16[32,32,128]{2,1,0:T(8,128)(2,1)S(1)}, bf16[32,32,128]{2,1,0:T(8,128)(2,1)S(1)}, u32[]{:S(2)}, u32[]{:S(2)}) collective-permute-start(bf16[32,32,128]{2,1,0:T(8,128)(2,1)S(1)} %subtract_convert_fusion.refs_3_), channel_id=1, source_target_pairs={{0,6},{1,7},{8,14},{9,15},{16,22},{17,23},{24,30},{25,31},{32,38},... | collective-permute-start | bytes 786440 | tf_op jit(solution)/shard_map/ppermute | solution.py:398
  95.0 11.0 %collective-permute-start.15 = (bf16[32,32,128]{2,1,0:T(8,128)(2,1)S(1)}, bf16[32,32,128]{2,1,0:T(8,128)(2,1)S(1)}, u32[]{:S(2)}, u32[]{:S(2)}) collective-permute-start(bf16[32,32,128]{2,1,0:T(8,128)(2,1)S(1)} %subtract_convert_fusion.refs_3_), channel_id=1, source_target_pairs={{2,6},{3,7},{10,14},{11,15},{18,22},{19,23},{26,30},{27,31},{34,38... | collective-permute-start | bytes 786440 | tf_op jit(solution)/shard_map/ppermute | solution.py:398
  95.7 10.3 %collective-permute-start.16 = (bf16[32,32,128]{2,1,0:T(8,128)(2,1)S(1)}, bf16[32,32,128]{2,1,0:T(8,128)(2,1)S(1)}, u32[]{:S(2)}, u32[]{:S(2)}) collective-permute-start(bf16[32,32,128]{2,1,0:T(8,128)(2,1)S(1)} %subtract_convert_fusion.refs_3_), channel_id=1, source_target_pairs={{4,6},{5,7},{12,14},{13,15},{20,22},{21,23},{28,30},{29,31},{36,38... | collective-permute-start | bytes 786440 | tf_op jit(solution)/shard_map/ppermute | solution.py:398
  96.4 9.7 %collective-permute-start.17 = (bf16[512,256]{1,0:T(8,128)(2,1)S(1)}, bf16[512,256]{1,0:T(8,128)(2,1)S(1)}, u32[]{:S(2)}, u32[]{:S(2)}) collective-permute-start(bf16[512,256]{1,0:T(8,128)(2,1)S(1)} %collective-permute-done.11.refs_4_.refs_1_), channel_id=1, source_target_pairs={{6,7},{7,6},{14,15},{15,14},{22,23},{23,22},{30,31},{31,30},{38,39... | collective-permute-start | bytes 786440 | tf_op jit(solution)/shard_map/ppermute | solution.py:402
  106.1 1.5 collective-permute-start.19
  107.6 1.4 copy-start.4
  110.4 2.7 %collective-permute-start.20 = (bf16[32,32,128]{2,1,0:T(8,128)(2,1)}, bf16[32,32,128]{2,1,0:T(8,128)(2,1)S(1)}, u32[]{:S(2)}, u32[]{:S(2)}) collective-permute-start(bf16[32,32,128]{2,1,0:T(8,128)(2,1)} %get-tuple-element.67), channel_id=1, source_target_pairs={{6,4},{7,5},{14,12},{15,13},{22,20},{23,21},{30,28},{31,29},{38,36... | collective-permute-start | bytes 786440 | tf_op jit(solution)/shard_map/ppermute | solution.py:398
  111.1 2.0 %collective-permute-start.21 = (bf16[32,32,128]{2,1,0:T(8,128)(2,1)S(1)}, bf16[32,32,128]{2,1,0:T(8,128)(2,1)S(1)}, u32[]{:S(2)}, u32[]{:S(2)}) collective-permute-start(bf16[32,32,128]{2,1,0:T(8,128)(2,1)S(1)} %get-tuple-element.68), channel_id=1, source_target_pairs={{6,2},{7,3},{14,10},{15,11},{22,18},{23,19},{30,26},{31,27},{38,34... | collective-permute-start | bytes 786440 | tf_op jit(solution)/shard_map/ppermute | solution.py:398
  111.7 29.4 %collective-permute-start.22 = (bf16[32,32,128]{2,1,0:T(8,128)(2,1)S(1)}, bf16[32,32,128]{2,1,0:T(8,128)(2,1)S(1)}, u32[]{:S(2)}, u32[]{:S(2)}) collective-permute-start(bf16[32,32,128]{2,1,0:T(8,128)(2,1)S(1)} %get-tuple-element.69), channel_id=1, source_target_pairs={{6,0},{7,1},{14,8},{15,9},{22,16},{23,17},{30,24},{31,25},{38,32},... | collective-permute-start | bytes 786440 | tf_op jit(solution)/shard_map/ppermute | solution.py:398
  141.9 15.6 %collective-permute-start.23 = (bf16[32,32,128]{2,1,0:T(8,128)(2,1)}, bf16[32,32,128]{2,1,0:T(8,128)(2,1)S(1)}, u32[]{:S(2)}, u32[]{:S(2)}) collective-permute-start(bf16[32,32,128]{2,1,0:T(8,128)(2,1)} %select_select_fusion.own), channel_id=1, source_target_pairs={{0,8},{8,16},{16,24},{24,32},{32,40},{40,48},{48,56},{56,64},{64,7... | collective-permute-start | bytes 786440 | tf_op jit(solution)/shard_map/ppermute | solution.py:394
  145.7 21.3 %collective-permute-start.24 = (bf16[32,32,128]{2,1,0:T(8,128)(2,1)}, bf16[32,32,128]{2,1,0:T(8,128)(2,1)S(1)}, u32[]{:S(2)}, u32[]{:S(2)}) collective-permute-start(bf16[32,32,128]{2,1,0:T(8,128)(2,1)} %select_select_fusion.own), channel_id=1, source_target_pairs={{0,16},{8,24},{16,32},{24,40},{32,48},{40,56},{48,64},{56,72},{64,... | collective-permute-start | bytes 786440 | tf_op jit(solution)/shard_map/ppermute | solution.py:394
  152.1 16.8 %all-to-all-start.2 = ((bf16[8,4,32,128]{3,2,1,0:T(8,128)(2,1)}), bf16[8,4,32,128]{3,2,1,0:T(8,128)(2,1)S(1)}, u32[]{:S(2)}, u32[]{:S(2)}) async-start(bf16[8,4,32,128]{3,2,1,0:T(8,128)(2,1)} %bitcast.5), calls=%async_computation.2 | async-start | bytes 524288 | tf_op jit(solution)/shard_map/all_to_all | solution.py:458
  168.9 15.7 %copy-start.5 = (bf16[8,4,32,128]{3,2,1,0:T(8,128)(2,1)}, bf16[8,4,32,128]{3,2,1,0:T(8,128)(2,1)S(1)}, u32[]{:S(2)}) copy-start(bf16[8,4,32,128]{3,2,1,0:T(8,128)(2,1)S(1)} %all-to-all-done.2.rows) | copy-start | bytes 786436
